TPU v7x, 32 devices: a whole 2x2x4 slice. The times are simulated.
32 devices in a mesh: orb: 2 (over x), grid: 16 (over z, y, core).
Axes of the slice: x: 2, y: 2, z: 4, core: 2. Of those that a mesh axis runs over, the one named last changes fastest.
Arguments:
- orbitals: bfloat16 [2, 1024, 2304], P('orb', 'grid'), may hold values from -6 to 6
- continuum: bfloat16 [4, 1024, 2304], P(None, 'grid'), may hold values from -6 to 6
- harmonic_table: bfloat16 [2560, 2304], P('orb'), may hold values from -0.125 to 0.125
- ang_weight: float32 [2560], P('orb'), may hold values from 0.5 to 2
- channel_lm: int32 [2304], replicated, may hold values from 0 to 2303, each once
Outputs:
- exchange_out: float32 [2304, 4, 1024], P('orb', None, 'grid')
Inputs may be any that keep to these rules, and one draw needn't show every extreme that they name: channel_lm names each harmonic index lm = l * l + l + m (l up to 47) exactly once.
All inputs are finite; a program needn't handle non-finite values.
Results may differ from a plain program's by a relative error of at most 0.03.
Values may be sent and summed in bfloat16 or wider, within the bound.
No kernel may reach another device: no remote copies, remote signals or barrier semaphores. Data moves between devices by JAX's collectives and lax.ppermute only.
A program may use at most 128 MiB of HBM per device.

v0:
```python
import math

import jax
import jax.numpy as jnp
from jax import lax
from jax.sharding import PartitionSpec as P

LMAX = 47
LM = 2304


LOG_SPAN = 7.0


def combine(earlier, later):
    return (earlier[0] * later[0], earlier[1] * later[0] + later[1])


def channel_degree(lm_index):
    levels = jnp.arange(1, LMAX + 1, dtype=jnp.int32)
    return jnp.sum((lm_index[:, None] >= levels * levels).astype(jnp.float32), axis=1)


def line_sums(forward_source, backward_source, decay_rate, block_size):
    lead_first, lead_second, count, channels = forward_source.shape
    block_count = count // block_size
    forward_blocks = forward_source.reshape(
        lead_first, lead_second, block_count, block_size, channels
    )
    backward_blocks = backward_source.reshape(
        lead_first, lead_second, block_count, block_size, channels
    )
    forward = forward_blocks
    backward = backward_blocks
    for distance in range(1, block_size):
        factor = jnp.exp(-decay_rate * distance)
        padding = jnp.zeros((lead_first, lead_second, block_count, distance, channels), jnp.float32)
        forward = forward + factor * jnp.concatenate(
            [padding, forward_blocks[:, :, :, : block_size - distance]], axis=3
        )
        backward = backward + factor * jnp.concatenate(
            [backward_blocks[:, :, :, distance:], padding], axis=3
        )
    block_decay = jnp.broadcast_to(
        jnp.exp(-decay_rate * block_size), (lead_first, lead_second, block_count, channels)
    )
    forward_total = lax.associative_scan(
        combine, (block_decay, forward[:, :, :, block_size - 1]), axis=2
    )[1]
    backward_total = lax.associative_scan(
        combine, (block_decay, backward[:, :, :, 0]), reverse=True, axis=2
    )[1]
    boundary = jnp.zeros((lead_first, lead_second, 1, channels), jnp.float32)
    earlier_sum = jnp.concatenate([boundary, forward_total[:, :, : block_count - 1]], axis=2)
    later_sum = jnp.concatenate([backward_total[:, :, 1:], boundary], axis=2)
    offsets = jnp.arange(block_size, dtype=jnp.float32)[:, None]
    forward = forward + jnp.exp(-decay_rate * (offsets + 1.0)) * earlier_sum[:, :, :, None, :]
    backward = (
        backward + jnp.exp(-decay_rate * (block_size - offsets)) * later_sum[:, :, :, None, :]
    )
    shape = forward_source.shape
    return (
        forward.reshape(shape),
        backward.reshape(shape),
        forward_total[:, :, block_count - 1],
        backward_total[:, :, 0],
    )


def local_lines(density, degree, points):
    count = density.shape[2]
    increment = LOG_SPAN / points
    positions = jnp.arange(count, dtype=jnp.int32).astype(jnp.float32)[:, None]
    radius = jnp.exp((positions + 1.0 - points) * increment)
    decay_rate = degree * increment
    source = increment * radius * density
    scaled = increment * density
    forward, backward, forward_end, backward_end = line_sums(
        source, scaled, decay_rate, math.gcd(count, 16)
    )
    return (forward, backward, forward_end, backward_end, radius, scaled, decay_rate)


def finish_potential(forward, backward, radius, scaled, degree):
    factor = 4.0 / (2.0 * degree + 1.0)
    return factor * (forward / radius + backward - scaled)


def shards(orbitals, continuum, harmonic_table, ang_weight, channel_lm):
    analysis = (ang_weight[:, None] * harmonic_table.astype(jnp.float32)).astype(jnp.bfloat16)
    phi_ang = jnp.einsum(
        "al,irl->ira",
        harmonic_table,
        lax.all_gather(orbitals, "orb", axis=0, tiled=True),
        preferred_element_type=jnp.float32,
    ).astype(jnp.bfloat16)
    continuum_angular = jnp.einsum(
        "al,krl->kra", harmonic_table, continuum, preferred_element_type=jnp.float32
    ).astype(jnp.bfloat16)
    pair_values = (
        phi_ang.astype(jnp.float32)[:, None] * continuum_angular.astype(jnp.float32)[None]
    ).astype(jnp.bfloat16)
    density = lax.psum_scatter(
        jnp.einsum(
            "al,ikra->ikrl", analysis, pair_values, preferred_element_type=jnp.float32
        ).astype(jnp.bfloat16),
        "orb",
        scatter_dimension=0,
        tiled=True,
    )
    local_count = LM // lax.axis_size("grid")
    local_channel_index = lax.dynamic_slice_in_dim(
        channel_lm, lax.axis_index("grid") * local_count, local_count
    )
    degree = channel_degree(local_channel_index)
    line_density = lax.all_to_all(density, "grid", split_axis=3, concat_axis=2, tiled=True)
    points = line_density.shape[2]
    forward, backward, forward_end, backward_end, radius, scaled, decay_rate = local_lines(
        line_density.astype(jnp.float32), degree, points
    )
    potential = finish_potential(forward, backward, radius, scaled, degree).astype(jnp.bfloat16)
    radial_potential = lax.all_to_all(potential, "grid", split_axis=2, concat_axis=3, tiled=True)
    pot_ang = jnp.einsum(
        "al,ikrl->ikra",
        harmonic_table,
        lax.all_gather(radial_potential, "orb", axis=0, tiled=True),
        preferred_element_type=jnp.float32,
    )
    weighted_values = jnp.sum(phi_ang.astype(jnp.float32)[:, None] * pot_ang, axis=0)
    product = weighted_values.astype(jnp.bfloat16)
    return -lax.psum_scatter(
        jnp.einsum("al,kra->lkr", analysis, product, preferred_element_type=jnp.float32),
        "orb",
        scatter_dimension=0,
        tiled=True,
    )


def solution(mesh):
    return jax.shard_map(
        shards,
        mesh=mesh,
        in_specs=(P("orb", "grid", None), P(None, "grid", None), P("orb", None), P("orb"), P()),
        out_specs=P("orb", None, "grid"),
        check_vma=False,
    )
```

profile of v0, /device:TPU:0, one launch (start us, length us, event | category | flops | bytes accessed | tf_op | source)
XLA Modules:
  0.0 536.8 jit_solution(362612435213121791)
XLA Ops:
  6.5 11.0 %all_gather.6 = bf16[2,64,2304]{2,1,0:T(8,128)(2,1)S(1)} all-gather(bf16[1,64,2304]{2,1,0:T(8,128)(2,1)} %param.5), channel_id=1, replica_groups=mesh['orb'=2,'grid'=16] {'orb'}, dimensions={0}, use_global_device_ids=true | all-gather | bytes 884736 | tf_op jit(solution)/shard_map/all_gather | solution.py:94
  17.5 4.8 fusion.27
  22.4 1.7 fusion.21
  24.1 5.0 fusion.10
  29.1 36.3 %reduce-scatter.3.cloned.1.call-done = bf16[1,4,64,2304]{3,2,1,0:T(8,128)(2,1)} async-done(((bf16[2,4,64,2304]{3,2,1,0:T(8,128)(2,1)}), bf16[1,4,64,2304]{3,2,1,0:T(8,128)(2,1)}) %reduce-scatter.3.cloned.1.call-update) | async-done | bytes 1179664 | tf_op jit(solution)/shard_map/reduce_scatter | solution.py:103
  65.5 4.2 copy.104
  69.7 2.4 reshape.319
  72.1 5.6 %all-to-all-start = ((bf16[16,2,18432]{2,1,0:T(2,128)(2,1)}), bf16[16,2,18432]{2,1,0:T(2,128)(2,1)S(1)}, u32[]{:S(2)}, u32[]{:S(2)}) async-start(bf16[16,2,18432]{2,1,0:T(2,128)(2,1)} %reshape.319), calls=%async_computation.1 | async-start | bytes 2359296 | tf_op jit(solution)/shard_map/all_to_all | solution.py:116
  81.4 21.5 %all-to-all-done = bf16[16,2,18432]{2,1,0:T(2,128)(2,1)S(1)} async-done(((bf16[16,2,18432]{2,1,0:T(2,128)(2,1)}), bf16[16,2,18432]{2,1,0:T(2,128)(2,1)S(1)}, u32[]{:S(2)}, u32[]{:S(2)}) %all-to-all-start) | async-done | bytes 1179680 | tf_op jit(solution)/shard_map/all_to_all | solution.py:116
  104.4 5.4 %copy.132 = f32[1,4,64,16,144]{4,2,3,1,0:T(8,128)} copy(bf16[1,4,64,16,144]{2,1,4,3,0:T(4,128)(2,1)S(1)} %bitcast.77) | data formatting | bytes 3538944 | tf_op jit(solution)/shard_map/convert_element_type | solution.py:119
  109.8 7.5 %copy_multiply_fusion = f32[1,4,64,16,144]{4,0,3,2,1:T(1,128)S(1)} fusion(f32[1,4,64,16,144]{4,3,2,1,0:T(8,128)} %bitcast.74, f32[64,16]{1,0:T(8,128)S(1)} %copy-done.29), kind=kLoop, calls=%fused_computation.17 | loop fusion | flops 589824 | bytes 4722688 | tf_op jit(solution)/shard_map/mul | solution.py:76
  117.3 5.5 %slice.492 = f32[1,4,64,15,144]{4,0,3,2,1:T(1,128)} slice(f32[1,4,64,16,144]{4,0,3,2,1:T(1,128)S(1)} %copy_multiply_fusion), slice={[0:1], [0:4], [0:64], [0:15], [0:144]} | slice | bytes 4423680 | tf_op jit(solution)/shard_map/slice | solution.py:39
  122.8 5.2 slice.493
  128.0 3.1 slice.494
  131.1 3.1 slice.495
  134.2 2.6 slice.496
  136.8 2.4 slice.497
  139.2 2.1 slice.498
  141.3 1.9 slice.499
  143.2 3.3 slice.500
  146.6 2.6 slice.501
  149.3 2.3 slice.502
  154.3 43.8 %multiply_add_fusion.3 = f32[1,4,64,16,144]{4,0,3,2,1:T(1,128)S(1)} fusion(f32[1,4,64,1,144]{4,0,3,2,1:T(1,128)S(1)} %slice.506, f32[1,4,64,2,144]{4,0,3,2,1:T(1,128)S(1)} %slice.505, f32[1,4,64,3,144]{4,0,3,2,1:T(1,128)S(1)} %slice.504, f32[1,4,64,4,144]{4,0,3,2,1:T(1,128)S(1)} %slice.503, f32[1,4,64,5,144]{4,0,3,2,1:T(1,128)} %slice.502, ...), kind=kLoop, calls=%fused_computation.21 | loop fusion | flops 18284544 | bytes 22426048 | tf_op jit(solution)/shard_map/add | solution.py:38
  198.2 2.0 copy-done.6
  205.7 2.7 broadcast_multiply_fusion.1
  208.4 3.0 slice.526
  211.3 2.6 slice.527
  213.9 2.7 slice.528
  216.6 2.6 slice.529
  219.3 2.6 slice.530
  221.9 2.6 slice.531
  224.5 2.7 slice.532
  228.8 1.6 slice.535
  235.5 8.1 %copy.157 = f32[1,4,64,15,144]{4,0,3,2,1:T(1,128)} copy(f32[1,4,64,15,144]{4,3,2,1,0:T(8,128)} %slice.526) | data formatting | bytes 4423680
  243.7 8.2 %copy.156 = f32[1,4,64,14,144]{4,0,3,2,1:T(1,128)} copy(f32[1,4,64,14,144]{4,3,2,1,0:T(8,128)} %slice.527) | data formatting | bytes 4128768
  251.9 5.4 %copy.155 = f32[1,4,64,13,144]{4,0,3,2,1:T(1,128)} copy(f32[1,4,64,13,144]{4,3,2,1,0:T(8,128)S(1)} %copy-done.10) | data formatting | bytes 3833856
  257.3 3.3 copy.154
  260.6 5.0 copy.153
  265.6 2.8 copy.152
  268.4 2.5 copy.151
  270.9 2.2 copy.150
  273.1 4.8 copy.149
  278.0 2.9 copy.148
  281.0 3.1 copy.147
  284.1 2.3 copy.146
  288.0 35.6 %multiply_add_fusion.1 = f32[1,4,64,16,144]{4,0,3,2,1:T(1,128)S(1)} fusion(f32[1,4,64,2,144]{4,0,3,2,1:T(1,128)S(1)} %copy.144, f32[1,4,64,3,144]{4,0,3,2,1:T(1,128)S(1)} %copy.145, f32[1,4,64,4,144]{4,0,3,2,1:T(1,128)S(1)} %copy.146, f32[1,4,64,5,144]{4,0,3,2,1:T(1,128)S(1)} %copy.147, f32[1,4,64,6,144]{4,0,3,2,1:T(1,128)} %copy.148, ...), kind=kLoop, calls=%fused_computation.19 | loop fusion | flops 16515072 | bytes 22273920 | tf_op jit(solution)/shard_map/add | solution.py:41
  330.7 10.6 %pad.124 = f32[1,4,16,144]{3,0,2,1:T(1,128)S(1)} pad(f32[1,4,8,144]{3,0,2,1:T(1,128)} %pad_maximum_fusion.5, f32[]{:T(128)} %constant.31.clone.1), padding=0_0_0x0_0_0x0_1_1x0_0_0 | pad | bytes 55300 | tf_op jit(solution)/shard_map/pad | solution.py:50
  342.2 3.0 broadcast_multiply_fusion
  345.2 1.6 pad.205
  347.0 1.8 pad.152
  349.2 9.2 %multiply_add_fusion.2 = f32[1,4,64,16,144]{4,0,3,2,1:T(1,128)} fusion(f32[1,4,64,16,144]{4,0,3,2,1:T(1,128)} %copy-done.6, f32[4,64,144]{2,1,0:T(8,128)S(1)} %pad_bitcast_fusion.1, f32[16,144]{1,0:T(8,128)S(1)} %copy-done.31), kind=kLoop, calls=%fused_computation.20 | loop fusion | flops 1179648 | bytes 4875264 | tf_op jit(solution)/shard_map/add | solution.py:57
  358.4 4.7 copy.136
  364.9 1.6 pad.204
  367.0 1.6 pad.154
  369.2 7.0 %copy.134 = f32[1,4,64,16,144]{4,2,3,1,0:T(8,128)} copy(f32[1,4,64,16,144]{2,1,4,3,0:T(4,128)} %bitcast.78) | data formatting | bytes 4718592 | tf_op jit(solution)/shard_map/mul | solution.py:77
  376.2 3.1 multiply_add_fusion
  382.5 1.6 copy.127
  384.2 54.9 %all_to_all.27 = bf16[1,4,1024,144]{3,1,0,2:T(4,128)(2,1)S(1)} all-to-all(bf16[1,4,1024,144]{3,1,0,2:T(4,128)(2,1)S(1)} %copy.127), channel_id=1, replica_groups=mesh['orb'=2,'grid'=16] {'grid'}, dimensions={2} | all-to-all | bytes 2359296 | tf_op jit(solution)/shard_map/all_to_all | solution.py:122
  440.2 4.1 all_to_all.24
  444.4 35.7 %all-gather.2.cloned.1.call-done = bf16[2,4,64,2304]{3,2,1,0:T(8,128)(2,1)} async-done(((bf16[1,4,64,2304]{3,2,1,0:T(8,128)(2,1)}), bf16[2,4,64,2304]{3,2,1,0:T(8,128)(2,1)}) %all-gather.2.cloned.1.call-update) | async-done | bytes 2359312 | tf_op jit(solution)/shard_map/all_gather | solution.py:126
  480.0 6.7 %fusion.30 = bf16[4,64,1280]{2,1,0:T(8,128)(2,1)S(1)} fusion(bf16[2,4,64,2304]{3,2,1,0:T(8,128)(2,1)} %all-gather.2.cloned.1.call-done, bf16[1280,2304]{1,0:T(8,128)(2,1)} %param.7, f32[2,64,1280]{2,1,0:T(8,128)S(1)} %copy-done.27), kind=kOutput, calls=%fused_computation.31 | convolution fusion | flops 3020881920 | bytes 9568256 | tf_op jit(solution)/shard_map/al,ikrl->ikra/dot_general | solution.py:123
  486.7 6.0 %fusion.8 = f32[2304,4,64]{0,2,1:T(8,128)} fusion(bf16[1280,2304]{1,0:T(8,128)(2,1)} %param.7, f32[1280]{0:T(1024)S(1)} %copy-done.75, bf16[4,64,1280]{2,1,0:T(8,128)(2,1)S(1)} %fusion.30), kind=kOutput, calls=%fused_computation.9 | convolution fusion | flops 1518796800 | bytes 8918016 | tf_op jit(solution)/shard_map/al,kra->lkr/dot_general | solution.py:132
  492.7 34.9 %reduce-scatter.5.cloned.1.call-done = f32[1152,4,64]{0,2,1:T(8,128)} async-done(((f32[2304,4,64]{0,2,1:T(8,128)}), f32[1152,4,64]{0,2,1:T(8,128)}) %reduce-scatter.5.cloned.1.call-update) | async-done | bytes 1179664 | tf_op jit(solution)/shard_map/reduce_scatter | solution.py:131
  527.6 2.4 neg.74
  (269 shorter events, 36.6 us)
Async XLA Ops:
  6.5 15.8 %copy-start = (bf16[4,64,2304]{2,1,0:T(8,128)(2,1)S(1)}, bf16[4,64,2304]{2,1,0:T(8,128)(2,1)}, u32[]{:S(2)}) copy-start(bf16[4,64,2304]{2,1,0:T(8,128)(2,1)} %param.6) | copy-start | bytes 3538948
  6.5 58.9 %reduce-scatter.3.cloned.1.call-start = ((), (), s32[]{:S(2)}) async-start(), calls=%async_computation.4 | async-start | bytes 3538944 | tf_op jit(solution)/shard_map/reduce_scatter | solution.py:103
  6.5 15.8 %slice-start.1 = ((s8[5898240]{0:T(1024)(128)(4,1)}), s8[4194304]{0:T(1024)(128)(4,1)S(1)}, s32[]{:S(2)}) async-start(s8[5898240]{0:T(1024)(128)(4,1)} %bitcast.80), calls=%async_computation.8 | async-start | bytes 8388608
  72.1 30.8 %all-to-all-start = ((bf16[16,2,18432]{2,1,0:T(2,128)(2,1)}), bf16[16,2,18432]{2,1,0:T(2,128)(2,1)S(1)}, u32[]{:S(2)}, u32[]{:S(2)}) async-start(bf16[16,2,18432]{2,1,0:T(2,128)(2,1)} %reshape.319), calls=%async_computation.1 | async-start | bytes 2359296 | tf_op jit(solution)/shard_map/all_to_all | solution.py:116
  77.8 402.2 %all-gather.2.cloned.1.call-start = ((), (), s32[]{:S(2)}) async-start(), calls=%async_computation.5 | async-start | bytes 3538944 | tf_op jit(solution)/shard_map/all_gather | solution.py:126
  104.4 5.4 %copy-start.29 = (f32[64,16]{1,0:T(8,128)S(1)}, f32[64,16]{1,0:T(8,128)}, u32[]{:S(2)}) copy-start(f32[64,16]{1,0:T(8,128)} %copy.103) | copy-start | bytes 12292
  143.2 10.9 %copy-start.16 = (f32[1,4,64,14,144]{4,0,3,2,1:T(1,128)S(1)}, f32[1,4,64,14,144]{4,0,3,2,1:T(1,128)}, u32[]{:S(2)}) copy-start(f32[1,4,64,14,144]{4,0,3,2,1:T(1,128)} %slice.493) | copy-start | bytes 6193156
  146.6 7.5 %copy-start.15 = (f32[1,4,64,15,144]{4,0,3,2,1:T(1,128)S(1)}, f32[1,4,64,15,144]{4,0,3,2,1:T(1,128)}, u32[]{:S(2)}) copy-start(f32[1,4,64,15,144]{4,0,3,2,1:T(1,128)} %slice.492) | copy-start | bytes 6635524
  149.2 5.0 copy-start.44
  149.2 5.0 copy-start.46
  149.2 5.0 copy-start.48
  149.2 5.0 copy-start.50
  149.2 5.0 copy-start.52
  149.2 5.0 copy-start.54
  149.3 5.0 copy-start.56
  149.3 5.0 copy-start.58
  149.3 5.0 copy-start.60
  149.3 5.0 copy-start.62
  149.3 5.0 copy-start.64
  154.3 46.2 %copy-start.32 = (f32[144]{0:T(256)S(1)}, f32[144]{0:T(256)}, u32[]{:S(2)}) copy-start(f32[144]{0:T(256)} %get-tuple-element.42) | copy-start | bytes 1732
  154.3 46.3 %copy-start.68 = (f32[144]{0:T(256)S(1)}, f32[144]{0:T(256)}, u32[]{:S(2)}) copy-start(f32[144]{0:T(256)} %get-tuple-element.43) | copy-start | bytes 1732
  154.3 46.4 %copy-start.69 = (f32[144]{0:T(256)S(1)}, f32[144]{0:T(256)}, u32[]{:S(2)}) copy-start(f32[144]{0:T(256)} %get-tuple-element.47) | copy-start | bytes 1732
  154.3 46.5 %copy-start.70 = (f32[144]{0:T(256)S(1)}, f32[144]{0:T(256)}, u32[]{:S(2)}) copy-start(f32[144]{0:T(256)} %get-tuple-element.46) | copy-start | bytes 1732
  154.3 46.5 %copy-start.71 = (f32[144]{0:T(256)S(1)}, f32[144]{0:T(256)}, u32[]{:S(2)}) copy-start(f32[144]{0:T(256)} %get-tuple-element.44) | copy-start | bytes 1732
  154.3 46.5 %copy-start.73 = (f32[144]{0:T(256)S(1)}, f32[144]{0:T(256)}, u32[]{:S(2)}) copy-start(f32[144]{0:T(256)} %get-tuple-element.45) | copy-start | bytes 1732
  200.5 7.9 %copy-start.25 = (f32[1,4,64,144]{3,0,2,1:T(1,128)}, f32[1,4,64,144]{3,0,2,1:T(1,128)S(1)}, u32[]{:S(2)}) copy-start(f32[1,4,64,144]{3,0,2,1:T(1,128)S(1)} %slice_bitcast_fusion.1) | copy-start | bytes 442372
  208.4 26.2 %copy-start.2 = (f32[1,4,64,16,144]{4,3,2,1,0:T(8,128)}, f32[1,4,64,16,144]{4,3,2,1,0:T(8,128)S(1)}, u32[]{:S(2)}) copy-start(f32[1,4,64,16,144]{4,3,2,1,0:T(8,128)S(1)} %broadcast_multiply_fusion.1) | copy-start | bytes 7077892
  243.7 8.2 %copy-start.10 = (f32[1,4,64,13,144]{4,3,2,1,0:T(8,128)S(1)}, f32[1,4,64,13,144]{4,3,2,1,0:T(8,128)}, u32[]{:S(2)}) copy-start(f32[1,4,64,13,144]{4,3,2,1,0:T(8,128)} %slice.528) | copy-start | bytes 5750788
  251.8 5.4 %copy-start.8 = (f32[1,4,64,12,144]{4,3,2,1,0:T(8,128)S(1)}, f32[1,4,64,12,144]{4,3,2,1,0:T(8,128)}, u32[]{:S(2)}) copy-start(f32[1,4,64,12,144]{4,3,2,1,0:T(8,128)} %slice.529) | copy-start | bytes 5308420
  260.6 5.0 copy-start.11
  268.4 9.6 %copy-start.20 = (f32[1,4,64,6,144]{4,3,2,1,0:T(8,128)S(1)}, f32[1,4,64,6,144]{4,3,2,1,0:T(8,128)}, u32[]{:S(2)}) copy-start(f32[1,4,64,6,144]{4,3,2,1,0:T(8,128)} %slice.535) | copy-start | bytes 2654212
  270.9 16.9 %copy-start.19 = (f32[1,4,64,11,144]{4,0,3,2,1:T(1,128)S(1)}, f32[1,4,64,11,144]{4,0,3,2,1:T(1,128)}, u32[]{:S(2)}) copy-start(f32[1,4,64,11,144]{4,0,3,2,1:T(1,128)} %copy.153) | copy-start | bytes 4866052
  273.1 14.2 %copy-start.23 = (f32[1,4,64,2,144]{4,3,2,1,0:T(2,128)S(1)}, f32[1,4,64,2,144]{4,3,2,1,0:T(2,128)}, u32[]{:S(2)}) copy-start(f32[1,4,64,2,144]{4,3,2,1,0:T(2,128)} %slice.539) | copy-start | bytes 884740
  273.1 14.7 %copy-start.18 = (f32[1,4,64,13,144]{4,0,3,2,1:T(1,128)S(1)}, f32[1,4,64,13,144]{4,0,3,2,1:T(1,128)}, u32[]{:S(2)}) copy-start(f32[1,4,64,13,144]{4,0,3,2,1:T(1,128)} %copy.155) | copy-start | bytes 5750788
  278.0 9.9 %copy-start.17 = (f32[1,4,64,14,144]{4,0,3,2,1:T(1,128)S(1)}, f32[1,4,64,14,144]{4,0,3,2,1:T(1,128)}, u32[]{:S(2)}) copy-start(f32[1,4,64,14,144]{4,0,3,2,1:T(1,128)} %copy.156) | copy-start | bytes 6193156
  280.9 6.9 %copy-start.3 = (f32[1,4,64,16,144]{4,3,2,1,0:T(8,128)S(1)}, f32[1,4,64,16,144]{4,3,2,1,0:T(8,128)}, u32[]{:S(2)}) copy-start(f32[1,4,64,16,144]{4,3,2,1,0:T(8,128)} %copy-done.2) | copy-start | bytes 7077892
  280.9 6.9 %copy-start.14 = (f32[1,4,64,15,144]{4,0,3,2,1:T(1,128)S(1)}, f32[1,4,64,15,144]{4,0,3,2,1:T(1,128)}, u32[]{:S(2)}) copy-start(f32[1,4,64,15,144]{4,0,3,2,1:T(1,128)} %copy.157) | copy-start | bytes 6635524
  280.9 7.0 %copy-start.41 = (f32[144]{0:T(256)S(1)}, f32[144]{0:T(256)}, u32[]{:S(2)}) copy-start(f32[144]{0:T(256)} %get-tuple-element.27) | copy-start | bytes 1732
  280.9 7.0 %copy-start.43 = (f32[144]{0:T(256)S(1)}, f32[144]{0:T(256)}, u32[]{:S(2)}) copy-start(f32[144]{0:T(256)} %get-tuple-element.28) | copy-start | bytes 1732
  280.9 7.0 %copy-start.45 = (f32[144]{0:T(256)S(1)}, f32[144]{0:T(256)}, u32[]{:S(2)}) copy-start(f32[144]{0:T(256)} %get-tuple-element.29) | copy-start | bytes 1732
  280.9 7.0 %copy-start.47 = (f32[144]{0:T(256)S(1)}, f32[144]{0:T(256)}, u32[]{:S(2)}) copy-start(f32[144]{0:T(256)} %get-tuple-element.30) | copy-start | bytes 1732
  280.9 7.0 %copy-start.49 = (f32[144]{0:T(256)S(1)}, f32[144]{0:T(256)}, u32[]{:S(2)}) copy-start(f32[144]{0:T(256)} %get-tuple-element.31) | copy-start | bytes 1732
  281.0 7.0 %copy-start.51 = (f32[144]{0:T(256)S(1)}, f32[144]{0:T(256)}, u32[]{:S(2)}) copy-start(f32[144]{0:T(256)} %get-tuple-element.32) | copy-start | bytes 1732
  281.0 7.0 %copy-start.53 = (f32[144]{0:T(256)S(1)}, f32[144]{0:T(256)}, u32[]{:S(2)}) copy-start(f32[144]{0:T(256)} %get-tuple-element.33) | copy-start | bytes 1732
  281.0 7.0 %copy-start.55 = (f32[144]{0:T(256)S(1)}, f32[144]{0:T(256)}, u32[]{:S(2)}) copy-start(f32[144]{0:T(256)} %get-tuple-element.34) | copy-start | bytes 1732
  281.0 7.0 %copy-start.57 = (f32[144]{0:T(256)S(1)}, f32[144]{0:T(256)}, u32[]{:S(2)}) copy-start(f32[144]{0:T(256)} %get-tuple-element.35) | copy-start | bytes 1732
  281.0 7.0 %copy-start.59 = (f32[144]{0:T(256)S(1)}, f32[144]{0:T(256)}, u32[]{:S(2)}) copy-start(f32[144]{0:T(256)} %get-tuple-element.36) | copy-start | bytes 1732
  281.0 7.0 %copy-start.61 = (f32[144]{0:T(256)S(1)}, f32[144]{0:T(256)}, u32[]{:S(2)}) copy-start(f32[144]{0:T(256)} %get-tuple-element.37) | copy-start | bytes 1732
  281.0 7.0 %copy-start.63 = (f32[144]{0:T(256)S(1)}, f32[144]{0:T(256)}, u32[]{:S(2)}) copy-start(f32[144]{0:T(256)} %get-tuple-element.38) | copy-start | bytes 1732
  281.0 7.0 %copy-start.65 = (f32[144]{0:T(256)S(1)}, f32[144]{0:T(256)}, u32[]{:S(2)}) copy-start(f32[144]{0:T(256)} %get-tuple-element.39) | copy-start | bytes 1732
  281.0 7.0 %copy-start.67 = (f32[144]{0:T(256)S(1)}, f32[144]{0:T(256)}, u32[]{:S(2)}) copy-start(f32[144]{0:T(256)} %get-tuple-element.40) | copy-start | bytes 1732
  288.0 35.6 %copy-start.22 = (f32[1,4,64,1,144]{4,3,2,1,0:T(1,128)S(1)}, f32[1,4,64,1,144]{4,3,2,1,0:T(1,128)}, u32[]{:S(2)}) copy-start(f32[1,4,64,1,144]{4,3,2,1,0:T(1,128)} %slice.540) | copy-start | bytes 442372
  288.0 35.6 %copy-start.36 = (f32[144]{0:T(256)S(1)}, f32[144]{0:T(256)}, u32[]{:S(2)}) copy-start(f32[144]{0:T(256)} %get-tuple-element.41) | copy-start | bytes 1732
  325.9 19.3 %copy-start.24 = (f32[1,4,64,144]{3,0,2,1:T(1,128)}, f32[1,4,64,144]{3,0,2,1:T(1,128)S(1)}, u32[]{:S(2)}) copy-start(f32[1,4,64,144]{3,0,2,1:T(1,128)S(1)} %slice_bitcast_fusion) | copy-start | bytes 442372
  329.3 17.6 %slice-start.4 = ((f32[1,4,64,144]{3,0,2,1:T(1,128)}), f32[1,4,1,144]{3,0,2,1:T(1,128)S(1)}, s32[]{:S(2)}) async-start(f32[1,4,64,144]{3,0,2,1:T(1,128)} %copy-done.25), calls=%async_computation.11 | async-start | bytes 8192 | tf_op jit(solution)/shard_map/slice | solution.py:47
  329.3 17.6 %copy-start.28 = (f32[1,4,31,144]{3,0,2,1:T(1,128)S(1)}, f32[1,4,31,144]{3,0,2,1:T(1,128)}, u32[]{:S(2)}) copy-start(f32[1,4,31,144]{3,0,2,1:T(1,128)} %fusion.38) | copy-start | bytes 214276
  342.2 7.0 %copy-start.31 = (f32[16,144]{1,0:T(8,128)S(1)}, f32[16,144]{1,0:T(8,128)}, u32[]{:S(2)}) copy-start(f32[16,144]{1,0:T(8,128)} %get-tuple-element.49) | copy-start | bytes 27652
  358.4 8.2 %copy-start.34 = (f32[144]{0:T(256)S(1)}, f32[144]{0:T(256)}, u32[]{:S(2)}) copy-start(f32[144]{0:T(256)} %get-tuple-element.42) | copy-start | bytes 1732
  358.4 8.5 %slice-start.3 = ((f32[1,4,64,144]{3,0,2,1:T(1,128)}), f32[1,4,1,144]{3,0,2,1:T(1,128)S(1)}, s32[]{:S(2)}) async-start(f32[1,4,64,144]{3,0,2,1:T(1,128)} %copy-done.24), calls=%async_computation.10 | async-start | bytes 8192 | tf_op jit(solution)/shard_map/slice | solution.py:50
  369.2 7.0 %copy-start.37 = (f32[144]{0:T(256)S(1)}, f32[144]{0:T(256)}, u32[]{:S(2)}) copy-start(f32[144]{0:T(256)} %get-tuple-element.41) | copy-start | bytes 1732
  439.0 41.0 %copy-start.27 = (f32[2,64,1280]{2,1,0:T(8,128)S(1)}, f32[2,64,1280]{2,1,0:T(8,128)}, u32[]{:S(2)}) copy-start(f32[2,64,1280]{2,1,0:T(8,128)} %copy-done.26) | copy-start | bytes 1966084
  444.3 42.4 %copy-start.75 = (f32[1280]{0:T(1024)S(1)}, f32[1280]{0:T(1024)}, u32[]{:S(2)}) copy-start(f32[1280]{0:T(1024)} %param.8) | copy-start | bytes 15364
  444.3 83.3 %reduce-scatter.5.cloned.1.call-start = ((), (), s32[]{:S(2)}) async-start(), calls=%async_computation.6 | async-start | bytes 3538944 | tf_op jit(solution)/shard_map/reduce_scatter | solution.py:131
  486.7 43.3 %copy-start.1 = (bf16[4,64,2304]{2,1,0:T(8,128)(2,1)S(1)}, bf16[4,64,2304]{2,1,0:T(8,128)(2,1)}, u32[]{:S(2)}) copy-start(bf16[4,64,2304]{2,1,0:T(8,128)(2,1)} %param.6) | copy-start | bytes 3538948
  (21 other events, 77.9 us)
Sparse Core Ops, SparseCore 0:
  29.3 36.1 reduce-scatter.2
  444.4 35.5 all-gather.1
  492.9 34.6 reduce-scatter.4
where the time goes:
time: 543 us; the launch traced here: 537 us
  local copies, waits for them, and re-layouts  180 us (33%)
  waiting for transfers between devices  128 us (24%)
  other arithmetic  118 us (22%)
  blocking collectives  65.8 us (12%)
  matrix products  24.2 us (4%)
  between operations  15 us (3%)
  starting transfers between devices  5.71 us (1%)
    unnamed x179, local copies, waits for them, and re-layouts  69.2 us
    all_to_all x1, blocking collectives, shards(): lax.all_to_all(potential, 'grid', split_axis=2, concat_axis=3, tiled=True)  54.9 us
    add x1, other arithmetic, line_sums(): forward + factor * jnp.concatenate([padding, forward_blocks[:, :, :, :blo...  43.8 us
    slice x15, local copies, waits for them, and re-layouts, line_sums(): forward_blocks[:, :, :, :block_size - distance]  36.5 us
    reduce_scatter x1, waiting for transfers between devices, shards(): lax.psum_scatter(jnp.einsum('al,ikra->ikrl', analysis, pair_values, prefe...  36.3 us
    add x2, other arithmetic, line_sums(): backward + factor * jnp.concatenate([backward_blocks[:, :, :, distance:],...  36.2 us
    all_gather x1, waiting for transfers between devices, shards(): lax.all_gather(radial_potential, 'orb', axis=0, tiled=True)  35.7 us
    reduce_scatter x1, waiting for transfers between devices, shards(): lax.psum_scatter(jnp.einsum('al,kra->lkr', analysis, product, preferred_e...  34.9 us
  transfers between devices with their start and end apart: 4, of which 4 were waited for; matrix products, arithmetic and copies ran while one was open for 1% of the time, Pallas kernels for 0%

commit v1 on v0

--- a/solution.py
+++ b/solution.py
@@ -1,8 +1,11 @@
+import functools
 import math
 
 import jax
 import jax.numpy as jnp
 from jax import lax
+from jax.experimental import pallas as pl
+from jax.experimental.pallas import tpu as pltpu
 from jax.sharding import PartitionSpec as P
 
 LMAX = 47
@@ -136,9 +139,346 @@
     )
 
 
+NC = 4
+NI = 2
+NP = NI * NC
+CHUNK = 256
+TILE = 768
+F32 = jnp.float32
+BF16 = jnp.bfloat16
+
+
+def dot_nt(a, b):
+    return lax.dot_general(a, b, (((1,), (1,)), ((), ())), preferred_element_type=F32)
+
+
+def dot_nn(a, b):
+    return jnp.dot(a, b, preferred_element_type=F32)
+
+
+def span_of(index, size):
+    return pl.ds(pl.multiple_of(index * size, size), size)
+
+
+def store_pairs(values, weight, points, pairs, span):
+    phi = values[: NI * points].astype(F32) * weight
+    psi = values[NI * points :].astype(F32)
+    for i in range(NI):
+        for k in range(NC):
+            product = phi[i * points : (i + 1) * points] * psi[k * points : (k + 1) * points]
+            row = (i * NC + k) * points
+            pairs[row : row + points, span] = product.astype(BF16)
+
+
+def own_kernel(
+    step, place, own, other, cont, weight, degree_ref, table_hbm,
+    part_ref, phi_ref, ends_ref,
+    table, rows, pairs, work, sems,
+):
+    x = place[0]
+    points = own.shape[0]
+    half = points // 2
+    steps = table.shape[0] // CHUNK
+
+    def fetch(i):
+        return pltpu.make_async_copy(
+            table_hbm.at[span_of(i, CHUNK)], table.at[span_of(i, CHUNK)], sems.at[i]
+        )
+
+    for i in range(steps):
+        fetch(i).start()
+    rows[span_of(x, points), :] = own[...]
+    rows[span_of(1 - x, points), :] = other[...]
+    rows[NI * points :, :] = cont[...]
+
+    def angular(i, carry):
+        fetch(i).wait()
+        span = span_of(i, CHUNK)
+        values = dot_nt(rows[...], table[span, :]).astype(BF16)
+        store_pairs(values, weight[:, span], points, pairs, span)
+        for o in range(NI):
+            lower = values[o * points : o * points + half]
+            upper = values[o * points + half : (o + 1) * points]
+            phi_ref[o * half : (o + 1) * half, span] = jnp.where(x == 0, lower, upper)
+        return carry
+
+    lax.fori_loop(0, steps, angular, 0)
+
+    def density(t, carry):
+        span = span_of(t, TILE)
+        degree = degree_ref[:, span]
+        work[...] = dot_nn(pairs[...], table[:, span])
+        position = lax.broadcasted_iota(jnp.int32, (half, TILE), 0).astype(F32)
+        ahead = jnp.exp((degree + 1.0) * step * (position - (half - 1.0)))
+        behind = jnp.exp(-degree * step * position)
+        for p in range(NP):
+            low = work[p * points : p * points + half, :]
+            high = work[p * points + half : (p + 1) * points, :]
+            part_ref[p * half : (p + 1) * half, span] = jnp.where(x == 0, low, high).astype(BF16)
+            ends = (low * ahead, high * ahead, low * behind, high * behind)
+            for n in range(4):
+                ends_ref[n * NP + p : n * NP + p + 1, span] = jnp.sum(ends[n], axis=0, keepdims=True)
+        return carry
+
+    lax.fori_loop(0, table.shape[1] // TILE, density, 0)
+
+
+def finish_kernel(
+    step, pieces, place, own, other, cont, weight, far_weight, degree_ref, earlier, later, part, phi, *refs
+):
+    table_hbm, far_hbm = refs[0], refs[1 : 1 + pieces]
+    send_ref, keep_ref, table, rows, pairs, far_phi, pot, product, work, total, sems = refs[1 + pieces :]
+    x = place[0]
+    points = own.shape[0]
+    half = points // 2
+    quad = table_hbm.shape[0]
+    size = quad // pieces
+    steps = quad // CHUNK
+    channels = table.shape[1]
+
+    def fetch_far(n):
+        start = pl.multiple_of(quad + place[1 + n], size)
+        return pltpu.make_async_copy(far_hbm[n], table.at[pl.ds(start, size)], sems.at[n])
+
+    fetch_own = pltpu.make_async_copy(table_hbm, table.at[pl.ds(0, quad)], sems.at[pieces])
+    for n in range(pieces):
+        fetch_far(n).start()
+    fetch_own.start()
+    rows[span_of(x, half), :] = own[span_of(x, half), :]
+    rows[span_of(1 - x, half), :] = other[span_of(x, half), :]
+    for k in range(NC):
+        rows[(NI + k) * half : (NI + k + 1) * half, :] = cont[span_of(2 * k + x, half), :]
+    for n in range(pieces):
+        fetch_far(n).wait()
+
+    def angular(i, carry):
+        span = span_of(i, CHUNK)
+        values = dot_nt(rows[...], table[span_of(i + steps, CHUNK), :]).astype(BF16)
+        store_pairs(values, far_weight[:, span], half, pairs, span)
+        far_phi[:, span] = values[: NI * half]
+        return carry
+
+    lax.fori_loop(0, steps, angular, 0)
+
+    def radial(t, carry):
+        span = span_of(t, TILE)
+        degree = degree_ref[:, span]
+        shrink_ahead = jnp.exp(-(degree + 1.0) * step)
+        shrink_behind = jnp.exp(-degree * step)
+        factor = 4.0 * step / (2.0 * degree + 1.0)
+        far = dot_nn(pairs[...], table[quad:, span])
+        density = part[:, span].astype(F32) + far.astype(BF16).astype(F32)
+        density = density.astype(BF16).astype(F32)
+        work[...] = density.reshape(NP, half, TILE)
+        ahead = earlier[:, span]
+        behind = later[:, span] * shrink_behind
+        for j in range(half):
+            ahead = ahead * shrink_ahead + work[:, j, :]
+            total[:, j, :] = ahead
+        for j in range(half - 1, -1, -1):
+            total[:, j, :] = factor * (total[:, j, :] + behind)
+            behind = (behind + work[:, j, :]) * shrink_behind
+        pot[:, span] = total[...].reshape(NP * half, TILE).astype(BF16)
+        return carry
+
+    lax.fori_loop(0, channels // TILE, radial, 0)
+    fetch_own.wait()
+
+    def weigh(i, table_at, phi_at, weight_at, span):
+        angle = dot_nt(pot[...], table[table_at, :])
+        for k in range(NC):
+            value = jnp.zeros((half, CHUNK), F32)
+            for o in range(NI):
+                value += phi_at[o * half : (o + 1) * half, span].astype(F32) * angle[
+                    (o * NC + k) * half : (o * NC + k + 1) * half
+                ]
+            product[k * half : (k + 1) * half, table_at] = (value * weight_at[:, span]).astype(BF16)
+
+    def near(i, carry):
+        weigh(i, span_of(i, CHUNK), phi, weight, span_of(i, CHUNK))
+        return carry
+
+    def distant(i, carry):
+        weigh(i, span_of(i + steps, CHUNK), far_phi, far_weight, span_of(i, CHUNK))
+        return carry
+
+    lax.fori_loop(0, steps, near, 0)
+    lax.fori_loop(0, steps, distant, 0)
+    share = channels // 2
+    third = share // 3
+    for t in range(3):
+        away = pl.ds(pl.multiple_of((1 - x) * share + t * third, third), third)
+        home = pl.ds(pl.multiple_of(x * share + t * third, third), third)
+        columns = slice(t * third, (t + 1) * third)
+        send_ref[:, columns] = (-dot_nn(product[...], table[:, away])).astype(BF16)
+        keep_ref[:, columns] = -dot_nn(product[...], table[:, home])
+
+
+def place_kernel(place, keep, came, out_ref):
+    x = place[0]
+    half = keep.shape[0] // NC
+    mine = keep[...]
+    theirs = came[...].astype(F32)
+    lower = jnp.where(x == 0, mine, theirs)
+    upper = jnp.where(x == 0, theirs, mine)
+    for k in range(NC):
+        rows = slice(k * half, (k + 1) * half)
+        out_ref[:, k, :] = jnp.concatenate([lower[rows], upper[rows]], axis=0).T
+
+
+VMEM_SPEC = pl.BlockSpec(memory_space=pltpu.VMEM)
+SMEM_SPEC = pl.BlockSpec(memory_space=pltpu.SMEM)
+HBM_SPEC = pl.BlockSpec(memory_space=pl.ANY)
+
+
+def shards_by_table(orbitals, continuum, harmonic_table, ang_weight, channel_lm):
+    quad, channels = harmonic_table.shape
+    points = orbitals.shape[1]
+    half = points // 2
+    step = LOG_SPAN / (points * lax.axis_size("grid"))
+    x = lax.axis_index("orb")
+    g = lax.axis_index("grid")
+    core, y, z = g % 2, (g // 2) % 2, g // 4
+    across = [(0, 1), (1, 0)]
+    everyone = range(16)
+
+    def over_x(value):
+        return lax.ppermute(value, "orb", across)
+
+    def flip(value, bits):
+        return lax.ppermute(value, "grid", [(n, n ^ bits) for n in everyone])
+
+    pieces = 8
+    size = quad // pieces
+    corner = 2 * (z % 2) + y
+
+    def offset(which, side):
+        return (which * 2 + side) * size
+
+    def slab(which):
+        return lax.dynamic_slice_in_dim(harmonic_table, offset(which, core), size)
+
+    own = orbitals[0]
+    other = over_x(own)
+    weight = ang_weight[None, :]
+    far_weight = over_x(weight)
+    first = over_x(slab(corner))
+    last = over_x(slab(corner ^ 3))
+    by_y = flip(first, 2)
+    by_z = flip(first, 4)
+    received = [first, last, by_y, by_z]
+    which = [corner, corner ^ 3, corner ^ 1, corner ^ 2]
+    far = received + [flip(value, 1) for value in received]
+    offsets = [offset(w, core) for w in which] + [offset(w, 1 - core) for w in which]
+    place = jnp.stack([x] + offsets).astype(jnp.int32)
+
+    degree = channel_degree(channel_lm)[None, :]
+    cont = continuum.reshape(NC * points, channels)
+    part, phi, ends = pl.pallas_call(
+        functools.partial(own_kernel, step),
+        out_shape=(
+            jax.ShapeDtypeStruct((NP * half, channels), BF16),
+            jax.ShapeDtypeStruct((NI * half, quad), BF16),
+            jax.ShapeDtypeStruct((4 * NP, channels), F32),
+        ),
+        in_specs=[SMEM_SPEC] + [VMEM_SPEC] * 5 + [HBM_SPEC],
+        out_specs=(VMEM_SPEC,) * 3,
+        scratch_shapes=[
+            pltpu.VMEM((quad, channels), BF16),
+            pltpu.VMEM(((NI + NC) * points, channels), BF16),
+            pltpu.VMEM((NP * points, quad), BF16),
+            pltpu.VMEM((NP * points, TILE), F32),
+            pltpu.SemaphoreType.DMA((quad // CHUNK,)),
+        ],
+        compiler_params=pltpu.CompilerParams(vmem_limit_bytes=40 << 20),
+        name="own_half",
+    )(place, own, other, cont, weight, degree, harmonic_table)
+
+    ends = (ends + over_x(ends.astype(BF16)).astype(F32)).reshape(4, NP, channels)
+    ahead_rate = (degree + 1.0) * step
+    behind_rate = degree * step
+
+    def ahead_by(count):
+        return jnp.exp(-ahead_rate * count)
+
+    def behind_by(count):
+        return jnp.exp(-behind_rate * count)
+
+    low_end, high_end, low_start, high_start = ends[0], ends[1], ends[2], ends[3]
+    block_end = high_end + ahead_by(half) * low_end
+    block_start = low_start + behind_by(half) * high_start
+    u = g % 4
+    both = jnp.concatenate([block_end, block_start], axis=0)
+    message = both.astype(BF16)
+    earlier = jnp.zeros((NP, channels), F32)
+    later = jnp.zeros((NP, channels), F32)
+    row_end = ahead_by(points * (3 - u)) * block_end
+    row_start = behind_by(points * u) * block_start
+    for bits in (1, 2, 3):
+        came = flip(message, bits).astype(F32)
+        v = u ^ bits
+        distance = jnp.abs(u - v) - 1
+        before = v < u
+        earlier += jnp.where(before, ahead_by(points * distance), 0.0) * came[:NP]
+        later += jnp.where(before, 0.0, behind_by(points * distance)) * came[NP:]
+        row_end += ahead_by(points * (3 - v)) * came[:NP]
+        row_start += behind_by(points * v) * came[NP:]
+    row_end, row_start = row_end.astype(BF16), row_start.astype(BF16)
+    for shift in (1, 2, 3):
+        message = jnp.where(z + shift < 4, row_end, row_start)
+        came = lax.ppermute(message, "grid", [(n, (n + 4 * shift) % 16) for n in everyone])
+        came = came.astype(F32)
+        source = (z - shift) % 4
+        before = source < z
+        distance = jnp.abs(z - source) - 1
+        earlier += jnp.where(before, ahead_by(points * (4 * distance + u)), 0.0) * came
+        later += jnp.where(before, 0.0, behind_by(points * (4 * distance + 3 - u))) * came
+    upper = x == 1
+    earlier = jnp.where(upper, low_end + ahead_by(half) * earlier, earlier)
+    later = jnp.where(upper, later, high_start + behind_by(half) * later)
+
+    send, keep = pl.pallas_call(
+        functools.partial(finish_kernel, step, pieces),
+        out_shape=(
+            jax.ShapeDtypeStruct((NC * half, channels // 2), BF16),
+            jax.ShapeDtypeStruct((NC * half, channels // 2), F32),
+        ),
+        in_specs=[SMEM_SPEC] + [VMEM_SPEC] * 10 + [HBM_SPEC] * (1 + pieces),
+        out_specs=(VMEM_SPEC,) * 2,
+        scratch_shapes=[
+            pltpu.VMEM((2 * quad, channels), BF16),
+            pltpu.VMEM(((NI + NC) * half, channels), BF16),
+            pltpu.VMEM((NP * half, quad), BF16),
+            pltpu.VMEM((NI * half, quad), BF16),
+            pltpu.VMEM((NP * half, channels), BF16),
+            pltpu.VMEM((NC * half, 2 * quad), BF16),
+            pltpu.VMEM((NP, half, TILE), F32),
+            pltpu.VMEM((NP, half, TILE), F32),
+            pltpu.SemaphoreType.DMA((pieces + 1,)),
+        ],
+        compiler_params=pltpu.CompilerParams(vmem_limit_bytes=48 << 20),
+        name="finish",
+    )(place, own, other, cont, weight, far_weight, degree, earlier, later, part, phi, harmonic_table, *far)
+    came = over_x(send)
+    block = 128
+    return pl.pallas_call(
+        place_kernel,
+        grid=(channels // 2 // block,),
+        out_shape=jax.ShapeDtypeStruct((channels // 2, NC, points), F32),
+        in_specs=[
+            SMEM_SPEC,
+            pl.BlockSpec((NC * half, block), lambda i: (0, i)),
+            pl.BlockSpec((NC * half, block), lambda i: (0, i)),
+        ],
+        out_specs=pl.BlockSpec((block, NC, points), lambda i: (i, 0, 0)),
+        name="place",
+    )(place, keep, came)
+
+
 def solution(mesh):
+    small = dict(mesh.shape) == {"orb": 2, "grid": 16}
     return jax.shard_map(
-        shards,
+        shards_by_table if small else shards,
         mesh=mesh,
         in_specs=(P("orb", "grid", None), P(None, "grid", None), P("orb", None), P("orb"), P()),
         out_specs=P("orb", None, "grid"),

time: 543 us -> 127 us (0.23); the launches traced: 537 us -> 126 us
  local copies, waits for them, and re-layouts: 180 us -> 12.9 us
  other arithmetic: 118 us -> 4.38 us
  waiting for transfers between devices: 128 us -> 49.6 us
  blocking collectives: 65.8 us -> 0 us
  Pallas kernels: 0 us -> 36.7 us
  matrix products: 24.2 us -> 0 us
  starting transfers between devices: 5.71 us -> 22.7 us
  between operations: 15 us -> 0.24 us
    add x30 -> x1, other arithmetic: 96.4 us -> 0.03 us  [shards_by_table(): ends + over_x(ends.astype(BF16)).astype(F32)]
    reduce_scatter x2 -> x0, waiting for transfers between devices: 71.2 us -> none  [the longest x1 36.3 us: shards(): lax.psum_scatter(jnp.einsum('al,ikra->ikrl', analysis, pair_values, prefe...]
    slice x48 -> x0, local copies, waits for them, and re-layouts: 68.4 us -> none  [the longest x15 36.5 us: line_sums(): forward_blocks[:, :, :, :block_size - distance]]
    unnamed x179 -> x32, local copies, waits for them, and re-layouts: 69.2 us -> 6.36 us
    all_to_all x1 -> x0, blocking collectives: 54.9 us -> none  [shards(): lax.all_to_all(potential, 'grid', split_axis=2, concat_axis=3, tiled=True)]
    ppermute x0 -> x18, waiting for transfers between devices: none -> 49.6 us  [the longest x6 28.7 us: over_x(): return lax.ppermute(value, 'orb', across)]
    pallas_call x0 -> x3, Pallas kernels: none -> 36.7 us  [the longest x1 20.8 us: shards_by_table(): pl.pallas_call(functools.partial(finish_kernel, step, pieces), out_shape=...]
    all_gather x1 -> x0, waiting for transfers between devices: 35.7 us -> none  [shards(): lax.all_gather(radial_potential, 'orb', axis=0, tiled=True)]
  transfers between devices with their start and end apart: 4 -> 18, of which waited for: 4 -> 9; matrix products, arithmetic and copies ran while one was open for 1% -> 6% of each run, Pallas kernels for 0% -> 7%
where the time goes in v1:
time: 127 us; the launch traced here: 126 us
  waiting for transfers between devices  49.6 us (39%)
  Pallas kernels  36.7 us (29%)
  starting transfers between devices  22.7 us (18%)
  local copies, waits for them, and re-layouts  12.9 us (10%)
  other arithmetic  4.38 us (3%)
    ppermute x6, waiting for transfers between devices, over_x(): return lax.ppermute(value, 'orb', across)  28.7 us
    pallas_call x1, Pallas kernels, shards_by_table(): pl.pallas_call(functools.partial(finish_kernel, step, pieces), out_shape=...  20.8 us
    ppermute x3, waiting for transfers between devices, shards_by_table(): lax.ppermute(message, 'grid', [(n, (n + 4 * shift) % 16) for n in everyone])  15.2 us
    ppermute x6, starting transfers between devices, over_x(): return lax.ppermute(value, 'orb', across)  10.2 us
    pallas_call x1, Pallas kernels, shards_by_table(): pl.pallas_call(functools.partial(own_kernel, step), out_shape=(jax.ShapeD...  9.35 us
    pallas_call x1, Pallas kernels, shards_by_table(): pl.pallas_call(place_kernel, grid=(channels // 2 // block,), out_shape=ja...  6.5 us
    ppermute x3, starting transfers between devices, shards_by_table(): lax.ppermute(message, 'grid', [(n, (n + 4 * shift) % 16) for n in everyone])  6.37 us
    unnamed x32, local copies, waits for them, and re-layouts  6.36 us
  transfers between devices with their start and end apart: 18, of which 9 were waited for; matrix products, arithmetic and copies ran while one was open for 6% of the time, Pallas kernels for 7%

profile of v1, /device:TPU:0, one launch (start us, length us, event | category | flops | bytes accessed | tf_op | source)
XLA Modules:
  0.0 126.5 jit_solution(9125193888125211559)
XLA Ops:
  0.0 3.0 %collective-permute-start = (bf16[64,2304]{1,0:T(8,128)(2,1)}, bf16[64,2304]{1,0:T(8,128)(2,1)S(1)}, u32[]{:S(2)}, u32[]{:S(2)}) collective-permute-start(bf16[64,2304]{1,0:T(8,128)(2,1)} %bitcast.13), channel_id=1, source_target_pairs={{0,16},{16,0},{1,17},{17,1},{2,18},{18,2},{3,19},{19,3},{4,20},{20... | collective-permute-start | bytes 884744 | tf_op jit(solution)/shard_map/ppermute | solution.py:346
  3.0 2.6 %constant_dynamic-slice_fusion = (bf16[160,2304]{1,0:T(8,128)(2,1)}, bf16[160,2304]{1,0:T(8,128)(2,1)}) fusion(bf16[1280,2304]{1,0:T(8,128)(2,1)} %refs_0_.1, s32[]{:T(128)S(6)} %select_n.237, s32[]{:T(128)S(6)} %select_n.236), kind=kLoop, calls=%fused_computation.51 | loop fusion | bytes 2949128 | tf_op jit(solution)/shard_map/dynamic_slice | solution.py:359
  5.6 0.2 collective-permute-start.9
  5.8 1.8 %collective-permute-start.10 = (bf16[160,2304]{1,0:T(8,128)(2,1)}, bf16[160,2304]{1,0:T(8,128)(2,1)S(1)}, u32[]{:S(2)}, u32[]{:S(2)}) collective-permute-start(bf16[160,2304]{1,0:T(8,128)(2,1)} %get-tuple-element.18), channel_id=1, source_target_pairs={{0,16},{16,0},{1,17},{17,1},{2,18},{18,2},{3,19},{19,3},{4,20},{20... | collective-permute-start | bytes 2211848 | tf_op jit(solution)/shard_map/ppermute | solution.py:346
  7.6 0.0 copy-done.14
  7.6 0.1 convert_reduce_fusion
  7.8 0.0 copy-done.15
  7.9 0.1 stack.39.place
  7.9 3.1 %collective-permute-done.other = bf16[64,2304]{1,0:T(8,128)(2,1)S(1)} collective-permute-done((bf16[64,2304]{1,0:T(8,128)(2,1)}, bf16[64,2304]{1,0:T(8,128)(2,1)S(1)}, u32[]{:S(2)}, u32[]{:S(2)}) %collective-permute-start) | collective-permute-done | bytes 294944 | tf_op jit(solution)/shard_map/ppermute | solution.py:346
  11.1 0.0 copy-done.3
  11.1 0.0 copy-done.1
  11.1 2.7 %copy-done = bf16[1280,2304]{1,0:T(8,128)(2,1)S(1)} copy-done((bf16[1280,2304]{1,0:T(8,128)(2,1)S(1)}, bf16[1280,2304]{1,0:T(8,128)(2,1)}, u32[]{:S(2)}) %copy-start) | copy-done | bytes 5898264
  13.8 9.3 %own_half.1 = (bf16[256,2304]{1,0:T(8,128)(2,1)S(1)}, bf16[64,1280]{1,0:T(8,128)(2,1)S(1)}, f32[32,2304]{1,0:T(8,128)S(1)}) custom-call(s32[9]{0:T(128)S(1)} %stack.39.place, bf16[64,2304]{1,0:T(8,128)(2,1)S(1)} %bitcast.14, bf16[64,2304]{1,0:T(8,128)(2,1)S(1)} %collective-permute-done.other, bf16[256,2304]{1,0:T(8,128)(2,1)S(1)} %bitcast.12, ...), custom_call_target="tpu_custom_call" | custom-call | tf_op jit(solution)/shard_map/own_half/pallas_call | solution.py:377
  23.1 0.0 copy-start.2
  23.1 1.0 copy-done.2
  24.1 2.1 %collective-permute-start.2 = (bf16[32,2304]{1,0:T(8,128)(2,1)S(1)}, bf16[32,2304]{1,0:T(8,128)(2,1)S(1)}, u32[]{:S(2)}, u32[]{:S(2)}) collective-permute-start(bf16[32,2304]{1,0:T(8,128)(2,1)S(1)} %convert_element_type.89), channel_id=1, source_target_pairs={{0,16},{16,0},{1,17},{17,1},{2,18},{18,2},{3,19},{19,3},{4,20},{20... | collective-permute-start | bytes 442376 | tf_op jit(solution)/shard_map/ppermute | solution.py:346
  26.3 0.7 exponential_select_fusion.5
  27.0 18.0 %collective-permute-done.2 = bf16[32,2304]{1,0:T(8,128)(2,1)S(1)} collective-permute-done((bf16[32,2304]{1,0:T(8,128)(2,1)S(1)}, bf16[32,2304]{1,0:T(8,128)(2,1)S(1)}, u32[]{:S(2)}, u32[]{:S(2)}) %collective-permute-start.2) | collective-permute-done | bytes 147488 | tf_op jit(solution)/shard_map/ppermute | solution.py:346
  45.0 0.0 copy-start.6
  45.1 0.1 collective-permute-start.3
  45.2 1.8 %collective-permute-start.4 = (bf16[16,2304]{1,0:T(8,128)(2,1)S(1)}, bf16[16,2304]{1,0:T(8,128)(2,1)S(1)}, u32[]{:S(2)}, u32[]{:S(2)}) collective-permute-start(bf16[16,2304]{1,0:T(8,128)(2,1)S(1)} %pad_maximum_fusion), channel_id=1, source_target_pairs={{0,2},{1,3},{2,0},{3,1},{4,6},{5,7},{6,4},{7,5},{8,10},{9,11},{10,... | collective-permute-start | bytes 221192 | tf_op jit(solution)/shard_map/ppermute | solution.py:349
  47.0 0.1 collective-permute-start.5
  47.1 0.6 exponential_select_fusion.2
  47.7 0.0 collective-permute-done.3
  47.7 0.0 copy-start.7
  47.7 2.1 %collective-permute-done.4 = bf16[16,2304]{1,0:T(8,128)(2,1)S(1)} collective-permute-done((bf16[16,2304]{1,0:T(8,128)(2,1)S(1)}, bf16[16,2304]{1,0:T(8,128)(2,1)S(1)}, u32[]{:S(2)}, u32[]{:S(2)}) %collective-permute-start.4) | collective-permute-done | bytes 73760 | tf_op jit(solution)/shard_map/ppermute | solution.py:349
  49.9 0.0 copy-start.8
  49.9 1.3 %collective-permute-done.5 = bf16[16,2304]{1,0:T(8,128)(2,1)S(1)} collective-permute-done((bf16[16,2304]{1,0:T(8,128)(2,1)S(1)}, bf16[16,2304]{1,0:T(8,128)(2,1)S(1)}, u32[]{:S(2)}, u32[]{:S(2)}) %collective-permute-start.5) | collective-permute-done | bytes 73760 | tf_op jit(solution)/shard_map/ppermute | solution.py:349
  51.3 0.7 broadcast_select_fusion.2
  52.0 0.0 collective-permute-done.9.refs_1_
  52.0 1.6 %collective-permute-start.11 = (bf16[160,2304]{1,0:T(8,128)(2,1)S(1)}, bf16[160,2304]{1,0:T(8,128)(2,1)S(1)}, u32[]{:S(2)}, u32[]{:S(2)}) collective-permute-start(bf16[160,2304]{1,0:T(8,128)(2,1)S(1)} %collective-permute-done.9.refs_1_), channel_id=1, source_target_pairs={{0,2},{1,3},{2,0},{3,1},{4,6},{5,7},{6,4},{7,5},{8,10},{9,11},{10,... | collective-permute-start | bytes 2211848 | tf_op jit(solution)/shard_map/ppermute | solution.py:349
  53.6 1.6 %collective-permute-start.12 = (bf16[160,2304]{1,0:T(8,128)(2,1)S(1)}, bf16[160,2304]{1,0:T(8,128)(2,1)}, u32[]{:S(2)}, u32[]{:S(2)}) collective-permute-start(bf16[160,2304]{1,0:T(8,128)(2,1)S(1)} %collective-permute-done.9.refs_1_), channel_id=1, source_target_pairs={{0,4},{1,5},{2,6},{3,7},{4,0},{5,1},{6,2},{7,3},{8,12},{9,13},{10,... | collective-permute-start | bytes 2211848 | tf_op jit(solution)/shard_map/ppermute | solution.py:349
  55.1 2.7 %collective-permute-start.7 = (bf16[8,2304]{1,0:T(8,128)(2,1)S(1)}, bf16[8,2304]{1,0:T(8,128)(2,1)S(1)}, u32[]{:S(2)}, u32[]{:S(2)}) collective-permute-start(bf16[8,2304]{1,0:T(8,128)(2,1)S(1)} %get-tuple-element.22), channel_id=1, source_target_pairs={{0,8},{1,9},{2,10},{3,11},{4,12},{5,13},{6,14},{7,15},{8,0},{9,1},... | collective-permute-start | bytes 110600 | tf_op jit(solution)/shard_map/ppermute | solution.py:429
  57.8 0.2 collective-permute-start.8
  58.0 14.2 %collective-permute-done.7 = bf16[8,2304]{1,0:T(8,128)(2,1)S(1)} collective-permute-done((bf16[8,2304]{1,0:T(8,128)(2,1)S(1)}, bf16[8,2304]{1,0:T(8,128)(2,1)S(1)}, u32[]{:S(2)}, u32[]{:S(2)}) %collective-permute-start.7) | collective-permute-done | bytes 36896 | tf_op jit(solution)/shard_map/ppermute | solution.py:429
  72.2 3.5 %collective-permute-start.6 = (bf16[8,2304]{1,0:T(8,128)(2,1)}, bf16[8,2304]{1,0:T(8,128)(2,1)S(1)}, u32[]{:S(2)}, u32[]{:S(2)}) collective-permute-start(bf16[8,2304]{1,0:T(8,128)(2,1)} %get-tuple-element.15), channel_id=1, source_target_pairs={{0,4},{1,5},{2,6},{3,7},{4,8},{5,9},{6,10},{7,11},{8,12},{9,13},{1... | collective-permute-start | bytes 110600 | tf_op jit(solution)/shard_map/ppermute | solution.py:429
  75.7 0.0 collective-permute-done.8
  75.7 1.5 %collective-permute-start.1 = (f32[1,1280]{1,0:T(1,128)S(1)}, f32[1,1280]{1,0:T(1,128)S(1)}, u32[]{:S(2)}, u32[]{:S(2)}) collective-permute-start(f32[1,1280]{1,0:T(1,128)S(1)} %broadcast_in_dim.24.weight), channel_id=1, source_target_pairs={{0,16},{16,0},{1,17},{17,1},{2,18},{18,2},{3,19},{19,3},{4,20},{20... | collective-permute-start | bytes 15368 | tf_op jit(solution)/shard_map/ppermute | solution.py:346
  77.2 1.0 collective-permute-done.6
  78.2 0.0 collective-permute-start.13
  78.2 0.0 collective-permute-done.10.refs_2_
  78.2 0.5 collective-permute-start.14
  78.7 0.0 collective-permute-done.11.refs_3_
  78.7 0.1 collective-permute-start.15
  78.8 0.0 collective-permute-done.12.refs_4_
  78.8 0.4 collective-permute-start.16
  79.2 1.1 add_select_fusion.later
  80.3 1.1 add_select_fusion.1.earlier
  81.4 0.0 collective-permute-done.1.far_weight
  81.4 0.0 collective-permute-done.13.refs_5_
  81.4 1.1 collective-permute-done.14.refs_6_
  82.5 1.1 collective-permute-done.15.refs_7_
  83.6 0.0 collective-permute-done.16.refs_8_
  83.6 0.0 copy-done.5
  83.6 0.8 copy-done.11
  84.4 0.2 copy-done.12
  84.7 20.8 %finish.1 = (bf16[128,1152]{1,0:T(8,128)(2,1)S(1)}, f32[128,1152]{1,0:T(8,128)S(1)}) custom-call(s32[9]{0:T(128)S(1)} %stack.39.place, bf16[64,2304]{1,0:T(8,128)(2,1)S(1)} %bitcast.15, bf16[64,2304]{1,0:T(8,128)(2,1)S(1)} %collective-permute-done.other, bf16[256,2304]{1,0:T(8,128)(2,1)} %bitcast.11, f32[1,1280]{1,0:T(1,128)S(1)} %broadcast_in_dim.24.weight, ...), custom_call_target="tpu_custom_call" | custom-call | tf_op jit(solution)/shard_map/finish/pallas_call | solution.py:440
  105.5 0.0 copy-start.4
  105.6 0.8 copy-done.4
  106.4 1.5 %collective-permute-start.17 = (bf16[128,1152]{1,0:T(8,128)(2,1)S(1)}, bf16[128,1152]{1,0:T(8,128)(2,1)S(1)}, u32[]{:S(2)}, u32[]{:S(2)}) collective-permute-start(bf16[128,1152]{1,0:T(8,128)(2,1)S(1)} %get-tuple-element.14), channel_id=1, source_target_pairs={{0,16},{16,0},{1,17},{17,1},{2,18},{18,2},{3,19},{19,3},{4,20},{20... | collective-permute-start | bytes 884744 | tf_op jit(solution)/shard_map/ppermute | solution.py:346
  107.9 7.6 %collective-permute-done.17.came = bf16[128,1152]{1,0:T(8,128)(2,1)S(1)} collective-permute-done((bf16[128,1152]{1,0:T(8,128)(2,1)S(1)}, bf16[128,1152]{1,0:T(8,128)(2,1)S(1)}, u32[]{:S(2)}, u32[]{:S(2)}) %collective-permute-start.17) | collective-permute-done | bytes 294944 | tf_op jit(solution)/shard_map/ppermute | solution.py:346
  115.4 0.7 copy-done.13
  116.1 6.5 %place.1 = f32[1152,4,64]{2,1,0:T(4,128)} custom-call(s32[9]{0:T(128)} %copy-done.5, f32[128,1152]{1,0:T(8,128)} %copy-done.4, bf16[128,1152]{1,0:T(8,128)(2,1)} %copy-done.13), custom_call_target="tpu_custom_call" | custom-call | tf_op jit(solution)/shard_map/place/pallas_call | solution.py:464
  122.7 3.8 %copy.7 = f32[1152,4,64]{0,2,1:T(8,128)} copy(f32[1152,4,64]{2,1,0:T(4,128)} %place.1) | data formatting | bytes 2359296 | tf_op jit(solution)/shard_map/place/pallas_call | solution.py:464
  (27 shorter events, 0.2 us)
Async XLA Ops:
  0.0 11.1 %copy-start.3 = (bf16[1,64,2304]{2,1,0:T(8,128)(2,1)S(1)}, bf16[1,64,2304]{2,1,0:T(8,128)(2,1)}, u32[]{:S(2)}) copy-start(bf16[1,64,2304]{2,1,0:T(8,128)(2,1)} %param.5) | copy-start | bytes 884740
  0.0 7.6 %copy-start.14 = (s32[2304]{0:T(1024)S(1)}, s32[2304]{0:T(1024)}, u32[]{:S(2)}) copy-start(s32[2304]{0:T(1024)} %param.9) | copy-start | bytes 27652
  0.0 7.8 %copy-start.15 = (f32[1280]{0:T(1024)S(1)}, f32[1280]{0:T(1024)}, u32[]{:S(2)}) copy-start(f32[1280]{0:T(1024)} %param.8) | copy-start | bytes 15364
  0.0 11.1 %copy-start.1 = (bf16[4,64,2304]{2,1,0:T(8,128)(2,1)S(1)}, bf16[4,64,2304]{2,1,0:T(8,128)(2,1)}, u32[]{:S(2)}) copy-start(bf16[4,64,2304]{2,1,0:T(8,128)(2,1)} %param.6) | copy-start | bytes 3538948
  0.0 11.1 %collective-permute-start = (bf16[64,2304]{1,0:T(8,128)(2,1)}, bf16[64,2304]{1,0:T(8,128)(2,1)S(1)}, u32[]{:S(2)}, u32[]{:S(2)}) collective-permute-start(bf16[64,2304]{1,0:T(8,128)(2,1)} %bitcast.13), channel_id=1, source_target_pairs={{0,16},{16,0},{1,17},{17,1},{2,18},{18,2},{3,19},{19,3},{4,20},{20... | collective-permute-start | bytes 884744 | tf_op jit(solution)/shard_map/ppermute | solution.py:346
  5.6 46.4 %collective-permute-start.9 = (bf16[160,2304]{1,0:T(8,128)(2,1)}, bf16[160,2304]{1,0:T(8,128)(2,1)S(1)}, u32[]{:S(2)}, u32[]{:S(2)}) collective-permute-start(bf16[160,2304]{1,0:T(8,128)(2,1)} %get-tuple-element.19), channel_id=1, source_target_pairs={{0,16},{16,0},{1,17},{17,1},{2,18},{18,2},{3,19},{19,3},{4,20},{20... | collective-permute-start | bytes 2211848 | tf_op jit(solution)/shard_map/ppermute | solution.py:346
  5.8 72.4 %collective-permute-start.10 = (bf16[160,2304]{1,0:T(8,128)(2,1)}, bf16[160,2304]{1,0:T(8,128)(2,1)S(1)}, u32[]{:S(2)}, u32[]{:S(2)}) collective-permute-start(bf16[160,2304]{1,0:T(8,128)(2,1)} %get-tuple-element.18), channel_id=1, source_target_pairs={{0,16},{16,0},{1,17},{17,1},{2,18},{18,2},{3,19},{19,3},{4,20},{20... | collective-permute-start | bytes 2211848 | tf_op jit(solution)/shard_map/ppermute | solution.py:346
  7.9 75.6 %copy-start.5 = (s32[9]{0:T(128)}, s32[9]{0:T(128)S(1)}, u32[]{:S(2)}) copy-start(s32[9]{0:T(128)S(1)} %stack.39.place) | copy-start | bytes 112
  11.1 2.7 %copy-start = (bf16[1280,2304]{1,0:T(8,128)(2,1)S(1)}, bf16[1280,2304]{1,0:T(8,128)(2,1)}, u32[]{:S(2)}) copy-start(bf16[1280,2304]{1,0:T(8,128)(2,1)} %refs_0_.1) | copy-start | bytes 17694724
  23.1 1.0 copy-start.2
  24.1 20.9 %collective-permute-start.2 = (bf16[32,2304]{1,0:T(8,128)(2,1)S(1)}, bf16[32,2304]{1,0:T(8,128)(2,1)S(1)}, u32[]{:S(2)}, u32[]{:S(2)}) collective-permute-start(bf16[32,2304]{1,0:T(8,128)(2,1)S(1)} %convert_element_type.89), channel_id=1, source_target_pairs={{0,16},{16,0},{1,17},{17,1},{2,18},{18,2},{3,19},{19,3},{4,20},{20... | collective-permute-start | bytes 442376 | tf_op jit(solution)/shard_map/ppermute | solution.py:346
  45.0 35.3 %copy-start.6 = (f32[32,2304]{1,0:T(8,128)}, f32[32,2304]{1,0:T(8,128)S(1)}, u32[]{:S(2)}) copy-start(f32[32,2304]{1,0:T(8,128)S(1)} %convert_add_fusion) | copy-start | bytes 884740
  45.1 2.6 %collective-permute-start.3 = (bf16[16,2304]{1,0:T(8,128)(2,1)S(1)}, bf16[16,2304]{1,0:T(8,128)(2,1)S(1)}, u32[]{:S(2)}, u32[]{:S(2)}) collective-permute-start(bf16[16,2304]{1,0:T(8,128)(2,1)S(1)} %pad_maximum_fusion), channel_id=1, source_target_pairs={{0,1},{1,0},{2,3},{3,2},{4,5},{5,4},{6,7},{7,6},{8,9},{9,8},{10,11... | collective-permute-start | bytes 221192 | tf_op jit(solution)/shard_map/ppermute | solution.py:349
  45.2 4.7 %collective-permute-start.4 = (bf16[16,2304]{1,0:T(8,128)(2,1)S(1)}, bf16[16,2304]{1,0:T(8,128)(2,1)S(1)}, u32[]{:S(2)}, u32[]{:S(2)}) collective-permute-start(bf16[16,2304]{1,0:T(8,128)(2,1)S(1)} %pad_maximum_fusion), channel_id=1, source_target_pairs={{0,2},{1,3},{2,0},{3,1},{4,6},{5,7},{6,4},{7,5},{8,10},{9,11},{10,... | collective-permute-start | bytes 221192 | tf_op jit(solution)/shard_map/ppermute | solution.py:349
  47.0 4.2 %collective-permute-start.5 = (bf16[16,2304]{1,0:T(8,128)(2,1)S(1)}, bf16[16,2304]{1,0:T(8,128)(2,1)S(1)}, u32[]{:S(2)}, u32[]{:S(2)}) collective-permute-start(bf16[16,2304]{1,0:T(8,128)(2,1)S(1)} %pad_maximum_fusion), channel_id=1, source_target_pairs={{0,3},{1,2},{2,1},{3,0},{4,7},{5,6},{6,5},{7,4},{8,11},{9,10},{10,... | collective-permute-start | bytes 221192 | tf_op jit(solution)/shard_map/ppermute | solution.py:349
  47.7 4.2 %copy-start.7 = (f32[16,2304]{1,0:T(8,128)}, f32[16,2304]{1,0:T(8,128)S(1)}, u32[]{:S(2)}) copy-start(f32[16,2304]{1,0:T(8,128)S(1)} %convert_element_type.92) | copy-start | bytes 442372
  49.9 2.1 %copy-start.8 = (f32[16,2304]{1,0:T(8,128)}, f32[16,2304]{1,0:T(8,128)S(1)}, u32[]{:S(2)}) copy-start(f32[16,2304]{1,0:T(8,128)S(1)} %convert_element_type.94) | copy-start | bytes 442372
  51.2 0.7 copy-start.9
  52.0 26.7 %collective-permute-start.11 = (bf16[160,2304]{1,0:T(8,128)(2,1)S(1)}, bf16[160,2304]{1,0:T(8,128)(2,1)S(1)}, u32[]{:S(2)}, u32[]{:S(2)}) collective-permute-start(bf16[160,2304]{1,0:T(8,128)(2,1)S(1)} %collective-permute-done.9.refs_1_), channel_id=1, source_target_pairs={{0,2},{1,3},{2,0},{3,1},{4,6},{5,7},{6,4},{7,5},{8,10},{9,11},{10,... | collective-permute-start | bytes 2211848 | tf_op jit(solution)/shard_map/ppermute | solution.py:349
  53.6 25.2 %collective-permute-start.12 = (bf16[160,2304]{1,0:T(8,128)(2,1)S(1)}, bf16[160,2304]{1,0:T(8,128)(2,1)}, u32[]{:S(2)}, u32[]{:S(2)}) collective-permute-start(bf16[160,2304]{1,0:T(8,128)(2,1)S(1)} %collective-permute-done.9.refs_1_), channel_id=1, source_target_pairs={{0,4},{1,5},{2,6},{3,7},{4,0},{5,1},{6,2},{7,3},{8,12},{9,13},{10,... | collective-permute-start | bytes 2211848 | tf_op jit(solution)/shard_map/ppermute | solution.py:349
  55.1 17.1 %collective-permute-start.7 = (bf16[8,2304]{1,0:T(8,128)(2,1)S(1)}, bf16[8,2304]{1,0:T(8,128)(2,1)S(1)}, u32[]{:S(2)}, u32[]{:S(2)}) collective-permute-start(bf16[8,2304]{1,0:T(8,128)(2,1)S(1)} %get-tuple-element.22), channel_id=1, source_target_pairs={{0,8},{1,9},{2,10},{3,11},{4,12},{5,13},{6,14},{7,15},{8,0},{9,1},... | collective-permute-start | bytes 110600 | tf_op jit(solution)/shard_map/ppermute | solution.py:429
  57.8 17.9 %collective-permute-start.8 = (bf16[8,2304]{1,0:T(8,128)(2,1)S(1)}, bf16[8,2304]{1,0:T(8,128)(2,1)S(1)}, u32[]{:S(2)}, u32[]{:S(2)}) collective-permute-start(bf16[8,2304]{1,0:T(8,128)(2,1)S(1)} %get-tuple-element.23), channel_id=1, source_target_pairs={{0,12},{1,13},{2,14},{3,15},{4,0},{5,1},{6,2},{7,3},{8,4},{9,5},{1... | collective-permute-start | bytes 110600 | tf_op jit(solution)/shard_map/ppermute | solution.py:429
  72.2 6.0 %collective-permute-start.6 = (bf16[8,2304]{1,0:T(8,128)(2,1)}, bf16[8,2304]{1,0:T(8,128)(2,1)S(1)}, u32[]{:S(2)}, u32[]{:S(2)}) collective-permute-start(bf16[8,2304]{1,0:T(8,128)(2,1)} %get-tuple-element.15), channel_id=1, source_target_pairs={{0,4},{1,5},{2,6},{3,7},{4,8},{5,9},{6,10},{7,11},{8,12},{9,13},{1... | collective-permute-start | bytes 110600 | tf_op jit(solution)/shard_map/ppermute | solution.py:429
  75.7 5.7 %collective-permute-start.1 = (f32[1,1280]{1,0:T(1,128)S(1)}, f32[1,1280]{1,0:T(1,128)S(1)}, u32[]{:S(2)}, u32[]{:S(2)}) collective-permute-start(f32[1,1280]{1,0:T(1,128)S(1)} %broadcast_in_dim.24.weight), channel_id=1, source_target_pairs={{0,16},{16,0},{1,17},{17,1},{2,18},{18,2},{3,19},{19,3},{4,20},{20... | collective-permute-start | bytes 15368 | tf_op jit(solution)/shard_map/ppermute | solution.py:346
  78.2 3.2 %collective-permute-start.13 = (bf16[160,2304]{1,0:T(8,128)(2,1)S(1)}, bf16[160,2304]{1,0:T(8,128)(2,1)S(1)}, u32[]{:S(2)}, u32[]{:S(2)}) collective-permute-start(bf16[160,2304]{1,0:T(8,128)(2,1)S(1)} %collective-permute-done.9.refs_1_), channel_id=1, source_target_pairs={{0,1},{1,0},{2,3},{3,2},{4,5},{5,4},{6,7},{7,6},{8,9},{9,8},{10,11... | collective-permute-start | bytes 2211848 | tf_op jit(solution)/shard_map/ppermute | solution.py:349
  78.2 4.3 %collective-permute-start.14 = (bf16[160,2304]{1,0:T(8,128)(2,1)S(1)}, bf16[160,2304]{1,0:T(8,128)(2,1)S(1)}, u32[]{:S(2)}, u32[]{:S(2)}) collective-permute-start(bf16[160,2304]{1,0:T(8,128)(2,1)S(1)} %collective-permute-done.10.refs_2_), channel_id=1, source_target_pairs={{0,1},{1,0},{2,3},{3,2},{4,5},{5,4},{6,7},{7,6},{8,9},{9,8},{10,11... | collective-permute-start | bytes 2211848 | tf_op jit(solution)/shard_map/ppermute | solution.py:349
  78.7 4.9 %collective-permute-start.15 = (bf16[160,2304]{1,0:T(8,128)(2,1)S(1)}, bf16[160,2304]{1,0:T(8,128)(2,1)S(1)}, u32[]{:S(2)}, u32[]{:S(2)}) collective-permute-start(bf16[160,2304]{1,0:T(8,128)(2,1)S(1)} %collective-permute-done.11.refs_3_), channel_id=1, source_target_pairs={{0,1},{1,0},{2,3},{3,2},{4,5},{5,4},{6,7},{7,6},{8,9},{9,8},{10,11... | collective-permute-start | bytes 2211848 | tf_op jit(solution)/shard_map/ppermute | solution.py:349
  78.8 4.8 %collective-permute-start.16 = (bf16[160,2304]{1,0:T(8,128)(2,1)}, bf16[160,2304]{1,0:T(8,128)(2,1)S(1)}, u32[]{:S(2)}, u32[]{:S(2)}) collective-permute-start(bf16[160,2304]{1,0:T(8,128)(2,1)} %collective-permute-done.12.refs_4_), channel_id=1, source_target_pairs={{0,1},{1,0},{2,3},{3,2},{4,5},{5,4},{6,7},{7,6},{8,9},{9,8},{10,11... | collective-permute-start | bytes 2211848 | tf_op jit(solution)/shard_map/ppermute | solution.py:349
  82.5 1.1 copy-start.10
  83.6 0.9 copy-start.11
  83.6 1.1 copy-start.12
  105.5 0.8 copy-start.4
  106.4 9.1 %collective-permute-start.17 = (bf16[128,1152]{1,0:T(8,128)(2,1)S(1)}, bf16[128,1152]{1,0:T(8,128)(2,1)S(1)}, u32[]{:S(2)}, u32[]{:S(2)}) collective-permute-start(bf16[128,1152]{1,0:T(8,128)(2,1)S(1)} %get-tuple-element.14), channel_id=1, source_target_pairs={{0,16},{16,0},{1,17},{17,1},{2,18},{18,2},{3,19},{19,3},{4,20},{20... | collective-permute-start | bytes 884744 | tf_op jit(solution)/shard_map/ppermute | solution.py:346
  115.4 0.7 copy-start.13

commit v2 on v1

--- a/solution.py
+++ b/solution.py
@@ -170,36 +170,21 @@
             pairs[row : row + points, span] = product.astype(BF16)
 
 
-def own_kernel(
-    step, place, own, other, cont, weight, degree_ref, table_hbm,
-    part_ref, phi_ref, ends_ref,
-    table, rows, pairs, work, sems,
-):
-    x = place[0]
-    points = own.shape[0]
-    half = points // 2
+def angular_density(step, x, values_of, store, table, weight, degree_ref, part_ref, ends_at, pairs, work):
+    half = part_ref.shape[0] // NC
+    points = 2 * half
     steps = table.shape[0] // CHUNK
 
-    def fetch(i):
-        return pltpu.make_async_copy(
-            table_hbm.at[span_of(i, CHUNK)], table.at[span_of(i, CHUNK)], sems.at[i]
-        )
-
-    for i in range(steps):
-        fetch(i).start()
-    rows[span_of(x, points), :] = own[...]
-    rows[span_of(1 - x, points), :] = other[...]
-    rows[NI * points :, :] = cont[...]
-
     def angular(i, carry):
-        fetch(i).wait()
         span = span_of(i, CHUNK)
-        values = dot_nt(rows[...], table[span, :]).astype(BF16)
-        store_pairs(values, weight[:, span], points, pairs, span)
-        for o in range(NI):
-            lower = values[o * points : o * points + half]
-            upper = values[o * points + half : (o + 1) * points]
-            phi_ref[o * half : (o + 1) * half, span] = jnp.where(x == 0, lower, upper)
+        phi, psi = values_of(i, span)
+        low_high = phi.reshape(2, half, CHUNK)
+        store(span, jnp.where(x == 0, low_high[0], low_high[1]), psi)
+        phi = phi.astype(F32) * weight[:, span]
+        psi = psi.astype(F32)
+        for k in range(NC):
+            rows = slice(k * points, (k + 1) * points)
+            pairs[rows, span] = (phi * psi[rows]).astype(BF16)
         return carry
 
     lax.fori_loop(0, steps, angular, 0)
@@ -211,51 +196,122 @@
         position = lax.broadcasted_iota(jnp.int32, (half, TILE), 0).astype(F32)
         ahead = jnp.exp((degree + 1.0) * step * (position - (half - 1.0)))
         behind = jnp.exp(-degree * step * position)
-        for p in range(NP):
-            low = work[p * points : p * points + half, :]
-            high = work[p * points + half : (p + 1) * points, :]
-            part_ref[p * half : (p + 1) * half, span] = jnp.where(x == 0, low, high).astype(BF16)
+        for k in range(NC):
+            low = work[k * points : k * points + half, :]
+            high = work[k * points + half : (k + 1) * points, :]
+            part_ref[k * half : (k + 1) * half, span] = jnp.where(x == 0, low, high).astype(BF16)
             ends = (low * ahead, high * ahead, low * behind, high * behind)
             for n in range(4):
-                ends_ref[n * NP + p : n * NP + p + 1, span] = jnp.sum(ends[n], axis=0, keepdims=True)
+                ends_at(n, k, span, jnp.sum(ends[n], axis=0, keepdims=True))
         return carry
 
     lax.fori_loop(0, table.shape[1] // TILE, density, 0)
 
 
+def own_kernel(
+    step, place, own, cont, weight, degree_ref, table_hbm,
+    part_ref, phi_ref, psi_ref, ends_ref, table,
+    rows, pairs, work, sems,
+):
+    points = own.shape[0]
+    steps = table.shape[0] // CHUNK
+
+    def fetch(i):
+        return pltpu.make_async_copy(
+            table_hbm.at[span_of(i, CHUNK)], table.at[span_of(i, CHUNK)], sems.at[i]
+        )
+
+    for i in range(steps):
+        fetch(i).start()
+    rows[:points, :] = own[...]
+    rows[points:, :] = cont[...]
+
+    def values_of(i, span):
+        fetch(i).wait()
+        values = dot_nt(rows[...], table[span, :]).astype(BF16)
+        return values[:points], values[points:]
+
+    def store(span, phi, psi):
+        phi_ref[:, span] = phi
+        psi_ref[:, span] = psi
+
+    def ends_at(n, k, span, value):
+        ends_ref[n * NC + k : n * NC + k + 1, span] = value
+
+    angular_density(
+        step, place[0], values_of, store, table, weight, degree_ref, part_ref, ends_at, pairs, work
+    )
+
+
+def other_kernel(
+    step, place, other, psi_ref, weight, degree_ref, own_ends, table,
+    part_ref, phi_ref, ends_ref,
+    pairs, work,
+):
+    x = place[0]
+
+    def values_of(i, span):
+        return dot_nt(other[...], table[span, :]).astype(BF16), psi_ref[:, span]
+
+    def store(span, phi, psi):
+        phi_ref[:, span] = phi
+
+    def ends_at(n, k, span, value):
+        ends_ref[pl.ds(n * NP + (1 - x) * NC + k, 1), span] = value
+
+    for n in range(4):
+        for k in range(NC):
+            ends_ref[pl.ds(n * NP + x * NC + k, 1), :] = own_ends[n * NC + k : n * NC + k + 1, :]
+    angular_density(
+        step, x, values_of, store, table, weight, degree_ref, part_ref, ends_at, pairs, work
+    )
+
+
 def finish_kernel(
-    step, pieces, place, own, other, cont, weight, far_weight, degree_ref, earlier, later, part, phi, *refs
+    step, pieces, place, own, other, cont, weight, far_weight, degree_ref, earlier, later,
+    part, other_part, phi, other_phi, table_hbm, *refs
 ):
-    table_hbm, far_hbm = refs[0], refs[1 : 1 + pieces]
-    send_ref, keep_ref, table, rows, pairs, far_phi, pot, product, work, total, sems = refs[1 + pieces :]
+    far_hbm = refs[:pieces]
+    send_ref, keep_ref, table, far_table, rows, pairs, phi_all, pot, product, work, total, sems = refs[pieces:]
     x = place[0]
     points = own.shape[0]
     half = points // 2
-    quad = table_hbm.shape[0]
-    size = quad // pieces
+    quad, channels = table.shape
     steps = quad // CHUNK
-    channels = table.shape[1]
 
     def fetch_far(n):
-        start = pl.multiple_of(quad + place[1 + n], size)
-        return pltpu.make_async_copy(far_hbm[n], table.at[pl.ds(start, size)], sems.at[n])
-
-    fetch_own = pltpu.make_async_copy(table_hbm, table.at[pl.ds(0, quad)], sems.at[pieces])
+        size = far_hbm[n].shape[0]
+        start = pl.multiple_of(place[1 + n], quad // 16)
+        return pltpu.make_async_copy(far_hbm[n], far_table.at[pl.ds(start, size)], sems.at[n])
+
+    def fetch_rows():
+        near = span_of(x, half)
+        yield pltpu.make_async_copy(own.at[near], rows.at[near], sems.at[pieces])
+        for k in range(NC):
+            at = span_of(2 * k + x, half)
+            to = pl.ds((NI + k) * half, half)
+            yield pltpu.make_async_copy(cont.at[at], rows.at[to], sems.at[pieces + 1 + k])
+
+    fetch_table = pltpu.make_async_copy(table_hbm, table, sems.at[pieces + 1 + NC])
+    for copy in fetch_rows():
+        copy.start()
+
     for n in range(pieces):
         fetch_far(n).start()
-    fetch_own.start()
-    rows[span_of(x, half), :] = own[span_of(x, half), :]
+    phi_all[span_of(x, half), :quad] = phi[...]
+    phi_all[span_of(1 - x, half), :quad] = other_phi[...]
+    fetch_table.start()
     rows[span_of(1 - x, half), :] = other[span_of(x, half), :]
-    for k in range(NC):
-        rows[(NI + k) * half : (NI + k + 1) * half, :] = cont[span_of(2 * k + x, half), :]
+    for copy in fetch_rows():
+        copy.wait()
     for n in range(pieces):
         fetch_far(n).wait()
 
     def angular(i, carry):
         span = span_of(i, CHUNK)
-        values = dot_nt(rows[...], table[span_of(i + steps, CHUNK), :]).astype(BF16)
+        values = dot_nt(rows[...], far_table[span, :]).astype(BF16)
         store_pairs(values, far_weight[:, span], half, pairs, span)
-        far_phi[:, span] = values[: NI * half]
+        phi_all[:, span_of(i + steps, CHUNK)] = values[: NI * half]
         return carry
 
     lax.fori_loop(0, steps, angular, 0)
@@ -266,10 +322,11 @@
         shrink_ahead = jnp.exp(-(degree + 1.0) * step)
         shrink_behind = jnp.exp(-degree * step)
         factor = 4.0 * step / (2.0 * degree + 1.0)
-        far = dot_nn(pairs[...], table[quad:, span])
-        density = part[:, span].astype(F32) + far.astype(BF16).astype(F32)
-        density = density.astype(BF16).astype(F32)
-        work[...] = density.reshape(NP, half, TILE)
+        far = dot_nn(pairs[...], far_table[:, span])
+        work[...] = far.reshape(NP, half, TILE)
+        for start, values in ((x * NC, part), (NC - x * NC, other_part)):
+            near = values[:, span].astype(F32).reshape(NC, half, TILE)
+            work[pl.ds(start, NC)] = work[pl.ds(start, NC)] + near
         ahead = earlier[:, span]
         behind = later[:, span] * shrink_behind
         for j in range(half):
@@ -282,48 +339,55 @@
         return carry
 
     lax.fori_loop(0, channels // TILE, radial, 0)
-    fetch_own.wait()
-
-    def weigh(i, table_at, phi_at, weight_at, span):
-        angle = dot_nt(pot[...], table[table_at, :])
-        for k in range(NC):
-            value = jnp.zeros((half, CHUNK), F32)
-            for o in range(NI):
-                value += phi_at[o * half : (o + 1) * half, span].astype(F32) * angle[
-                    (o * NC + k) * half : (o * NC + k + 1) * half
-                ]
-            product[k * half : (k + 1) * half, table_at] = (value * weight_at[:, span]).astype(BF16)
-
-    def near(i, carry):
-        weigh(i, span_of(i, CHUNK), phi, weight, span_of(i, CHUNK))
-        return carry
-
-    def distant(i, carry):
-        weigh(i, span_of(i + steps, CHUNK), far_phi, far_weight, span_of(i, CHUNK))
-        return carry
-
-    lax.fori_loop(0, steps, near, 0)
-    lax.fori_loop(0, steps, distant, 0)
+
+    def weigh(source, weight_at, first):
+        def chunk(i, carry):
+            span = span_of(i, CHUNK)
+            at = span_of(i + first, CHUNK)
+            angle = dot_nt(pot[...], source[span, :])
+            values = phi_all[:, at].astype(F32) * weight_at[:, span]
+            for k in range(NC):
+                value = jnp.zeros((half, CHUNK), F32)
+                for o in range(NI):
+                    row = (o * NC + k) * half
+                    value += values[o * half : (o + 1) * half] * angle[row : row + half]
+                product[k * half : (k + 1) * half, at] = value.astype(BF16)
+            return carry
+
+        lax.fori_loop(0, steps, chunk, 0)
+
+    weigh(far_table, far_weight, steps)
+    fetch_table.wait()
+    weigh(table, weight, 0)
     share = channels // 2
     third = share // 3
     for t in range(3):
         away = pl.ds(pl.multiple_of((1 - x) * share + t * third, third), third)
         home = pl.ds(pl.multiple_of(x * share + t * third, third), third)
         columns = slice(t * third, (t + 1) * third)
-        send_ref[:, columns] = (-dot_nn(product[...], table[:, away])).astype(BF16)
-        keep_ref[:, columns] = -dot_nn(product[...], table[:, home])
+        for out, place_at in ((send_ref, away), (keep_ref, home)):
+            value = dot_nn(product[:, :quad], table[:, place_at])
+            value += dot_nn(product[:, quad:], far_table[:, place_at])
+            out[:, columns] = (-value).astype(out.dtype)
+
+
+def slab_kernel(place, table, *refs):
+    sems = refs[-1]
+    copies = []
+    for n, out in enumerate(refs[:-1]):
+        start = pl.multiple_of(place[n], 80)
+        copies.append(pltpu.make_async_copy(table.at[pl.ds(start, out.shape[0])], out, sems.at[n]))
+    for copy in copies:
+        copy.start()
+    for copy in copies:
+        copy.wait()
 
 
 def place_kernel(place, keep, came, out_ref):
     x = place[0]
     half = keep.shape[0] // NC
-    mine = keep[...]
-    theirs = came[...].astype(F32)
-    lower = jnp.where(x == 0, mine, theirs)
-    upper = jnp.where(x == 0, theirs, mine)
-    for k in range(NC):
-        rows = slice(k * half, (k + 1) * half)
-        out_ref[:, k, :] = jnp.concatenate([lower[rows], upper[rows]], axis=0).T
+    out_ref[:, span_of(x, half), :] = keep[...].reshape(NC, half, -1)
+    out_ref[:, span_of(1 - x, half), :] = came[...].astype(F32).reshape(NC, half, -1)
 
 
 VMEM_SPEC = pl.BlockSpec(memory_space=pltpu.VMEM)
@@ -348,53 +412,77 @@
     def flip(value, bits):
         return lax.ppermute(value, "grid", [(n, n ^ bits) for n in everyone])
 
-    pieces = 8
-    size = quad // pieces
+    pieces = 14
+    size = quad // 16
     corner = 2 * (z % 2) + y
 
-    def offset(which, side):
-        return (which * 2 + side) * size
-
-    def slab(which):
-        return lax.dynamic_slice_in_dim(harmonic_table, offset(which, core), size)
+    def offset(which, side, n):
+        return ((which * 2 + side) * 2 + n) * size
+
+    def after(value, *others):
+        return lax.optimization_barrier((value, *others))[0]
+
+    def in_hbm(value):
+        return pltpu.with_memory_space_constraint(value, pltpu.HBM)
+
+    hbm = pl.BlockSpec(memory_space=pltpu.HBM)
+    slabs = pl.pallas_call(
+        slab_kernel,
+        out_shape=tuple(jax.ShapeDtypeStruct((n * size, channels), BF16) for n in (1, 1, 2)),
+        in_specs=[SMEM_SPEC, hbm],
+        out_specs=(VMEM_SPEC,) * 3,
+        scratch_shapes=[pltpu.SemaphoreType.DMA((3,))],
+        name="slabs",
+    )(
+        jnp.stack([offset(corner, core, 0), offset(corner, core, 1), offset(corner ^ 3, core, 0)]),
+        in_hbm(harmonic_table),
+    )
 
     own = orbitals[0]
-    other = over_x(own)
     weight = ang_weight[None, :]
-    far_weight = over_x(weight)
-    first = over_x(slab(corner))
-    last = over_x(slab(corner ^ 3))
-    by_y = flip(first, 2)
-    by_z = flip(first, 4)
-    received = [first, last, by_y, by_z]
-    which = [corner, corner ^ 3, corner ^ 1, corner ^ 2]
-    far = received + [flip(value, 1) for value in received]
-    offsets = [offset(w, core) for w in which] + [offset(w, 1 - core) for w in which]
-    place = jnp.stack([x] + offsets).astype(jnp.int32)
-
     degree = channel_degree(channel_lm)[None, :]
     cont = continuum.reshape(NC * points, channels)
-    part, phi, ends = pl.pallas_call(
+    place = jnp.stack([x]).astype(jnp.int32)
+    part_shape = jax.ShapeDtypeStruct((NC * half, channels), BF16)
+    phi_shape = jax.ShapeDtypeStruct((half, quad), BF16)
+
+    other = over_x(own)
+    first_a = over_x(slabs[0])
+    first_b = over_x(slabs[1])
+    last = over_x(slabs[2])
+    part, phi, psi, own_ends, table = pl.pallas_call(
         functools.partial(own_kernel, step),
         out_shape=(
-            jax.ShapeDtypeStruct((NP * half, channels), BF16),
-            jax.ShapeDtypeStruct((NI * half, quad), BF16),
-            jax.ShapeDtypeStruct((4 * NP, channels), F32),
+            part_shape,
+            phi_shape,
+            jax.ShapeDtypeStruct((NC * points, quad), BF16),
+            jax.ShapeDtypeStruct((4 * NC, channels), F32),
+            jax.ShapeDtypeStruct((quad, channels), BF16),
         ),
-        in_specs=[SMEM_SPEC] + [VMEM_SPEC] * 5 + [HBM_SPEC],
+        in_specs=[SMEM_SPEC] + [VMEM_SPEC] * 4 + [pl.BlockSpec(memory_space=pltpu.HBM)],
+        out_specs=(VMEM_SPEC,) * 5,
+        scratch_shapes=[
+            pltpu.VMEM(((1 + NC) * points, channels), BF16),
+            pltpu.VMEM((NC * points, quad), BF16),
+            pltpu.VMEM((NC * points, TILE), F32),
+            pltpu.SemaphoreType.DMA((quad // CHUNK,)),
+        ],
+        compiler_params=pltpu.CompilerParams(vmem_limit_bytes=16 << 20),
+        name="own_orbital",
+    )(place, own, cont, weight, degree, in_hbm(after(harmonic_table, slabs[0])))
+    other_part, other_phi, ends = pl.pallas_call(
+        functools.partial(other_kernel, step),
+        out_shape=(part_shape, phi_shape, jax.ShapeDtypeStruct((4 * NP, channels), F32)),
+        in_specs=[SMEM_SPEC] + [VMEM_SPEC] * 6,
         out_specs=(VMEM_SPEC,) * 3,
         scratch_shapes=[
-            pltpu.VMEM((quad, channels), BF16),
-            pltpu.VMEM(((NI + NC) * points, channels), BF16),
-            pltpu.VMEM((NP * points, quad), BF16),
-            pltpu.VMEM((NP * points, TILE), F32),
-            pltpu.SemaphoreType.DMA((quad // CHUNK,)),
+            pltpu.VMEM((NC * points, quad), BF16),
+            pltpu.VMEM((NC * points, TILE), F32),
         ],
-        compiler_params=pltpu.CompilerParams(vmem_limit_bytes=40 << 20),
-        name="own_half",
-    )(place, own, other, cont, weight, degree, harmonic_table)
-
-    ends = (ends + over_x(ends.astype(BF16)).astype(F32)).reshape(4, NP, channels)
+        compiler_params=pltpu.CompilerParams(vmem_limit_bytes=8 << 20),
+        name="other_orbital",
+    )(place, other, psi, weight, degree, own_ends, table)
+    ends = ends.reshape(4, NP, channels)
     ahead_rate = (degree + 1.0) * step
     behind_rate = degree * step
 
@@ -410,6 +498,7 @@
     u = g % 4
     both = jnp.concatenate([block_end, block_start], axis=0)
     message = both.astype(BF16)
+    first_a = after(first_a, message)
     earlier = jnp.zeros((NP, channels), F32)
     later = jnp.zeros((NP, channels), F32)
     row_end = ahead_by(points * (3 - u)) * block_end
@@ -423,7 +512,8 @@
         later += jnp.where(before, 0.0, behind_by(points * distance)) * came[NP:]
         row_end += ahead_by(points * (3 - v)) * came[:NP]
         row_start += behind_by(points * v) * came[NP:]
-    row_end, row_start = row_end.astype(BF16), row_start.astype(BF16)
+    row_end = after(row_end.astype(BF16), first_a, first_b)
+    row_start = after(row_start.astype(BF16), first_a, first_b)
     for shift in (1, 2, 3):
         message = jnp.where(z + shift < 4, row_end, row_start)
         came = lax.ppermute(message, "grid", [(n, (n + 4 * shift) % 16) for n in everyone])
@@ -433,9 +523,24 @@
         distance = jnp.abs(z - source) - 1
         earlier += jnp.where(before, ahead_by(points * (4 * distance + u)), 0.0) * came
         later += jnp.where(before, 0.0, behind_by(points * (4 * distance + 3 - u))) * came
-    upper = x == 1
-    earlier = jnp.where(upper, low_end + ahead_by(half) * earlier, earlier)
-    later = jnp.where(upper, later, high_start + behind_by(half) * later)
+    upper_earlier = low_end + ahead_by(half) * earlier
+    lower_later = high_start + behind_by(half) * later
+    theirs = jnp.concatenate(
+        [jnp.where(x == 0, upper_earlier, earlier), jnp.where(x == 0, later, lower_later)], axis=0
+    )
+    theirs = after(theirs.astype(BF16), last)
+    came = over_x(theirs).astype(F32)
+    earlier = jnp.where(x == 0, earlier, upper_earlier) + came[:NP]
+    later = jnp.where(x == 0, lower_later, later) + came[NP:]
+    first_b = after(first_b, row_end)
+    received = [first_a, first_b, last]
+    received += [flip(first_a, 2), flip(first_a, 4), flip(first_b, 2), flip(first_b, 4)]
+    which = [(corner, 0), (corner, 1), (corner ^ 3, 0)]
+    which += [(corner ^ 1, 0), (corner ^ 2, 0), (corner ^ 1, 1), (corner ^ 2, 1)]
+    far_weight = over_x(after(weight, received[3]))
+    far = received + [flip(value, 1) for value in received]
+    offsets = [offset(w, core, n) for w, n in which] + [offset(w, 1 - core, n) for w, n in which]
+    places = jnp.stack([x] + offsets).astype(jnp.int32)
 
     send, keep = pl.pallas_call(
         functools.partial(finish_kernel, step, pieces),
@@ -443,36 +548,35 @@
             jax.ShapeDtypeStruct((NC * half, channels // 2), BF16),
             jax.ShapeDtypeStruct((NC * half, channels // 2), F32),
         ),
-        in_specs=[SMEM_SPEC] + [VMEM_SPEC] * 10 + [HBM_SPEC] * (1 + pieces),
+        in_specs=[SMEM_SPEC, hbm, VMEM_SPEC, hbm] + [VMEM_SPEC] * 9 + [hbm] + [HBM_SPEC] * pieces,
         out_specs=(VMEM_SPEC,) * 2,
         scratch_shapes=[
-            pltpu.VMEM((2 * quad, channels), BF16),
+            pltpu.VMEM((quad, channels), BF16),
+            pltpu.VMEM((quad, channels), BF16),
             pltpu.VMEM(((NI + NC) * half, channels), BF16),
             pltpu.VMEM((NP * half, quad), BF16),
-            pltpu.VMEM((NI * half, quad), BF16),
+            pltpu.VMEM((NI * half, 2 * quad), BF16),
             pltpu.VMEM((NP * half, channels), BF16),
             pltpu.VMEM((NC * half, 2 * quad), BF16),
             pltpu.VMEM((NP, half, TILE), F32),
             pltpu.VMEM((NP, half, TILE), F32),
-            pltpu.SemaphoreType.DMA((pieces + 1,)),
+            pltpu.SemaphoreType.DMA((pieces + 2 + NC,)),
         ],
-        compiler_params=pltpu.CompilerParams(vmem_limit_bytes=48 << 20),
+        compiler_params=pltpu.CompilerParams(vmem_limit_bytes=26 << 20),
         name="finish",
-    )(place, own, other, cont, weight, far_weight, degree, earlier, later, part, phi, harmonic_table, *far)
+    )(
+        places, in_hbm(own), other, in_hbm(cont), weight, far_weight, degree, earlier, later,
+        part, other_part, phi, other_phi, in_hbm(harmonic_table), *far,
+    )
     came = over_x(send)
-    block = 128
-    return pl.pallas_call(
+    out = pl.pallas_call(
         place_kernel,
-        grid=(channels // 2 // block,),
-        out_shape=jax.ShapeDtypeStruct((channels // 2, NC, points), F32),
-        in_specs=[
-            SMEM_SPEC,
-            pl.BlockSpec((NC * half, block), lambda i: (0, i)),
-            pl.BlockSpec((NC * half, block), lambda i: (0, i)),
-        ],
-        out_specs=pl.BlockSpec((block, NC, points), lambda i: (i, 0, 0)),
+        out_shape=jax.ShapeDtypeStruct((NC, points, channels // 2), F32),
+        in_specs=[SMEM_SPEC, VMEM_SPEC, VMEM_SPEC],
+        out_specs=VMEM_SPEC,
         name="place",
     )(place, keep, came)
+    return jnp.transpose(out, (2, 0, 1))
 
 
 def solution(mesh):

time: 127 us -> 98.6 us (0.78)
  waiting for transfers between devices: 49.6 us -> 28.9 us
  local copies, waits for them, and re-layouts: 12.9 us -> 8.18 us
  starting transfers between devices: 22.7 us -> 20 us
    ppermute x3, waiting for transfers between devices: 15.2 us -> 0.13 us  [shards_by_table(): lax.ppermute(message, 'grid', [(n, (n + 4 * shift) % 16) for n in everyone])]
    ppermute x6 -> x7, waiting for transfers between devices: 28.7 us -> 18 us  [over_x(): return lax.ppermute(value, 'orb', across)]
    ppermute x9 -> x14, waiting for transfers between devices: 5.66 us -> 10.7 us  [flip(): return lax.ppermute(value, 'grid', [(n, n ^ bits) for n in everyone])]
    pallas_call x1 -> x0, local copies, waits for them, and re-layouts: 3.8 us -> none  [shards_by_table(): pl.pallas_call(place_kernel, grid=(channels // 2 // block,), out_shape=ja...]
    select_n x3 -> x1, other arithmetic: 2.8 us -> 0.07 us  [shards_by_table(): earlier += jnp.where(before, ahead_by(points * distance), 0.0) * came[:NP]]
    dynamic_slice x1 -> x0, local copies, waits for them, and re-layouts: 2.59 us -> none  [slab(): return lax.dynamic_slice_in_dim(harmonic_table, offset(which, core), size)]
    ppermute x6 -> x7, starting transfers between devices: 10.2 us -> 7.78 us  [over_x(): return lax.ppermute(value, 'orb', across)]
    another operation x1 -> x4, other arithmetic: 0.03 us -> 1.96 us
  transfers between devices with their start and end apart: 18 -> 24, of which waited for: 9 -> 9; matrix products, arithmetic and copies ran while one was open for 6% -> 4% of each run, Pallas kernels for 7% -> 15%
where the time goes in v2:
time: 98.6 us; the launch traced here: 98.1 us
  Pallas kernels  36.5 us (37%)
  waiting for transfers between devices  28.9 us (29%)
  starting transfers between devices  20 us (20%)
  local copies, waits for them, and re-layouts  8.18 us (8%)
  other arithmetic  4.23 us (4%)
    pallas_call x1, Pallas kernels, shards_by_table(): pl.pallas_call(functools.partial(finish_kernel, step, pieces), out_shape=...  19.5 us
    ppermute x7, waiting for transfers between devices, over_x(): return lax.ppermute(value, 'orb', across)  18 us
    ppermute x14, waiting for transfers between devices, flip(): return lax.ppermute(value, 'grid', [(n, n ^ bits) for n in everyone])  10.7 us
    unnamed x32, local copies, waits for them, and re-layouts  8.08 us
    ppermute x7, starting transfers between devices, over_x(): return lax.ppermute(value, 'orb', across)  7.78 us
    ppermute x14, starting transfers between devices, flip(): return lax.ppermute(value, 'grid', [(n, n ^ bits) for n in everyone])  7.54 us
    pallas_call x1, Pallas kernels, shards_by_table(): pl.pallas_call(functools.partial(own_kernel, step), out_shape=(part_shape...  6.6 us
    pallas_call x1, Pallas kernels, shards_by_table(): pl.pallas_call(functools.partial(other_kernel, step), out_shape=(part_sha...  5.03 us
  transfers between devices with their start and end apart: 24, of which 9 were waited for; matrix products, arithmetic and copies ran while one was open for 4% of the time, Pallas kernels for 15%

profile of v2, /device:TPU:0, one launch (start us, length us, event | category | flops | bytes accessed | tf_op | source)
XLA Modules:
  0.0 98.1 jit_solution(7184307644390383491)
XLA Ops:
  0.0 3.0 %collective-permute-start = (bf16[64,2304]{1,0:T(8,128)(2,1)}, bf16[64,2304]{1,0:T(8,128)(2,1)S(1)}, u32[]{:S(2)}, u32[]{:S(2)}) collective-permute-start(bf16[64,2304]{1,0:T(8,128)(2,1)} %bitcast.20), channel_id=1, source_target_pairs={{0,16},{16,0},{1,17},{17,1},{2,18},{18,2},{3,19},{19,3},{4,20},{20... | collective-permute-start | bytes 884744 | tf_op jit(solution)/shard_map/ppermute | solution.py:410
  3.0 0.6 pad_add_fusion.place
  3.6 3.1 %slabs.1 = (bf16[80,2304]{1,0:T(8,128)(2,1)}, bf16[80,2304]{1,0:T(8,128)(2,1)}, bf16[160,2304]{1,0:T(8,128)(2,1)}) custom-call(s32[3]{0:T(128)} %pad_add_fusion.place, bf16[1280,2304]{1,0:T(8,128)(2,1)} %table_hbm.2), custom_call_target="tpu_custom_call" | custom-call | tf_op jit(solution)/shard_map/slabs/pallas_call | solution.py:429
  6.7 0.1 collective-permute-start.1
  6.9 1.9 %collective-permute-start.7 = (bf16[80,2304]{1,0:T(8,128)(2,1)}, bf16[80,2304]{1,0:T(8,128)(2,1)}, u32[]{:S(2)}, u32[]{:S(2)}) collective-permute-start(bf16[80,2304]{1,0:T(8,128)(2,1)} %get-tuple-element.33), channel_id=1, source_target_pairs={{0,16},{16,0},{1,17},{17,1},{2,18},{18,2},{3,19},{19,3},{4,20},{20... | collective-permute-start | bytes 1105928 | tf_op jit(solution)/shard_map/ppermute | solution.py:410
  8.8 0.1 convert_reduce_fusion
  9.1 6.6 %own_orbital.1 = (bf16[128,2304]{1,0:T(8,128)(2,1)S(1)}, bf16[32,1280]{1,0:T(8,128)(2,1)S(1)}, bf16[256,1280]{1,0:T(8,128)(2,1)S(1)}, f32[16,2304]{1,0:T(8,128)S(1)}, bf16[1280,2304]{1,0:T(8,128)(2,1)S(1)}) custom-call(s32[1]{0:T(128)} %bitcast.place, bf16[64,2304]{1,0:T(8,128)(2,1)S(1)} %bitcast.22, bf16[256,2304]{1,0:T(8,128)(2,1)S(1)} %bitcast.19, ...), custom_call_target="tpu_custom_call" | custom-call | tf_op jit(solution)/shard_map/own_orbital/pallas_call | solution.py:453
  15.7 0.1 exponential_select_fusion.11
  15.8 0.0 collective-permute-done.other
  15.8 5.0 %other_orbital.1 = (bf16[128,2304]{1,0:T(8,128)(2,1)S(1)}, bf16[32,1280]{1,0:T(8,128)(2,1)S(1)}, f32[32,2304]{1,0:T(8,128)S(1)}) custom-call(s32[1]{0:T(128)} %bitcast.place, bf16[64,2304]{1,0:T(8,128)(2,1)S(1)} %collective-permute-done.other, bf16[256,1280]{1,0:T(8,128)(2,1)S(1)} %get-tuple-element.27.psi_ref, f32[1,1280]{1,0:T(1,128)S(1)} %broadcast_in_dim.24.weight, ...), custom_call_target="tpu_custom_call" | custom-call | tf_op jit(solution)/shard_map/other_orbital/pallas_call | solution.py:473
  20.8 0.8 copy-done.2
  21.7 0.2 collective-permute-start.6
  21.9 1.5 %collective-permute-start.5 = (bf16[16,2304]{1,0:T(8,128)(2,1)S(1)}, bf16[16,2304]{1,0:T(8,128)(2,1)S(1)}, u32[]{:S(2)}, u32[]{:S(2)}) collective-permute-start(bf16[16,2304]{1,0:T(8,128)(2,1)S(1)} %pad_maximum_fusion), channel_id=1, source_target_pairs={{0,2},{1,3},{2,0},{3,1},{4,6},{5,7},{6,4},{7,5},{8,10},{9,11},{10,... | collective-permute-start | bytes 221192 | tf_op jit(solution)/shard_map/ppermute | solution.py:413
  23.4 0.3 collective-permute-start.4
  23.7 0.0 collective-permute-done.1.refs_0_
  23.7 2.6 %collective-permute-done.6 = bf16[16,2304]{1,0:T(8,128)(2,1)S(1)} collective-permute-done((bf16[16,2304]{1,0:T(8,128)(2,1)S(1)}, bf16[16,2304]{1,0:T(8,128)(2,1)S(1)}, u32[]{:S(2)}, u32[]{:S(2)}) %collective-permute-start.6) | collective-permute-done | bytes 73760 | tf_op jit(solution)/shard_map/ppermute | solution.py:413
  26.3 1.6 %collective-permute-done.5 = bf16[16,2304]{1,0:T(8,128)(2,1)S(1)} collective-permute-done((bf16[16,2304]{1,0:T(8,128)(2,1)S(1)}, bf16[16,2304]{1,0:T(8,128)(2,1)S(1)}, u32[]{:S(2)}, u32[]{:S(2)}) %collective-permute-start.5) | collective-permute-done | bytes 73760 | tf_op jit(solution)/shard_map/ppermute | solution.py:413
  27.9 0.0 collective-permute-done.4
  28.0 0.1 add_convert_fusion.1
  28.0 0.0 collective-permute-done.7.refs_1_
  28.0 0.1 add_convert_fusion
  28.1 3.7 %collective-permute-start.10 = (bf16[8,2304]{1,0:T(8,128)(2,1)S(1)}, bf16[8,2304]{1,0:T(8,128)(2,1)S(1)}, u32[]{:S(2)}, u32[]{:S(2)}) collective-permute-start(bf16[8,2304]{1,0:T(8,128)(2,1)S(1)} %get-tuple-element.54), channel_id=1, source_target_pairs={{0,12},{1,13},{2,14},{3,15},{4,0},{5,1},{6,2},{7,3},{8,4},{9,5},{1... | collective-permute-start | bytes 110600 | tf_op jit(solution)/shard_map/ppermute | solution.py:519
  31.8 0.0 collective-permute-start.9
  31.8 1.0 %collective-permute-start.8 = (bf16[8,2304]{1,0:T(8,128)(2,1)S(1)}, bf16[8,2304]{1,0:T(8,128)(2,1)S(1)}, u32[]{:S(2)}, u32[]{:S(2)}) collective-permute-start(bf16[8,2304]{1,0:T(8,128)(2,1)S(1)} %get-tuple-element.53), channel_id=1, source_target_pairs={{0,4},{1,5},{2,6},{3,7},{4,8},{5,9},{6,10},{7,11},{8,12},{9,13},{1... | collective-permute-start | bytes 110600 | tf_op jit(solution)/shard_map/ppermute | solution.py:519
  32.8 0.5 collective-permute-start.11
  33.3 0.9 collective-permute-start.2
  34.2 0.0 collective-permute-done.10
  34.2 2.5 %collective-permute-start.13 = (bf16[80,2304]{1,0:T(8,128)(2,1)S(1)}, bf16[80,2304]{1,0:T(8,128)(2,1)S(1)}, u32[]{:S(2)}, u32[]{:S(2)}) collective-permute-start(bf16[80,2304]{1,0:T(8,128)(2,1)S(1)} %collective-permute-done.1.refs_0_), channel_id=1, source_target_pairs={{0,4},{1,5},{2,6},{3,7},{4,0},{5,1},{6,2},{7,3},{8,12},{9,13},{10,... | collective-permute-start | bytes 1105928 | tf_op jit(solution)/shard_map/ppermute | solution.py:413
  36.6 0.1 collective-permute-done.9
  36.8 1.1 %collective-permute-start.14 = (bf16[80,2304]{1,0:T(8,128)(2,1)}, bf16[80,2304]{1,0:T(8,128)(2,1)S(1)}, u32[]{:S(2)}, u32[]{:S(2)}) collective-permute-start(bf16[80,2304]{1,0:T(8,128)(2,1)} %collective-permute-done.7.refs_1_), channel_id=1, source_target_pairs={{0,2},{1,3},{2,0},{3,1},{4,6},{5,7},{6,4},{7,5},{8,10},{9,11},{10,... | collective-permute-start | bytes 1105928 | tf_op jit(solution)/shard_map/ppermute | solution.py:413
  37.8 0.1 collective-permute-start.15
  37.9 0.7 select_convert_fusion
  38.6 0.7 select_convert_fusion.1
  39.3 5.6 %collective-permute-done.2.refs_3_ = bf16[80,2304]{1,0:T(8,128)(2,1)S(1)} collective-permute-done((bf16[80,2304]{1,0:T(8,128)(2,1)S(1)}, bf16[80,2304]{1,0:T(8,128)(2,1)S(1)}, u32[]{:S(2)}, u32[]{:S(2)}) %collective-permute-start.2) | collective-permute-done | bytes 368672 | tf_op jit(solution)/shard_map/ppermute | solution.py:413
  44.8 0.0 collective-permute-start.16
  44.8 5.8 %collective-permute-done.11.refs_2_ = bf16[160,2304]{1,0:T(8,128)(2,1)S(1)} collective-permute-done((bf16[160,2304]{1,0:T(8,128)(2,1)}, bf16[160,2304]{1,0:T(8,128)(2,1)S(1)}, u32[]{:S(2)}, u32[]{:S(2)}) %collective-permute-start.11) | collective-permute-done | bytes 737312 | tf_op jit(solution)/shard_map/ppermute | solution.py:410
  50.6 0.0 collective-permute-done.13.refs_4_
  50.6 0.0 copy-start.5
  50.6 0.6 collective-permute-start.12
  51.2 0.2 copy-done.5
  51.4 0.0 collective-permute-done.14.refs_5_
  51.4 0.7 copy-done.7
  52.1 0.5 collective-permute-start.18
  52.6 2.9 %collective-permute-done.12 = bf16[16,2304]{1,0:T(8,128)(2,1)} collective-permute-done((bf16[16,2304]{1,0:T(8,128)(2,1)S(1)}, bf16[16,2304]{1,0:T(8,128)(2,1)}, u32[]{:S(2)}, u32[]{:S(2)}) %collective-permute-start.12) | collective-permute-done | bytes 73760 | tf_op jit(solution)/shard_map/ppermute | solution.py:410
  55.5 0.5 collective-permute-start.3
  56.0 0.1 stack.70.place
  56.1 0.9 convert_element_type.112
  57.0 0.1 collective-permute-start.19
  57.1 0.5 collective-permute-start.20
  57.6 0.1 collective-permute-start.21
  57.7 1.4 %collective-permute-done.3.far_weight = f32[1,1280]{1,0:T(1,128)S(1)} collective-permute-done((f32[1,1280]{1,0:T(1,128)S(1)}, f32[1,1280]{1,0:T(1,128)S(1)}, u32[]{:S(2)}, u32[]{:S(2)}) %collective-permute-start.3) | collective-permute-done | bytes 5152 | tf_op jit(solution)/shard_map/ppermute | solution.py:410
  59.1 1.0 slice_add_fusion
  60.1 0.9 collective-permute-done.22.refs_13_
  61.0 1.1 %copy-done.3 = bf16[128,2304]{1,0:T(8,128)(2,1)S(1)} copy-done((bf16[128,2304]{1,0:T(8,128)(2,1)S(1)}, bf16[128,2304]{1,0:T(8,128)(2,1)}, u32[]{:S(2)}) %copy-start.3) | copy-done | bytes 589848
  62.1 1.0 %copy-done.6 = bf16[80,2304]{1,0:T(8,128)(2,1)S(1)} copy-done((bf16[80,2304]{1,0:T(8,128)(2,1)S(1)}, bf16[80,2304]{1,0:T(8,128)(2,1)}, u32[]{:S(2)}) %copy-start.6) | copy-done | bytes 368664
  63.0 1.0 %copy-done.8 = bf16[80,2304]{1,0:T(8,128)(2,1)S(1)} copy-done((bf16[80,2304]{1,0:T(8,128)(2,1)S(1)}, bf16[80,2304]{1,0:T(8,128)(2,1)}, u32[]{:S(2)}) %copy-start.8) | copy-done | bytes 368664
  64.0 0.9 copy-done.10
  64.9 0.9 copy-done.12
  65.8 19.5 %finish.1 = (bf16[128,1152]{1,0:T(8,128)(2,1)S(1)}, f32[128,1152]{1,0:T(8,128)S(1)}) custom-call(s32[15]{0:T(128)S(1)} %stack.70.place, bf16[64,2304]{1,0:T(8,128)(2,1)} %bitcast.21, bf16[64,2304]{1,0:T(8,128)(2,1)S(1)} %collective-permute-done.other, bf16[256,2304]{1,0:T(8,128)(2,1)} %bitcast.18, f32[1,1280]{1,0:T(1,128)S(1)} %broadcast_in_dim.24.weight, ...), custom_call_target="tpu_custom_call" | custom-call | tf_op jit(solution)/shard_map/finish/pallas_call | solution.py:545
  85.3 0.8 copy-done.4
  86.1 1.1 %collective-permute-start.23 = (bf16[128,1152]{1,0:T(8,128)(2,1)S(1)}, bf16[128,1152]{1,0:T(8,128)(2,1)S(1)}, u32[]{:S(2)}, u32[]{:S(2)}) collective-permute-start(bf16[128,1152]{1,0:T(8,128)(2,1)S(1)} %get-tuple-element.44), channel_id=1, source_target_pairs={{0,16},{16,0},{1,17},{17,1},{2,18},{18,2},{3,19},{19,3},{4,20},{20... | collective-permute-start | bytes 884744 | tf_op jit(solution)/shard_map/ppermute | solution.py:410
  87.2 8.0 %collective-permute-done.23.came = bf16[128,1152]{1,0:T(8,128)(2,1)S(1)} collective-permute-done((bf16[128,1152]{1,0:T(8,128)(2,1)S(1)}, bf16[128,1152]{1,0:T(8,128)(2,1)S(1)}, u32[]{:S(2)}, u32[]{:S(2)}) %collective-permute-start.23) | collective-permute-done | bytes 294944 | tf_op jit(solution)/shard_map/ppermute | solution.py:410
  95.1 0.7 copy-done.13
  95.9 2.2 %place.1 = f32[4,64,1152]{2,1,0:T(8,128)} custom-call(s32[1]{0:T(128)} %bitcast.place, f32[128,1152]{1,0:T(8,128)} %copy-done.4, bf16[128,1152]{1,0:T(8,128)(2,1)} %copy-done.13), custom_call_target="tpu_custom_call" | custom-call | tf_op jit(solution)/shard_map/place/pallas_call | solution.py:572
  (42 shorter events, 0.2 us)
Async XLA Ops:
  0.0 9.1 %copy-start.1 = (bf16[1,64,2304]{2,1,0:T(8,128)(2,1)S(1)}, bf16[1,64,2304]{2,1,0:T(8,128)(2,1)}, u32[]{:S(2)}) copy-start(bf16[1,64,2304]{2,1,0:T(8,128)(2,1)} %param.5) | copy-start | bytes 884740
  0.0 8.8 %copy-start.15 = (f32[1280]{0:T(1024)S(1)}, f32[1280]{0:T(1024)}, u32[]{:S(2)}) copy-start(f32[1280]{0:T(1024)} %param.8) | copy-start | bytes 15364
  0.0 8.8 %copy-start.14 = (s32[2304]{0:T(1024)S(1)}, s32[2304]{0:T(1024)}, u32[]{:S(2)}) copy-start(s32[2304]{0:T(1024)} %param.9) | copy-start | bytes 27652
  0.0 9.1 %copy-start = (bf16[4,64,2304]{2,1,0:T(8,128)(2,1)S(1)}, bf16[4,64,2304]{2,1,0:T(8,128)(2,1)}, u32[]{:S(2)}) copy-start(bf16[4,64,2304]{2,1,0:T(8,128)(2,1)} %param.6) | copy-start | bytes 3538948
  0.0 15.8 %collective-permute-start = (bf16[64,2304]{1,0:T(8,128)(2,1)}, bf16[64,2304]{1,0:T(8,128)(2,1)S(1)}, u32[]{:S(2)}, u32[]{:S(2)}) collective-permute-start(bf16[64,2304]{1,0:T(8,128)(2,1)} %bitcast.20), channel_id=1, source_target_pairs={{0,16},{16,0},{1,17},{17,1},{2,18},{18,2},{3,19},{19,3},{4,20},{20... | collective-permute-start | bytes 884744 | tf_op jit(solution)/shard_map/ppermute | solution.py:410
  6.7 16.9 %collective-permute-start.1 = (bf16[80,2304]{1,0:T(8,128)(2,1)}, bf16[80,2304]{1,0:T(8,128)(2,1)S(1)}, u32[]{:S(2)}, u32[]{:S(2)}) collective-permute-start(bf16[80,2304]{1,0:T(8,128)(2,1)} %get-tuple-element.25), channel_id=1, source_target_pairs={{0,16},{16,0},{1,17},{17,1},{2,18},{18,2},{3,19},{19,3},{4,20},{20... | collective-permute-start | bytes 1105928 | tf_op jit(solution)/shard_map/ppermute | solution.py:410
  6.9 21.1 %collective-permute-start.7 = (bf16[80,2304]{1,0:T(8,128)(2,1)}, bf16[80,2304]{1,0:T(8,128)(2,1)}, u32[]{:S(2)}, u32[]{:S(2)}) collective-permute-start(bf16[80,2304]{1,0:T(8,128)(2,1)} %get-tuple-element.33), channel_id=1, source_target_pairs={{0,16},{16,0},{1,17},{17,1},{2,18},{18,2},{3,19},{19,3},{4,20},{20... | collective-permute-start | bytes 1105928 | tf_op jit(solution)/shard_map/ppermute | solution.py:410
  15.7 5.1 %copy-start.9 = (bf16[32,1280]{1,0:T(8,128)(2,1)}, bf16[32,1280]{1,0:T(8,128)(2,1)S(1)}, u32[]{:S(2)}) copy-start(bf16[32,1280]{1,0:T(8,128)(2,1)S(1)} %get-tuple-element.40.phi) | copy-start | bytes 245764
  20.8 0.8 copy-start.2
  21.7 11.1 %copy-start.11 = (bf16[32,1280]{1,0:T(8,128)(2,1)}, bf16[32,1280]{1,0:T(8,128)(2,1)S(1)}, u32[]{:S(2)}) copy-start(bf16[32,1280]{1,0:T(8,128)(2,1)S(1)} %get-tuple-element.41.other_phi) | copy-start | bytes 245764
  21.7 4.6 %collective-permute-start.6 = (bf16[16,2304]{1,0:T(8,128)(2,1)S(1)}, bf16[16,2304]{1,0:T(8,128)(2,1)S(1)}, u32[]{:S(2)}, u32[]{:S(2)}) collective-permute-start(bf16[16,2304]{1,0:T(8,128)(2,1)S(1)} %pad_maximum_fusion), channel_id=1, source_target_pairs={{0,3},{1,2},{2,1},{3,0},{4,7},{5,6},{6,5},{7,4},{8,11},{9,10},{10,... | collective-permute-start | bytes 221192 | tf_op jit(solution)/shard_map/ppermute | solution.py:413
  21.9 6.0 %collective-permute-start.5 = (bf16[16,2304]{1,0:T(8,128)(2,1)S(1)}, bf16[16,2304]{1,0:T(8,128)(2,1)S(1)}, u32[]{:S(2)}, u32[]{:S(2)}) collective-permute-start(bf16[16,2304]{1,0:T(8,128)(2,1)S(1)} %pad_maximum_fusion), channel_id=1, source_target_pairs={{0,2},{1,3},{2,0},{3,1},{4,6},{5,7},{6,4},{7,5},{8,10},{9,11},{10,... | collective-permute-start | bytes 221192 | tf_op jit(solution)/shard_map/ppermute | solution.py:413
  23.4 4.6 %collective-permute-start.4 = (bf16[16,2304]{1,0:T(8,128)(2,1)S(1)}, bf16[16,2304]{1,0:T(8,128)(2,1)S(1)}, u32[]{:S(2)}, u32[]{:S(2)}) collective-permute-start(bf16[16,2304]{1,0:T(8,128)(2,1)S(1)} %pad_maximum_fusion), channel_id=1, source_target_pairs={{0,1},{1,0},{2,3},{3,2},{4,5},{5,4},{6,7},{7,6},{8,9},{9,8},{10,11... | collective-permute-start | bytes 221192 | tf_op jit(solution)/shard_map/ppermute | solution.py:413
  28.1 6.1 %collective-permute-start.10 = (bf16[8,2304]{1,0:T(8,128)(2,1)S(1)}, bf16[8,2304]{1,0:T(8,128)(2,1)S(1)}, u32[]{:S(2)}, u32[]{:S(2)}) collective-permute-start(bf16[8,2304]{1,0:T(8,128)(2,1)S(1)} %get-tuple-element.54), channel_id=1, source_target_pairs={{0,12},{1,13},{2,14},{3,15},{4,0},{5,1},{6,2},{7,3},{8,4},{9,5},{1... | collective-permute-start | bytes 110600 | tf_op jit(solution)/shard_map/ppermute | solution.py:519
  31.8 5.0 %collective-permute-start.9 = (bf16[8,2304]{1,0:T(8,128)(2,1)S(1)}, bf16[8,2304]{1,0:T(8,128)(2,1)S(1)}, u32[]{:S(2)}, u32[]{:S(2)}) collective-permute-start(bf16[8,2304]{1,0:T(8,128)(2,1)S(1)} %get-tuple-element.55), channel_id=1, source_target_pairs={{0,8},{1,9},{2,10},{3,11},{4,12},{5,13},{6,14},{7,15},{8,0},{9,1},... | collective-permute-start | bytes 110600 | tf_op jit(solution)/shard_map/ppermute | solution.py:519
  31.8 6.1 %collective-permute-start.8 = (bf16[8,2304]{1,0:T(8,128)(2,1)S(1)}, bf16[8,2304]{1,0:T(8,128)(2,1)S(1)}, u32[]{:S(2)}, u32[]{:S(2)}) collective-permute-start(bf16[8,2304]{1,0:T(8,128)(2,1)S(1)} %get-tuple-element.53), channel_id=1, source_target_pairs={{0,4},{1,5},{2,6},{3,7},{4,8},{5,9},{6,10},{7,11},{8,12},{9,13},{1... | collective-permute-start | bytes 110600 | tf_op jit(solution)/shard_map/ppermute | solution.py:519
  32.8 17.8 %collective-permute-start.11 = (bf16[160,2304]{1,0:T(8,128)(2,1)}, bf16[160,2304]{1,0:T(8,128)(2,1)S(1)}, u32[]{:S(2)}, u32[]{:S(2)}) collective-permute-start(bf16[160,2304]{1,0:T(8,128)(2,1)} %get-tuple-element.36), channel_id=1, source_target_pairs={{0,16},{16,0},{1,17},{17,1},{2,18},{18,2},{3,19},{19,3},{4,20},{20... | collective-permute-start | bytes 2211848 | tf_op jit(solution)/shard_map/ppermute | solution.py:410
  33.3 11.5 %collective-permute-start.2 = (bf16[80,2304]{1,0:T(8,128)(2,1)S(1)}, bf16[80,2304]{1,0:T(8,128)(2,1)S(1)}, u32[]{:S(2)}, u32[]{:S(2)}) collective-permute-start(bf16[80,2304]{1,0:T(8,128)(2,1)S(1)} %collective-permute-done.1.refs_0_), channel_id=1, source_target_pairs={{0,2},{1,3},{2,0},{3,1},{4,6},{5,7},{6,4},{7,5},{8,10},{9,11},{10,... | collective-permute-start | bytes 1105928 | tf_op jit(solution)/shard_map/ppermute | solution.py:413
  34.2 16.4 %collective-permute-start.13 = (bf16[80,2304]{1,0:T(8,128)(2,1)S(1)}, bf16[80,2304]{1,0:T(8,128)(2,1)S(1)}, u32[]{:S(2)}, u32[]{:S(2)}) collective-permute-start(bf16[80,2304]{1,0:T(8,128)(2,1)S(1)} %collective-permute-done.1.refs_0_), channel_id=1, source_target_pairs={{0,4},{1,5},{2,6},{3,7},{4,0},{5,1},{6,2},{7,3},{8,12},{9,13},{10,... | collective-permute-start | bytes 1105928 | tf_op jit(solution)/shard_map/ppermute | solution.py:413
  36.8 14.6 %collective-permute-start.14 = (bf16[80,2304]{1,0:T(8,128)(2,1)}, bf16[80,2304]{1,0:T(8,128)(2,1)S(1)}, u32[]{:S(2)}, u32[]{:S(2)}) collective-permute-start(bf16[80,2304]{1,0:T(8,128)(2,1)} %collective-permute-done.7.refs_1_), channel_id=1, source_target_pairs={{0,2},{1,3},{2,0},{3,1},{4,6},{5,7},{6,4},{7,5},{8,10},{9,11},{10,... | collective-permute-start | bytes 1105928 | tf_op jit(solution)/shard_map/ppermute | solution.py:413
  37.8 19.2 %collective-permute-start.15 = (bf16[80,2304]{1,0:T(8,128)(2,1)}, bf16[80,2304]{1,0:T(8,128)(2,1)}, u32[]{:S(2)}, u32[]{:S(2)}) collective-permute-start(bf16[80,2304]{1,0:T(8,128)(2,1)} %collective-permute-done.7.refs_1_), channel_id=1, source_target_pairs={{0,4},{1,5},{2,6},{3,7},{4,0},{5,1},{6,2},{7,3},{8,12},{9,13},{10,... | collective-permute-start | bytes 1105928 | tf_op jit(solution)/shard_map/ppermute | solution.py:413
  44.8 12.2 %collective-permute-start.16 = (bf16[80,2304]{1,0:T(8,128)(2,1)S(1)}, bf16[80,2304]{1,0:T(8,128)(2,1)}, u32[]{:S(2)}, u32[]{:S(2)}) collective-permute-start(bf16[80,2304]{1,0:T(8,128)(2,1)S(1)} %collective-permute-done.1.refs_0_), channel_id=1, source_target_pairs={{0,1},{1,0},{2,3},{3,2},{4,5},{5,4},{6,7},{7,6},{8,9},{9,8},{10,11... | collective-permute-start | bytes 1105928 | tf_op jit(solution)/shard_map/ppermute | solution.py:413
  50.6 7.0 %collective-permute-start.17 = (bf16[80,2304]{1,0:T(8,128)(2,1)}, bf16[80,2304]{1,0:T(8,128)(2,1)}, u32[]{:S(2)}, u32[]{:S(2)}) collective-permute-start(bf16[80,2304]{1,0:T(8,128)(2,1)} %collective-permute-done.7.refs_1_), channel_id=1, source_target_pairs={{0,1},{1,0},{2,3},{3,2},{4,5},{5,4},{6,7},{7,6},{8,9},{9,8},{10,11... | collective-permute-start | bytes 1105928 | tf_op jit(solution)/shard_map/ppermute | solution.py:413
  50.6 0.7 copy-start.5
  50.6 4.8 %collective-permute-start.12 = (bf16[16,2304]{1,0:T(8,128)(2,1)S(1)}, bf16[16,2304]{1,0:T(8,128)(2,1)}, u32[]{:S(2)}, u32[]{:S(2)}) collective-permute-start(bf16[16,2304]{1,0:T(8,128)(2,1)S(1)} %pad_maximum_fusion.1), channel_id=1, source_target_pairs={{0,16},{16,0},{1,17},{17,1},{2,18},{18,2},{3,19},{19,3},{4,20},{20... | collective-permute-start | bytes 221192 | tf_op jit(solution)/shard_map/ppermute | solution.py:410
  51.4 0.8 copy-start.7
  52.1 8.9 %collective-permute-start.18 = (bf16[160,2304]{1,0:T(8,128)(2,1)S(1)}, bf16[160,2304]{1,0:T(8,128)(2,1)S(1)}, u32[]{:S(2)}, u32[]{:S(2)}) collective-permute-start(bf16[160,2304]{1,0:T(8,128)(2,1)S(1)} %collective-permute-done.11.refs_2_), channel_id=1, source_target_pairs={{0,1},{1,0},{2,3},{3,2},{4,5},{5,4},{6,7},{7,6},{8,9},{9,8},{10,11... | collective-permute-start | bytes 2211848 | tf_op jit(solution)/shard_map/ppermute | solution.py:413
  55.5 3.6 %collective-permute-start.3 = (f32[1,1280]{1,0:T(1,128)S(1)}, f32[1,1280]{1,0:T(1,128)S(1)}, u32[]{:S(2)}, u32[]{:S(2)}) collective-permute-start(f32[1,1280]{1,0:T(1,128)S(1)} %broadcast_in_dim.24.weight), channel_id=1, source_target_pairs={{0,16},{16,0},{1,17},{17,1},{2,18},{18,2},{3,19},{19,3},{4,20},{20... | collective-permute-start | bytes 15368 | tf_op jit(solution)/shard_map/ppermute | solution.py:410
  57.0 3.1 %collective-permute-start.19 = (bf16[80,2304]{1,0:T(8,128)(2,1)S(1)}, bf16[80,2304]{1,0:T(8,128)(2,1)S(1)}, u32[]{:S(2)}, u32[]{:S(2)}) collective-permute-start(bf16[80,2304]{1,0:T(8,128)(2,1)S(1)} %collective-permute-done.2.refs_3_), channel_id=1, source_target_pairs={{0,1},{1,0},{2,3},{3,2},{4,5},{5,4},{6,7},{7,6},{8,9},{9,8},{10,11... | collective-permute-start | bytes 1105928 | tf_op jit(solution)/shard_map/ppermute | solution.py:413
  57.1 3.0 %collective-permute-start.20 = (bf16[80,2304]{1,0:T(8,128)(2,1)}, bf16[80,2304]{1,0:T(8,128)(2,1)S(1)}, u32[]{:S(2)}, u32[]{:S(2)}) collective-permute-start(bf16[80,2304]{1,0:T(8,128)(2,1)} %copy-done.5), channel_id=1, source_target_pairs={{0,1},{1,0},{2,3},{3,2},{4,5},{5,4},{6,7},{7,6},{8,9},{9,8},{10,11... | collective-permute-start | bytes 1105928 | tf_op jit(solution)/shard_map/ppermute | solution.py:413
  57.6 2.5 %collective-permute-start.21 = (bf16[80,2304]{1,0:T(8,128)(2,1)}, bf16[80,2304]{1,0:T(8,128)(2,1)S(1)}, u32[]{:S(2)}, u32[]{:S(2)}) collective-permute-start(bf16[80,2304]{1,0:T(8,128)(2,1)} %copy-done.7), channel_id=1, source_target_pairs={{0,1},{1,0},{2,3},{3,2},{4,5},{5,4},{6,7},{7,6},{8,9},{9,8},{10,11... | collective-permute-start | bytes 1105928 | tf_op jit(solution)/shard_map/ppermute | solution.py:413
  59.1 1.9 %collective-permute-start.22 = (bf16[80,2304]{1,0:T(8,128)(2,1)}, bf16[80,2304]{1,0:T(8,128)(2,1)S(1)}, u32[]{:S(2)}, u32[]{:S(2)}) collective-permute-start(bf16[80,2304]{1,0:T(8,128)(2,1)} %collective-permute-done.15.refs_6_), channel_id=1, source_target_pairs={{0,1},{1,0},{2,3},{3,2},{4,5},{5,4},{6,7},{7,6},{8,9},{9,8},{10,11... | collective-permute-start | bytes 1105928 | tf_op jit(solution)/shard_map/ppermute | solution.py:413
  61.0 1.1 %copy-start.3 = (bf16[128,2304]{1,0:T(8,128)(2,1)S(1)}, bf16[128,2304]{1,0:T(8,128)(2,1)}, u32[]{:S(2)}) copy-start(bf16[128,2304]{1,0:T(8,128)(2,1)} %copy-done.2) | copy-start | bytes 1769476
  62.1 1.0 %copy-start.6 = (bf16[80,2304]{1,0:T(8,128)(2,1)S(1)}, bf16[80,2304]{1,0:T(8,128)(2,1)}, u32[]{:S(2)}) copy-start(bf16[80,2304]{1,0:T(8,128)(2,1)} %copy-done.5) | copy-start | bytes 1105924
  63.0 1.0 %copy-start.8 = (bf16[80,2304]{1,0:T(8,128)(2,1)S(1)}, bf16[80,2304]{1,0:T(8,128)(2,1)}, u32[]{:S(2)}) copy-start(bf16[80,2304]{1,0:T(8,128)(2,1)} %copy-done.7) | copy-start | bytes 1105924
  64.0 0.9 copy-start.10
  64.9 0.9 copy-start.12
  85.3 0.8 copy-start.4
  86.1 9.0 %collective-permute-start.23 = (bf16[128,1152]{1,0:T(8,128)(2,1)S(1)}, bf16[128,1152]{1,0:T(8,128)(2,1)S(1)}, u32[]{:S(2)}, u32[]{:S(2)}) collective-permute-start(bf16[128,1152]{1,0:T(8,128)(2,1)S(1)} %get-tuple-element.44), channel_id=1, source_target_pairs={{0,16},{16,0},{1,17},{17,1},{2,18},{18,2},{3,19},{19,3},{4,20},{20... | collective-permute-start | bytes 884744 | tf_op jit(solution)/shard_map/ppermute | solution.py:410
  95.1 0.7 copy-start.13

commit v3 on v2

--- a/solution.py
+++ b/solution.py
@@ -143,6 +143,7 @@
 NI = 2
 NP = NI * NC
 CHUNK = 256
+WIDE = 640
 TILE = 768
 F32 = jnp.float32
 BF16 = jnp.bfloat16
@@ -210,8 +211,8 @@
 
 def own_kernel(
     step, place, own, cont, weight, degree_ref, table_hbm,
-    part_ref, phi_ref, psi_ref, ends_ref, table,
-    rows, pairs, work, sems,
+    part_any, phi_any, psi_ref, ends_ref, table,
+    part_ref, phi_ref, rows, pairs, work, sems,
 ):
     points = own.shape[0]
     steps = table.shape[0] // CHUNK
@@ -241,14 +242,25 @@
     angular_density(
         step, place[0], values_of, store, table, weight, degree_ref, part_ref, ends_at, pairs, work
     )
+    copies = [
+        pltpu.make_async_copy(part_ref, part_any, sems.at[0]),
+        pltpu.make_async_copy(phi_ref, phi_any, sems.at[1]),
+    ]
+    for copy in copies:
+        copy.start()
+    for copy in copies:
+        copy.wait()
 
 
 def other_kernel(
     step, place, other, psi_ref, weight, degree_ref, own_ends, table,
-    part_ref, phi_ref, ends_ref,
-    pairs, work,
+    part_any, phi_any, ends_ref, slab_any,
+    part_ref, phi_ref, pairs, work, sems,
 ):
     x = place[0]
+    slab = pl.ds(pl.multiple_of(place[1], slab_any.shape[0]), slab_any.shape[0])
+    copies = [pltpu.make_async_copy(table.at[slab], slab_any, sems.at[0])]
+    copies[0].start()
 
     def values_of(i, span):
         return dot_nt(other[...], table[span, :]).astype(BF16), psi_ref[:, span]
@@ -265,19 +277,25 @@
     angular_density(
         step, x, values_of, store, table, weight, degree_ref, part_ref, ends_at, pairs, work
     )
+    copies.append(pltpu.make_async_copy(part_ref, part_any, sems.at[1]))
+    copies.append(pltpu.make_async_copy(phi_ref, phi_any, sems.at[2]))
+    for copy in copies[1:]:
+        copy.start()
+    for copy in copies:
+        copy.wait()
 
 
 def finish_kernel(
     step, pieces, place, own, other, cont, weight, far_weight, degree_ref, earlier, later,
-    part, other_part, phi, other_phi, table_hbm, *refs
+    part_any, other_part_any, phi_any, other_phi_any, table_hbm, *refs
 ):
     far_hbm = refs[:pieces]
-    send_ref, keep_ref, table, far_table, rows, pairs, phi_all, pot, product, work, total, sems = refs[pieces:]
+    send_any, keep_any, send_ref, keep_ref, part, table, far_table, rows, pairs, sorted_pairs, phi_all, pot, product, work, total, sems = refs[pieces:]
     x = place[0]
     points = own.shape[0]
     half = points // 2
     quad, channels = table.shape
-    steps = quad // CHUNK
+    steps = quad // WIDE
 
     def fetch_far(n):
         size = far_hbm[n].shape[0]
@@ -298,8 +316,14 @@
 
     for n in range(pieces):
         fetch_far(n).start()
-    phi_all[span_of(x, half), :quad] = phi[...]
-    phi_all[span_of(1 - x, half), :quad] = other_phi[...]
+    near = [
+        pltpu.make_async_copy(phi_any, phi_all.at[span_of(x, half), pl.ds(0, quad)], sems.at[pieces + 2 + NC]),
+        pltpu.make_async_copy(other_phi_any, phi_all.at[span_of(1 - x, half), pl.ds(0, quad)], sems.at[pieces + 3 + NC]),
+        pltpu.make_async_copy(part_any, part.at[span_of(x, NC * half)], sems.at[pieces + 4 + NC]),
+        pltpu.make_async_copy(other_part_any, part.at[span_of(1 - x, NC * half)], sems.at[pieces + 5 + NC]),
+    ]
+    for copy in near:
+        copy.start()
     fetch_table.start()
     rows[span_of(1 - x, half), :] = other[span_of(x, half), :]
     for copy in fetch_rows():
@@ -307,14 +331,22 @@
     for n in range(pieces):
         fetch_far(n).wait()
 
+    shape = (NP * half, NP * half)
+    row, column = (lax.broadcasted_iota(jnp.int32, shape, n) for n in range(2))
+    by_point = ((row & (NP - 1)) * half + (row >> 3) == column).astype(F32).astype(BF16)
+    by_pair = ((column & (NP - 1)) * half + (column >> 3) == row).astype(F32).astype(BF16)
+
     def angular(i, carry):
-        span = span_of(i, CHUNK)
+        span = span_of(i, WIDE)
         values = dot_nt(rows[...], far_table[span, :]).astype(BF16)
         store_pairs(values, far_weight[:, span], half, pairs, span)
-        phi_all[:, span_of(i + steps, CHUNK)] = values[: NI * half]
+        phi_all[:, span_of(i + steps, WIDE)] = values[: NI * half]
+        sorted_pairs[:, span] = dot_nn(by_point, pairs[:, span]).astype(BF16)
         return carry
 
     lax.fori_loop(0, steps, angular, 0)
+    for copy in near:
+        copy.wait()
 
     def radial(t, carry):
         span = span_of(t, TILE)
@@ -322,32 +354,30 @@
         shrink_ahead = jnp.exp(-(degree + 1.0) * step)
         shrink_behind = jnp.exp(-degree * step)
         factor = 4.0 * step / (2.0 * degree + 1.0)
-        far = dot_nn(pairs[...], far_table[:, span])
-        work[...] = far.reshape(NP, half, TILE)
-        for start, values in ((x * NC, part), (NC - x * NC, other_part)):
-            near = values[:, span].astype(F32).reshape(NC, half, TILE)
-            work[pl.ds(start, NC)] = work[pl.ds(start, NC)] + near
+        density = dot_nn(sorted_pairs[...], far_table[:, span]) + dot_nn(by_point, part[:, span])
+        work[...] = density.reshape(half, NP, TILE)
         ahead = earlier[:, span]
         behind = later[:, span] * shrink_behind
         for j in range(half):
-            ahead = ahead * shrink_ahead + work[:, j, :]
-            total[:, j, :] = ahead
+            ahead = ahead * shrink_ahead + work[j]
+            total[j] = ahead
         for j in range(half - 1, -1, -1):
-            total[:, j, :] = factor * (total[:, j, :] + behind)
-            behind = (behind + work[:, j, :]) * shrink_behind
-        pot[:, span] = total[...].reshape(NP * half, TILE).astype(BF16)
+            total[j] = factor * (total[j] + behind)
+            behind = (behind + work[j]) * shrink_behind
+        potential = total[...].reshape(NP * half, TILE).astype(BF16)
+        pot[:, span] = dot_nn(by_pair, potential).astype(BF16)
         return carry
 
     lax.fori_loop(0, channels // TILE, radial, 0)
 
     def weigh(source, weight_at, first):
         def chunk(i, carry):
-            span = span_of(i, CHUNK)
-            at = span_of(i + first, CHUNK)
+            span = span_of(i, WIDE)
+            at = span_of(i + first, WIDE)
             angle = dot_nt(pot[...], source[span, :])
             values = phi_all[:, at].astype(F32) * weight_at[:, span]
             for k in range(NC):
-                value = jnp.zeros((half, CHUNK), F32)
+                value = jnp.zeros((half, WIDE), F32)
                 for o in range(NI):
                     row = (o * NC + k) * half
                     value += values[o * half : (o + 1) * half] * angle[row : row + half]
@@ -360,15 +390,17 @@
     fetch_table.wait()
     weigh(table, weight, 0)
     share = channels // 2
-    third = share // 3
-    for t in range(3):
-        away = pl.ds(pl.multiple_of((1 - x) * share + t * third, third), third)
-        home = pl.ds(pl.multiple_of(x * share + t * third, third), third)
-        columns = slice(t * third, (t + 1) * third)
-        for out, place_at in ((send_ref, away), (keep_ref, home)):
-            value = dot_nn(product[:, :quad], table[:, place_at])
-            value += dot_nn(product[:, quad:], far_table[:, place_at])
-            out[:, columns] = (-value).astype(out.dtype)
+    leave = []
+    for n, (out, to, first) in enumerate(
+        ((send_ref, send_any, (1 - x) * share), (keep_ref, keep_any, x * share))
+    ):
+        at = pl.ds(pl.multiple_of(first, share), share)
+        value = dot_nn(product[:, :quad], table[:, at]) + dot_nn(product[:, quad:], far_table[:, at])
+        out[...] = (-value).astype(out.dtype)
+        leave.append(pltpu.make_async_copy(out, to, sems.at[n]))
+        leave[n].start()
+    for copy in leave:
+        copy.wait()
 
 
 def slab_kernel(place, table, *refs):
@@ -393,6 +425,7 @@
 VMEM_SPEC = pl.BlockSpec(memory_space=pltpu.VMEM)
 SMEM_SPEC = pl.BlockSpec(memory_space=pltpu.SMEM)
 HBM_SPEC = pl.BlockSpec(memory_space=pl.ANY)
+ANY_SPEC = HBM_SPEC
 
 
 def shards_by_table(orbitals, continuum, harmonic_table, ang_weight, channel_lm):
@@ -428,13 +461,13 @@
     hbm = pl.BlockSpec(memory_space=pltpu.HBM)
     slabs = pl.pallas_call(
         slab_kernel,
-        out_shape=tuple(jax.ShapeDtypeStruct((n * size, channels), BF16) for n in (1, 1, 2)),
+        out_shape=tuple(jax.ShapeDtypeStruct((n * size, channels), BF16) for n in (1, 2)),
         in_specs=[SMEM_SPEC, hbm],
-        out_specs=(VMEM_SPEC,) * 3,
-        scratch_shapes=[pltpu.SemaphoreType.DMA((3,))],
+        out_specs=(VMEM_SPEC,) * 2,
+        scratch_shapes=[pltpu.SemaphoreType.DMA((2,))],
         name="slabs",
     )(
-        jnp.stack([offset(corner, core, 0), offset(corner, core, 1), offset(corner ^ 3, core, 0)]),
+        jnp.stack([offset(corner, core, 0), offset(corner ^ 3, core, 0)]),
         in_hbm(harmonic_table),
     )
 
@@ -442,14 +475,13 @@
     weight = ang_weight[None, :]
     degree = channel_degree(channel_lm)[None, :]
     cont = continuum.reshape(NC * points, channels)
-    place = jnp.stack([x]).astype(jnp.int32)
+    place = jnp.stack([x, offset(corner, core, 1)]).astype(jnp.int32)
     part_shape = jax.ShapeDtypeStruct((NC * half, channels), BF16)
     phi_shape = jax.ShapeDtypeStruct((half, quad), BF16)
 
     other = over_x(own)
     first_a = over_x(slabs[0])
-    first_b = over_x(slabs[1])
-    last = over_x(slabs[2])
+    last = over_x(slabs[1])
     part, phi, psi, own_ends, table = pl.pallas_call(
         functools.partial(own_kernel, step),
         out_shape=(
@@ -460,8 +492,10 @@
             jax.ShapeDtypeStruct((quad, channels), BF16),
         ),
         in_specs=[SMEM_SPEC] + [VMEM_SPEC] * 4 + [pl.BlockSpec(memory_space=pltpu.HBM)],
-        out_specs=(VMEM_SPEC,) * 5,
+        out_specs=(ANY_SPEC,) * 2 + (VMEM_SPEC,) * 3,
         scratch_shapes=[
+            pltpu.VMEM((NC * half, channels), BF16),
+            pltpu.VMEM((half, quad), BF16),
             pltpu.VMEM(((1 + NC) * points, channels), BF16),
             pltpu.VMEM((NC * points, quad), BF16),
             pltpu.VMEM((NC * points, TILE), F32),
@@ -470,14 +504,22 @@
         compiler_params=pltpu.CompilerParams(vmem_limit_bytes=16 << 20),
         name="own_orbital",
     )(place, own, cont, weight, degree, in_hbm(after(harmonic_table, slabs[0])))
-    other_part, other_phi, ends = pl.pallas_call(
+    other_part, other_phi, ends, slab = pl.pallas_call(
         functools.partial(other_kernel, step),
-        out_shape=(part_shape, phi_shape, jax.ShapeDtypeStruct((4 * NP, channels), F32)),
+        out_shape=(
+            part_shape,
+            phi_shape,
+            jax.ShapeDtypeStruct((4 * NP, channels), F32),
+            jax.ShapeDtypeStruct((size, channels), BF16),
+        ),
         in_specs=[SMEM_SPEC] + [VMEM_SPEC] * 6,
-        out_specs=(VMEM_SPEC,) * 3,
+        out_specs=(ANY_SPEC, ANY_SPEC, VMEM_SPEC, ANY_SPEC),
         scratch_shapes=[
+            pltpu.VMEM((NC * half, channels), BF16),
+            pltpu.VMEM((half, quad), BF16),
             pltpu.VMEM((NC * points, quad), BF16),
             pltpu.VMEM((NC * points, TILE), F32),
+            pltpu.SemaphoreType.DMA((3,)),
         ],
         compiler_params=pltpu.CompilerParams(vmem_limit_bytes=8 << 20),
         name="other_orbital",
@@ -512,8 +554,9 @@
         later += jnp.where(before, 0.0, behind_by(points * distance)) * came[NP:]
         row_end += ahead_by(points * (3 - v)) * came[:NP]
         row_start += behind_by(points * v) * came[NP:]
-    row_end = after(row_end.astype(BF16), first_a, first_b)
-    row_start = after(row_start.astype(BF16), first_a, first_b)
+    row_end = after(row_end.astype(BF16), first_a, last)
+    row_start = after(row_start.astype(BF16), first_a, last)
+    first_b = over_x(after(slab, row_end))
     for shift in (1, 2, 3):
         message = jnp.where(z + shift < 4, row_end, row_start)
         came = lax.ppermute(message, "grid", [(n, (n + 4 * shift) % 16) for n in everyone])
@@ -528,16 +571,22 @@
     theirs = jnp.concatenate(
         [jnp.where(x == 0, upper_earlier, earlier), jnp.where(x == 0, later, lower_later)], axis=0
     )
-    theirs = after(theirs.astype(BF16), last)
+    terms, rest = [], weight
+    for _ in range(3):
+        terms.append(lax.reduce_precision(rest, 8, 7))
+        rest = rest - terms[-1]
+    terms = jnp.pad(jnp.concatenate(terms, axis=0), ((0, NP - 3), (0, channels - quad)))
+    theirs = jnp.concatenate([theirs, terms], axis=0)
+    theirs = theirs.astype(BF16)
     came = over_x(theirs).astype(F32)
+    far_weight = jnp.sum(came[2 * NP : 2 * NP + 3, :quad], axis=0, keepdims=True)
     earlier = jnp.where(x == 0, earlier, upper_earlier) + came[:NP]
-    later = jnp.where(x == 0, lower_later, later) + came[NP:]
-    first_b = after(first_b, row_end)
+    later = jnp.where(x == 0, lower_later, later) + came[NP : 2 * NP]
+    first_b = after(first_b, theirs)
     received = [first_a, first_b, last]
     received += [flip(first_a, 2), flip(first_a, 4), flip(first_b, 2), flip(first_b, 4)]
     which = [(corner, 0), (corner, 1), (corner ^ 3, 0)]
     which += [(corner ^ 1, 0), (corner ^ 2, 0), (corner ^ 1, 1), (corner ^ 2, 1)]
-    far_weight = over_x(after(weight, received[3]))
     far = received + [flip(value, 1) for value in received]
     offsets = [offset(w, core, n) for w, n in which] + [offset(w, 1 - core, n) for w, n in which]
     places = jnp.stack([x] + offsets).astype(jnp.int32)
@@ -548,21 +597,25 @@
             jax.ShapeDtypeStruct((NC * half, channels // 2), BF16),
             jax.ShapeDtypeStruct((NC * half, channels // 2), F32),
         ),
-        in_specs=[SMEM_SPEC, hbm, VMEM_SPEC, hbm] + [VMEM_SPEC] * 9 + [hbm] + [HBM_SPEC] * pieces,
-        out_specs=(VMEM_SPEC,) * 2,
+        in_specs=[SMEM_SPEC, hbm, VMEM_SPEC, hbm] + [VMEM_SPEC] * 5 + [ANY_SPEC] * 4 + [hbm] + [HBM_SPEC] * pieces,
+        out_specs=(ANY_SPEC,) * 2,
         scratch_shapes=[
+            pltpu.VMEM((NC * half, channels // 2), BF16),
+            pltpu.VMEM((NC * half, channels // 2), F32),
+            pltpu.VMEM((NP * half, channels), BF16),
             pltpu.VMEM((quad, channels), BF16),
             pltpu.VMEM((quad, channels), BF16),
             pltpu.VMEM(((NI + NC) * half, channels), BF16),
             pltpu.VMEM((NP * half, quad), BF16),
+            pltpu.VMEM((NP * half, quad), BF16),
             pltpu.VMEM((NI * half, 2 * quad), BF16),
             pltpu.VMEM((NP * half, channels), BF16),
             pltpu.VMEM((NC * half, 2 * quad), BF16),
-            pltpu.VMEM((NP, half, TILE), F32),
-            pltpu.VMEM((NP, half, TILE), F32),
-            pltpu.SemaphoreType.DMA((pieces + 2 + NC,)),
+            pltpu.VMEM((half, NP, TILE), F32),
+            pltpu.VMEM((half, NP, TILE), F32),
+            pltpu.SemaphoreType.DMA((pieces + 6 + NC,)),
         ],
-        compiler_params=pltpu.CompilerParams(vmem_limit_bytes=26 << 20),
+        compiler_params=pltpu.CompilerParams(vmem_limit_bytes=30 << 20),
         name="finish",
     )(
         places, in_hbm(own), other, in_hbm(cont), weight, far_weight, degree, earlier, later,

time: 98.6 us -> 95 us (0.963)
  other arithmetic: 4.23 us -> 11.9 us
  waiting for transfers between devices: 28.9 us -> 22.1 us
  local copies, waits for them, and re-layouts: 8.18 us -> 3.84 us
  Pallas kernels: 36.5 us -> 34.9 us
  starting transfers between devices: 20 us -> 21.2 us
    ppermute x7 -> x6, waiting for transfers between devices: 18 us -> 12.7 us  [over_x(): return lax.ppermute(value, 'orb', across)]
    unnamed x32 -> x34, local copies, waits for them, and re-layouts: 8.08 us -> 3.72 us
    pallas_call x1, Pallas kernels: 19.5 us -> 16.4 us  [shards_by_table(): pl.pallas_call(functools.partial(finish_kernel, step, pieces), out_shape=...]
    convert_element_type x3, other arithmetic: 0.04 us -> 1.8 us  [shards_by_table(): came = flip(message, bits).astype(F32)]
    another operation x4 -> x6, other arithmetic: 1.96 us -> 3.68 us
    convert_element_type x2, other arithmetic: 0.11 us -> 1.66 us  [the longest x1 0.87 us: shards_by_table(): row_end = after(row_end.astype(BF16), first_a, last)]
    ppermute x14, waiting for transfers between devices: 10.7 us -> 9.41 us  [flip(): return lax.ppermute(value, 'grid', [(n, n ^ bits) for n in everyone])]
    ppermute x3, starting transfers between devices: 4.67 us -> 5.76 us  [shards_by_table(): lax.ppermute(message, 'grid', [(n, (n + 4 * shift) % 16) for n in everyone])]
  transfers between devices with their start and end apart: 24 -> 23, of which waited for: 9 -> 10; matrix products, arithmetic and copies ran while one was open for 4% -> 12% of each run, Pallas kernels for 15% -> 17%
where the time goes in v3:
time: 95 us; the launch traced here: 94.4 us
  Pallas kernels  34.9 us (37%)
  waiting for transfers between devices  22.1 us (23%)
  starting transfers between devices  21.2 us (22%)
  other arithmetic  11.9 us (13%)
  local copies, waits for them, and re-layouts  3.84 us (4%)
    pallas_call x1, Pallas kernels, shards_by_table(): pl.pallas_call(functools.partial(finish_kernel, step, pieces), out_shape=...  16.4 us
    ppermute x6, waiting for transfers between devices, over_x(): return lax.ppermute(value, 'orb', across)  12.7 us
    ppermute x14, waiting for transfers between devices, flip(): return lax.ppermute(value, 'grid', [(n, n ^ bits) for n in everyone])  9.41 us
    ppermute x6, starting transfers between devices, over_x(): return lax.ppermute(value, 'orb', across)  8.69 us
    pallas_call x1, Pallas kernels, shards_by_table(): pl.pallas_call(functools.partial(own_kernel, step), out_shape=(part_shape...  7.36 us
    ppermute x14, starting transfers between devices, flip(): return lax.ppermute(value, 'grid', [(n, n ^ bits) for n in everyone])  6.7 us
    pallas_call x1, Pallas kernels, shards_by_table(): pl.pallas_call(functools.partial(other_kernel, step), out_shape=(part_sha...  6.01 us
    ppermute x3, starting transfers between devices, shards_by_table(): lax.ppermute(message, 'grid', [(n, (n + 4 * shift) % 16) for n in everyone])  5.76 us
  transfers between devices with their start and end apart: 23, of which 10 were waited for; matrix products, arithmetic and copies ran while one was open for 12% of the time, Pallas kernels for 17%

profile of v3, /device:TPU:0, one launch (start us, length us, event | category | flops | bytes accessed | tf_op | source)
XLA Modules:
  0.0 94.4 jit_solution(15363298300753216345)
XLA Ops:
  0.0 3.0 %collective-permute-start = (bf16[64,2304]{1,0:T(8,128)(2,1)}, bf16[64,2304]{1,0:T(8,128)(2,1)S(1)}, u32[]{:S(2)}, u32[]{:S(2)}) collective-permute-start(bf16[64,2304]{1,0:T(8,128)(2,1)} %bitcast.20), channel_id=1, source_target_pairs={{0,16},{16,0},{1,17},{17,1},{2,18},{18,2},{3,19},{19,3},{4,20},{20... | collective-permute-start | bytes 884744 | tf_op jit(solution)/shard_map/ppermute | solution.py:443
  3.0 0.6 pad_add_fusion.1.place
  3.7 2.9 %slabs.1 = (bf16[80,2304]{1,0:T(8,128)(2,1)}, bf16[160,2304]{1,0:T(8,128)(2,1)}) custom-call(s32[2]{0:T(128)} %pad_add_fusion.1.place, bf16[1280,2304]{1,0:T(8,128)(2,1)} %table_hbm.2), custom_call_target="tpu_custom_call" | custom-call | tf_op jit(solution)/shard_map/slabs/pallas_call | solution.py:462
  6.6 0.1 collective-permute-start.4
  6.7 1.9 %collective-permute-start.5 = (bf16[160,2304]{1,0:T(8,128)(2,1)}, bf16[160,2304]{1,0:T(8,128)(2,1)S(1)}, u32[]{:S(2)}, u32[]{:S(2)}) collective-permute-start(bf16[160,2304]{1,0:T(8,128)(2,1)} %get-tuple-element.31), channel_id=1, source_target_pairs={{0,16},{16,0},{1,17},{17,1},{2,18},{18,2},{3,19},{19,3},{4,20},{20... | collective-permute-start | bytes 2211848 | tf_op jit(solution)/shard_map/ppermute | solution.py:443
  8.7 0.1 convert_reduce_fusion
  8.9 0.6 exponential_select_fusion.2
  9.6 0.1 pad_add_fusion.place
  9.6 7.4 %own_orbital.1 = (bf16[128,2304]{1,0:T(8,128)(2,1)S(1)}, bf16[32,1280]{1,0:T(8,128)(2,1)S(1)}, bf16[256,1280]{1,0:T(8,128)(2,1)S(1)}, f32[16,2304]{1,0:T(8,128)S(1)}, bf16[1280,2304]{1,0:T(8,128)(2,1)S(1)}) custom-call(s32[2]{0:T(128)S(1)} %pad_add_fusion.place, bf16[64,2304]{1,0:T(8,128)(2,1)S(1)} %bitcast.22, bf16[256,2304]{1,0:T(8,128)(2,1)S(1)} %bitcast.19, ...), custom_call_target="tpu_custom_call" | custom-call | tf_op jit(solution)/shard_map/own_orbital/pallas_call | solution.py:485
  17.0 0.7 exponential_select_fusion.11
  17.7 0.0 collective-permute-done.other
  17.8 6.0 %other_orbital.1 = (bf16[128,2304]{1,0:T(8,128)(2,1)S(1)}, bf16[32,1280]{1,0:T(8,128)(2,1)S(1)}, f32[32,2304]{1,0:T(8,128)S(1)}, bf16[80,2304]{1,0:T(8,128)(2,1)S(1)}) custom-call(s32[2]{0:T(128)S(1)} %pad_add_fusion.place, bf16[64,2304]{1,0:T(8,128)(2,1)S(1)} %collective-permute-done.other, bf16[256,1280]{1,0:T(8,128)(2,1)S(1)} %get-tuple-element.26.psi_ref, ...), custom_call_target="tpu_custom_call" | custom-call | tf_op jit(solution)/shard_map/other_orbital/pallas_call | solution.py:507
  23.8 0.7 pad_maximum_fusion.1
  24.6 1.5 %collective-permute-start.2 = (bf16[16,2304]{1,0:T(8,128)(2,1)}, bf16[16,2304]{1,0:T(8,128)(2,1)}, u32[]{:S(2)}, u32[]{:S(2)}) collective-permute-start(bf16[16,2304]{1,0:T(8,128)(2,1)} %pad_maximum_fusion.1), channel_id=1, source_target_pairs={{0,2},{1,3},{2,0},{3,1},{4,6},{5,7},{6,4},{7,5},{8,10},{9,11},{10,... | collective-permute-start | bytes 221192 | tf_op jit(solution)/shard_map/ppermute | solution.py:446
  26.1 0.3 collective-permute-start.3
  26.5 0.9 convert_element_type.90
  27.4 2.4 %collective-permute-done.2 = bf16[16,2304]{1,0:T(8,128)(2,1)} collective-permute-done((bf16[16,2304]{1,0:T(8,128)(2,1)}, bf16[16,2304]{1,0:T(8,128)(2,1)}, u32[]{:S(2)}, u32[]{:S(2)}) %collective-permute-start.2) | collective-permute-done | bytes 73760 | tf_op jit(solution)/shard_map/ppermute | solution.py:446
  29.7 0.9 convert_element_type.92
  30.6 0.1 collective-permute-done.3
  30.8 0.9 add_convert_fusion.1
  31.7 0.0 collective-permute-done.4.refs_0_
  31.7 0.8 add_convert_fusion
  32.5 1.4 %collective-permute-done.5.refs_2_ = bf16[160,2304]{1,0:T(8,128)(2,1)S(1)} collective-permute-done((bf16[160,2304]{1,0:T(8,128)(2,1)}, bf16[160,2304]{1,0:T(8,128)(2,1)S(1)}, u32[]{:S(2)}, u32[]{:S(2)}) %collective-permute-start.5) | collective-permute-done | bytes 737312 | tf_op jit(solution)/shard_map/ppermute | solution.py:443
  33.9 0.6 broadcast_select_fusion.2
  34.6 1.8 %collective-permute-start.6 = (bf16[8,2304]{1,0:T(8,128)(2,1)}, bf16[8,2304]{1,0:T(8,128)(2,1)S(1)}, u32[]{:S(2)}, u32[]{:S(2)}) collective-permute-start(bf16[8,2304]{1,0:T(8,128)(2,1)} %get-tuple-element.51), channel_id=1, source_target_pairs={{0,4},{1,5},{2,6},{3,7},{4,8},{5,9},{6,10},{7,11},{8,12},{9,13},{1... | collective-permute-start | bytes 110600 | tf_op jit(solution)/shard_map/ppermute | solution.py:562
  36.4 2.6 %collective-permute-start.7 = (bf16[8,2304]{1,0:T(8,128)(2,1)}, bf16[8,2304]{1,0:T(8,128)(2,1)S(1)}, u32[]{:S(2)}, u32[]{:S(2)}) collective-permute-start(bf16[8,2304]{1,0:T(8,128)(2,1)} %get-tuple-element.53), channel_id=1, source_target_pairs={{0,8},{1,9},{2,10},{3,11},{4,12},{5,13},{6,14},{7,15},{8,0},{9,1},... | collective-permute-start | bytes 110600 | tf_op jit(solution)/shard_map/ppermute | solution.py:562
  39.0 1.3 %collective-permute-start.8 = (bf16[8,2304]{1,0:T(8,128)(2,1)}, bf16[8,2304]{1,0:T(8,128)(2,1)}, u32[]{:S(2)}, u32[]{:S(2)}) collective-permute-start(bf16[8,2304]{1,0:T(8,128)(2,1)} %get-tuple-element.52), channel_id=1, source_target_pairs={{0,12},{1,13},{2,14},{3,15},{4,0},{5,1},{6,2},{7,3},{8,4},{9,5},{1... | collective-permute-start | bytes 110600 | tf_op jit(solution)/shard_map/ppermute | solution.py:562
  40.4 1.6 %collective-permute-start.11 = (bf16[80,2304]{1,0:T(8,128)(2,1)S(1)}, bf16[80,2304]{1,0:T(8,128)(2,1)S(1)}, u32[]{:S(2)}, u32[]{:S(2)}) collective-permute-start(bf16[80,2304]{1,0:T(8,128)(2,1)S(1)} %collective-permute-done.4.refs_0_), channel_id=1, source_target_pairs={{0,2},{1,3},{2,0},{3,1},{4,6},{5,7},{6,4},{7,5},{8,10},{9,11},{10,... | collective-permute-start | bytes 1105928 | tf_op jit(solution)/shard_map/ppermute | solution.py:446
  42.0 0.7 collective-permute-start.12
  42.7 1.5 %collective-permute-start.10 = (bf16[80,2304]{1,0:T(8,128)(2,1)}, bf16[80,2304]{1,0:T(8,128)(2,1)}, u32[]{:S(2)}, u32[]{:S(2)}) collective-permute-start(bf16[80,2304]{1,0:T(8,128)(2,1)} %copy-done.6), channel_id=1, source_target_pairs={{0,16},{16,0},{1,17},{17,1},{2,18},{18,2},{3,19},{19,3},{4,20},{20... | collective-permute-start | bytes 1105928 | tf_op jit(solution)/shard_map/ppermute | solution.py:443
  44.2 0.0 collective-permute-done.7
  44.2 0.0 collective-permute-done.8
  44.2 0.6 copy-done.12
  44.8 1.2 %select_convert_fusion.1 = (bf16[8,2304]{1,0:T(8,128)(2,1)S(1)}, f32[8,2304]{1,0:T(8,128)S(1)}) fusion(f32[32,2304]{1,0:T(8,128)S(1)} %get-tuple-element.29, f32[2304]{0:T(1024)S(1)} %get-tuple-element.69, pred[]{:T(512)S(6)} %eq.14, bf16[8,2304]{1,0:T(8,128)(2,1)} %collective-permute-done.8, f32[2304]{0:T(1024)} %get-tuple-element.63, ...), kind=kLoop, calls=%fused_computation.25 | loop fusion | flops 331776 | bytes 580609 | tf_op jit(solution)/shard_map/convert
  46.0 1.8 %select_convert_fusion = (bf16[8,2304]{1,0:T(8,128)(2,1)S(1)}, f32[8,2304]{1,0:T(8,128)}) fusion(f32[32,2304]{1,0:T(8,128)S(1)} %get-tuple-element.29, f32[2304]{0:T(1024)S(1)} %get-tuple-element.68, pred[]{:T(512)S(6)} %eq.14, bf16[8,2304]{1,0:T(8,128)(2,1)} %collective-permute-done.8, f32[2304]{0:T(1024)} %get-tuple-element.75, ...), kind=kLoop, calls=%fused_computation.23 | loop fusion | flops 331776 | bytes 580609 | tf_op jit(solution)/shard_map/convert.1
  47.7 0.6 collective-permute-start.9
  48.3 0.0 collective-permute-start.15
  48.3 0.8 collective-permute-done.11.refs_3_
  49.1 0.0 collective-permute-start.18
  49.1 3.1 %collective-permute-done.10.refs_1_ = bf16[80,2304]{1,0:T(8,128)(2,1)} collective-permute-done((bf16[80,2304]{1,0:T(8,128)(2,1)}, bf16[80,2304]{1,0:T(8,128)(2,1)}, u32[]{:S(2)}, u32[]{:S(2)}) %collective-permute-start.10) | collective-permute-done | bytes 368672 | tf_op jit(solution)/shard_map/ppermute | solution.py:443
  52.2 0.5 collective-permute-start.13
  52.7 0.6 collective-permute-done.9
  53.3 0.6 copy-done.13
  54.0 1.3 %collective-permute-start.14 = (bf16[80,2304]{1,0:T(8,128)(2,1)}, bf16[80,2304]{1,0:T(8,128)(2,1)}, u32[]{:S(2)}, u32[]{:S(2)}) collective-permute-start(bf16[80,2304]{1,0:T(8,128)(2,1)} %collective-permute-done.10.refs_1_), channel_id=1, source_target_pairs={{0,4},{1,5},{2,6},{3,7},{4,0},{5,1},{6,2},{7,3},{8,12},{9,13},{10,... | collective-permute-start | bytes 1105928 | tf_op jit(solution)/shard_map/ppermute | solution.py:446
  55.3 0.1 stack.74.place
  55.4 0.9 convert_element_type.114
  56.3 0.0 collective-permute-done.12.refs_4_
  56.3 0.1 collective-permute-start.17
  56.5 0.6 collective-permute-start.19
  57.0 0.0 collective-permute-done.18.refs_10_
  57.0 0.1 collective-permute-start.16
  57.1 3.3 %collective-permute-done.13.refs_5_ = bf16[80,2304]{1,0:T(8,128)(2,1)} collective-permute-done((bf16[80,2304]{1,0:T(8,128)(2,1)}, bf16[80,2304]{1,0:T(8,128)(2,1)}, u32[]{:S(2)}, u32[]{:S(2)}) %collective-permute-start.13) | collective-permute-done | bytes 368672 | tf_op jit(solution)/shard_map/ppermute | solution.py:446
  60.4 0.0 collective-permute-start.20
  60.4 1.9 %collective-permute-done.14.refs_6_ = bf16[80,2304]{1,0:T(8,128)(2,1)} collective-permute-done((bf16[80,2304]{1,0:T(8,128)(2,1)}, bf16[80,2304]{1,0:T(8,128)(2,1)}, u32[]{:S(2)}, u32[]{:S(2)}) %collective-permute-start.14) | collective-permute-done | bytes 368672 | tf_op jit(solution)/shard_map/ppermute | solution.py:446
  62.3 0.9 slice_add_fusion
  63.2 0.0 collective-permute-done.16.refs_8_
  63.3 0.9 collective-permute-done.21.refs_13_
  64.2 0.9 copy-done.4
  65.1 16.4 %finish.1 = (bf16[128,1152]{1,0:T(8,128)(2,1)S(1)}, f32[128,1152]{1,0:T(8,128)S(1)}) custom-call(s32[15]{0:T(128)S(1)} %stack.74.place, bf16[64,2304]{1,0:T(8,128)(2,1)} %bitcast.21, bf16[64,2304]{1,0:T(8,128)(2,1)S(1)} %collective-permute-done.other, bf16[256,2304]{1,0:T(8,128)(2,1)} %bitcast.18, f32[1,1280]{1,0:T(1,128)S(1)} %broadcast_in_dim.27.weight, ...), custom_call_target="tpu_custom_call" | custom-call | tf_op jit(solution)/shard_map/finish/pallas_call | solution.py:594
  81.5 0.8 copy-done.2
  82.3 1.5 %collective-permute-start.22 = (bf16[128,1152]{1,0:T(8,128)(2,1)S(1)}, bf16[128,1152]{1,0:T(8,128)(2,1)S(1)}, u32[]{:S(2)}, u32[]{:S(2)}) collective-permute-start(bf16[128,1152]{1,0:T(8,128)(2,1)S(1)} %get-tuple-element.42), channel_id=1, source_target_pairs={{0,16},{16,0},{1,17},{17,1},{2,18},{18,2},{3,19},{19,3},{4,20},{20... | collective-permute-start | bytes 884744 | tf_op jit(solution)/shard_map/ppermute | solution.py:443
  83.8 7.6 %collective-permute-done.22.came = bf16[128,1152]{1,0:T(8,128)(2,1)S(1)} collective-permute-done((bf16[128,1152]{1,0:T(8,128)(2,1)S(1)}, bf16[128,1152]{1,0:T(8,128)(2,1)S(1)}, u32[]{:S(2)}, u32[]{:S(2)}) %collective-permute-start.22) | collective-permute-done | bytes 294944 | tf_op jit(solution)/shard_map/ppermute | solution.py:443
  91.4 0.7 copy-done.10
  92.1 2.2 %place.1 = f32[4,64,1152]{2,1,0:T(8,128)} custom-call(s32[2]{0:T(128)} %copy-done.5, f32[128,1152]{1,0:T(8,128)} %copy-done.2, bf16[128,1152]{1,0:T(8,128)(2,1)} %copy-done.10), custom_call_target="tpu_custom_call" | custom-call | tf_op jit(solution)/shard_map/place/pallas_call | solution.py:625
  (50 shorter events, 0.2 us)
Async XLA Ops:
  0.0 9.6 %copy-start.1 = (bf16[1,64,2304]{2,1,0:T(8,128)(2,1)S(1)}, bf16[1,64,2304]{2,1,0:T(8,128)(2,1)}, u32[]{:S(2)}) copy-start(bf16[1,64,2304]{2,1,0:T(8,128)(2,1)} %param.5) | copy-start | bytes 884740
  0.0 8.7 %copy-start.16 = (s32[2304]{0:T(1024)S(1)}, s32[2304]{0:T(1024)}, u32[]{:S(2)}) copy-start(s32[2304]{0:T(1024)} %param.9) | copy-start | bytes 27652
  0.0 8.8 %copy-start.15 = (f32[1280]{0:T(1024)S(1)}, f32[1280]{0:T(1024)}, u32[]{:S(2)}) copy-start(f32[1280]{0:T(1024)} %param.8) | copy-start | bytes 15364
  0.0 9.6 %copy-start = (bf16[4,64,2304]{2,1,0:T(8,128)(2,1)S(1)}, bf16[4,64,2304]{2,1,0:T(8,128)(2,1)}, u32[]{:S(2)}) copy-start(bf16[4,64,2304]{2,1,0:T(8,128)(2,1)} %param.6) | copy-start | bytes 3538948
  0.0 17.7 %collective-permute-start = (bf16[64,2304]{1,0:T(8,128)(2,1)}, bf16[64,2304]{1,0:T(8,128)(2,1)S(1)}, u32[]{:S(2)}, u32[]{:S(2)}) collective-permute-start(bf16[64,2304]{1,0:T(8,128)(2,1)} %bitcast.20), channel_id=1, source_target_pairs={{0,16},{16,0},{1,17},{17,1},{2,18},{18,2},{3,19},{19,3},{4,20},{20... | collective-permute-start | bytes 884744 | tf_op jit(solution)/shard_map/ppermute | solution.py:443
  6.6 25.1 %collective-permute-start.4 = (bf16[80,2304]{1,0:T(8,128)(2,1)}, bf16[80,2304]{1,0:T(8,128)(2,1)S(1)}, u32[]{:S(2)}, u32[]{:S(2)}) collective-permute-start(bf16[80,2304]{1,0:T(8,128)(2,1)} %get-tuple-element.24), channel_id=1, source_target_pairs={{0,16},{16,0},{1,17},{17,1},{2,18},{18,2},{3,19},{19,3},{4,20},{20... | collective-permute-start | bytes 1105928 | tf_op jit(solution)/shard_map/ppermute | solution.py:443
  6.7 27.2 %collective-permute-start.5 = (bf16[160,2304]{1,0:T(8,128)(2,1)}, bf16[160,2304]{1,0:T(8,128)(2,1)S(1)}, u32[]{:S(2)}, u32[]{:S(2)}) collective-permute-start(bf16[160,2304]{1,0:T(8,128)(2,1)} %get-tuple-element.31), channel_id=1, source_target_pairs={{0,16},{16,0},{1,17},{17,1},{2,18},{18,2},{3,19},{19,3},{4,20},{20... | collective-permute-start | bytes 2211848 | tf_op jit(solution)/shard_map/ppermute | solution.py:443
  9.6 14.1 %copy-start.5 = (s32[2]{0:T(128)}, s32[2]{0:T(128)S(1)}, u32[]{:S(2)}) copy-start(s32[2]{0:T(128)S(1)} %pad_add_fusion.place) | copy-start | bytes 28
  17.0 6.8 %copy-start.3 = (bf16[32,1280]{1,0:T(8,128)(2,1)}, bf16[32,1280]{1,0:T(8,128)(2,1)S(1)}, u32[]{:S(2)}) copy-start(bf16[32,1280]{1,0:T(8,128)(2,1)S(1)} %get-tuple-element.36.phi_any) | copy-start | bytes 245764
  17.7 14.0 %copy-start.14 = (f32[2304]{0:T(1024)S(1)}, f32[2304]{0:T(1024)}, u32[]{:S(2)}) copy-start(f32[2304]{0:T(1024)} %get-tuple-element.65) | copy-start | bytes 27652
  23.8 16.6 %copy-start.6 = (bf16[80,2304]{1,0:T(8,128)(2,1)}, bf16[80,2304]{1,0:T(8,128)(2,1)S(1)}, u32[]{:S(2)}) copy-start(bf16[80,2304]{1,0:T(8,128)(2,1)S(1)} %get-tuple-element.39) | copy-start | bytes 1105924
  24.6 1.9 %collective-permute-start.1 = (bf16[16,2304]{1,0:T(8,128)(2,1)}, bf16[16,2304]{1,0:T(8,128)(2,1)}, u32[]{:S(2)}, u32[]{:S(2)}) collective-permute-start(bf16[16,2304]{1,0:T(8,128)(2,1)} %pad_maximum_fusion.1), channel_id=1, source_target_pairs={{0,1},{1,0},{2,3},{3,2},{4,5},{5,4},{6,7},{7,6},{8,9},{9,8},{10,11... | collective-permute-start | bytes 221192 | tf_op jit(solution)/shard_map/ppermute | solution.py:446
  24.6 5.2 %collective-permute-start.2 = (bf16[16,2304]{1,0:T(8,128)(2,1)}, bf16[16,2304]{1,0:T(8,128)(2,1)}, u32[]{:S(2)}, u32[]{:S(2)}) collective-permute-start(bf16[16,2304]{1,0:T(8,128)(2,1)} %pad_maximum_fusion.1), channel_id=1, source_target_pairs={{0,2},{1,3},{2,0},{3,1},{4,6},{5,7},{6,4},{7,5},{8,10},{9,11},{10,... | collective-permute-start | bytes 221192 | tf_op jit(solution)/shard_map/ppermute | solution.py:446
  26.1 4.7 %collective-permute-start.3 = (bf16[16,2304]{1,0:T(8,128)(2,1)}, bf16[16,2304]{1,0:T(8,128)(2,1)S(1)}, u32[]{:S(2)}, u32[]{:S(2)}) collective-permute-start(bf16[16,2304]{1,0:T(8,128)(2,1)} %pad_maximum_fusion.1), channel_id=1, source_target_pairs={{0,3},{1,2},{2,1},{3,0},{4,7},{5,6},{6,5},{7,4},{8,11},{9,10},{10,... | collective-permute-start | bytes 221192 | tf_op jit(solution)/shard_map/ppermute | solution.py:446
  27.4 6.6 %copy-start.7 = (f32[16,2304]{1,0:T(8,128)}, f32[16,2304]{1,0:T(8,128)S(1)}, u32[]{:S(2)}) copy-start(f32[16,2304]{1,0:T(8,128)S(1)} %convert_element_type.90) | copy-start | bytes 442372
  30.6 4.0 %copy-start.8 = (f32[16,2304]{1,0:T(8,128)}, f32[16,2304]{1,0:T(8,128)S(1)}, u32[]{:S(2)}) copy-start(f32[16,2304]{1,0:T(8,128)S(1)} %convert_element_type.92) | copy-start | bytes 442372
  30.8 3.8 %copy-start.9 = (f32[16,2304]{1,0:T(8,128)}, f32[16,2304]{1,0:T(8,128)S(1)}, u32[]{:S(2)}) copy-start(f32[16,2304]{1,0:T(8,128)S(1)} %convert_element_type.94) | copy-start | bytes 442372
  34.6 8.1 %collective-permute-start.6 = (bf16[8,2304]{1,0:T(8,128)(2,1)}, bf16[8,2304]{1,0:T(8,128)(2,1)S(1)}, u32[]{:S(2)}, u32[]{:S(2)}) collective-permute-start(bf16[8,2304]{1,0:T(8,128)(2,1)} %get-tuple-element.51), channel_id=1, source_target_pairs={{0,4},{1,5},{2,6},{3,7},{4,8},{5,9},{6,10},{7,11},{8,12},{9,13},{1... | collective-permute-start | bytes 110600 | tf_op jit(solution)/shard_map/ppermute | solution.py:562
  36.4 7.8 %collective-permute-start.7 = (bf16[8,2304]{1,0:T(8,128)(2,1)}, bf16[8,2304]{1,0:T(8,128)(2,1)S(1)}, u32[]{:S(2)}, u32[]{:S(2)}) collective-permute-start(bf16[8,2304]{1,0:T(8,128)(2,1)} %get-tuple-element.53), channel_id=1, source_target_pairs={{0,8},{1,9},{2,10},{3,11},{4,12},{5,13},{6,14},{7,15},{8,0},{9,1},... | collective-permute-start | bytes 110600 | tf_op jit(solution)/shard_map/ppermute | solution.py:562
  39.0 5.2 %collective-permute-start.8 = (bf16[8,2304]{1,0:T(8,128)(2,1)}, bf16[8,2304]{1,0:T(8,128)(2,1)}, u32[]{:S(2)}, u32[]{:S(2)}) collective-permute-start(bf16[8,2304]{1,0:T(8,128)(2,1)} %get-tuple-element.52), channel_id=1, source_target_pairs={{0,12},{1,13},{2,14},{3,15},{4,0},{5,1},{6,2},{7,3},{8,4},{9,5},{1... | collective-permute-start | bytes 110600 | tf_op jit(solution)/shard_map/ppermute | solution.py:562
  40.4 8.7 %collective-permute-start.11 = (bf16[80,2304]{1,0:T(8,128)(2,1)S(1)}, bf16[80,2304]{1,0:T(8,128)(2,1)S(1)}, u32[]{:S(2)}, u32[]{:S(2)}) collective-permute-start(bf16[80,2304]{1,0:T(8,128)(2,1)S(1)} %collective-permute-done.4.refs_0_), channel_id=1, source_target_pairs={{0,2},{1,3},{2,0},{3,1},{4,6},{5,7},{6,4},{7,5},{8,10},{9,11},{10,... | collective-permute-start | bytes 1105928 | tf_op jit(solution)/shard_map/ppermute | solution.py:446
  42.0 14.3 %collective-permute-start.12 = (bf16[80,2304]{1,0:T(8,128)(2,1)S(1)}, bf16[80,2304]{1,0:T(8,128)(2,1)}, u32[]{:S(2)}, u32[]{:S(2)}) collective-permute-start(bf16[80,2304]{1,0:T(8,128)(2,1)S(1)} %collective-permute-done.4.refs_0_), channel_id=1, source_target_pairs={{0,4},{1,5},{2,6},{3,7},{4,0},{5,1},{6,2},{7,3},{8,12},{9,13},{10,... | collective-permute-start | bytes 1105928 | tf_op jit(solution)/shard_map/ppermute | solution.py:446
  42.7 1.5 %copy-start.11 = (bf16[8,2304]{1,0:T(8,128)(2,1)}, bf16[8,2304]{1,0:T(8,128)(2,1)S(1)}, u32[]{:S(2)}) copy-start(bf16[8,2304]{1,0:T(8,128)(2,1)S(1)} %collective-permute-done.6) | copy-start | bytes 110596
  42.7 9.6 %collective-permute-start.10 = (bf16[80,2304]{1,0:T(8,128)(2,1)}, bf16[80,2304]{1,0:T(8,128)(2,1)}, u32[]{:S(2)}, u32[]{:S(2)}) collective-permute-start(bf16[80,2304]{1,0:T(8,128)(2,1)} %copy-done.6), channel_id=1, source_target_pairs={{0,16},{16,0},{1,17},{17,1},{2,18},{18,2},{3,19},{19,3},{4,20},{20... | collective-permute-start | bytes 1105928 | tf_op jit(solution)/shard_map/ppermute | solution.py:443
  44.2 0.6 copy-start.12
  47.7 5.6 %collective-permute-start.9 = (bf16[24,2304]{1,0:T(8,128)(2,1)S(1)}, bf16[24,2304]{1,0:T(8,128)(2,1)S(1)}, u32[]{:S(2)}, u32[]{:S(2)}) collective-permute-start(bf16[24,2304]{1,0:T(8,128)(2,1)S(1)} %pad_maximum_fusion), channel_id=1, source_target_pairs={{0,16},{16,0},{1,17},{17,1},{2,18},{18,2},{3,19},{19,3},{4,20},{20... | collective-permute-start | bytes 331784 | tf_op jit(solution)/shard_map/ppermute | solution.py:443
  48.3 8.1 %collective-permute-start.15 = (bf16[80,2304]{1,0:T(8,128)(2,1)S(1)}, bf16[80,2304]{1,0:T(8,128)(2,1)}, u32[]{:S(2)}, u32[]{:S(2)}) collective-permute-start(bf16[80,2304]{1,0:T(8,128)(2,1)S(1)} %collective-permute-done.4.refs_0_), channel_id=1, source_target_pairs={{0,1},{1,0},{2,3},{3,2},{4,5},{5,4},{6,7},{7,6},{8,9},{9,8},{10,11... | collective-permute-start | bytes 1105928 | tf_op jit(solution)/shard_map/ppermute | solution.py:446
  49.1 7.9 %collective-permute-start.18 = (bf16[80,2304]{1,0:T(8,128)(2,1)S(1)}, bf16[80,2304]{1,0:T(8,128)(2,1)}, u32[]{:S(2)}, u32[]{:S(2)}) collective-permute-start(bf16[80,2304]{1,0:T(8,128)(2,1)S(1)} %collective-permute-done.11.refs_3_), channel_id=1, source_target_pairs={{0,1},{1,0},{2,3},{3,2},{4,5},{5,4},{6,7},{7,6},{8,9},{9,8},{10,11... | collective-permute-start | bytes 1105928 | tf_op jit(solution)/shard_map/ppermute | solution.py:446
  52.2 8.2 %collective-permute-start.13 = (bf16[80,2304]{1,0:T(8,128)(2,1)}, bf16[80,2304]{1,0:T(8,128)(2,1)}, u32[]{:S(2)}, u32[]{:S(2)}) collective-permute-start(bf16[80,2304]{1,0:T(8,128)(2,1)} %collective-permute-done.10.refs_1_), channel_id=1, source_target_pairs={{0,2},{1,3},{2,0},{3,1},{4,6},{5,7},{6,4},{7,5},{8,10},{9,11},{10,... | collective-permute-start | bytes 1105928 | tf_op jit(solution)/shard_map/ppermute | solution.py:446
  53.3 0.6 copy-start.13
  54.0 8.3 %collective-permute-start.14 = (bf16[80,2304]{1,0:T(8,128)(2,1)}, bf16[80,2304]{1,0:T(8,128)(2,1)}, u32[]{:S(2)}, u32[]{:S(2)}) collective-permute-start(bf16[80,2304]{1,0:T(8,128)(2,1)} %collective-permute-done.10.refs_1_), channel_id=1, source_target_pairs={{0,4},{1,5},{2,6},{3,7},{4,0},{5,1},{6,2},{7,3},{8,12},{9,13},{10,... | collective-permute-start | bytes 1105928 | tf_op jit(solution)/shard_map/ppermute | solution.py:446
  56.3 6.9 %collective-permute-start.17 = (bf16[160,2304]{1,0:T(8,128)(2,1)S(1)}, bf16[160,2304]{1,0:T(8,128)(2,1)S(1)}, u32[]{:S(2)}, u32[]{:S(2)}) collective-permute-start(bf16[160,2304]{1,0:T(8,128)(2,1)S(1)} %collective-permute-done.5.refs_2_), channel_id=1, source_target_pairs={{0,1},{1,0},{2,3},{3,2},{4,5},{5,4},{6,7},{7,6},{8,9},{9,8},{10,11... | collective-permute-start | bytes 2211848 | tf_op jit(solution)/shard_map/ppermute | solution.py:446
  56.5 6.8 %collective-permute-start.19 = (bf16[80,2304]{1,0:T(8,128)(2,1)}, bf16[80,2304]{1,0:T(8,128)(2,1)S(1)}, u32[]{:S(2)}, u32[]{:S(2)}) collective-permute-start(bf16[80,2304]{1,0:T(8,128)(2,1)} %collective-permute-done.12.refs_4_), channel_id=1, source_target_pairs={{0,1},{1,0},{2,3},{3,2},{4,5},{5,4},{6,7},{7,6},{8,9},{9,8},{10,11... | collective-permute-start | bytes 1105928 | tf_op jit(solution)/shard_map/ppermute | solution.py:446
  57.0 6.2 %collective-permute-start.16 = (bf16[80,2304]{1,0:T(8,128)(2,1)}, bf16[80,2304]{1,0:T(8,128)(2,1)S(1)}, u32[]{:S(2)}, u32[]{:S(2)}) collective-permute-start(bf16[80,2304]{1,0:T(8,128)(2,1)} %collective-permute-done.10.refs_1_), channel_id=1, source_target_pairs={{0,1},{1,0},{2,3},{3,2},{4,5},{5,4},{6,7},{7,6},{8,9},{9,8},{10,11... | collective-permute-start | bytes 1105928 | tf_op jit(solution)/shard_map/ppermute | solution.py:446
  60.4 2.9 %collective-permute-start.20 = (bf16[80,2304]{1,0:T(8,128)(2,1)}, bf16[80,2304]{1,0:T(8,128)(2,1)S(1)}, u32[]{:S(2)}, u32[]{:S(2)}) collective-permute-start(bf16[80,2304]{1,0:T(8,128)(2,1)} %collective-permute-done.13.refs_5_), channel_id=1, source_target_pairs={{0,1},{1,0},{2,3},{3,2},{4,5},{5,4},{6,7},{7,6},{8,9},{9,8},{10,11... | collective-permute-start | bytes 1105928 | tf_op jit(solution)/shard_map/ppermute | solution.py:446
  62.3 1.9 %collective-permute-start.21 = (bf16[80,2304]{1,0:T(8,128)(2,1)}, bf16[80,2304]{1,0:T(8,128)(2,1)S(1)}, u32[]{:S(2)}, u32[]{:S(2)}) collective-permute-start(bf16[80,2304]{1,0:T(8,128)(2,1)} %collective-permute-done.14.refs_6_), channel_id=1, source_target_pairs={{0,1},{1,0},{2,3},{3,2},{4,5},{5,4},{6,7},{7,6},{8,9},{9,8},{10,11... | collective-permute-start | bytes 1105928 | tf_op jit(solution)/shard_map/ppermute | solution.py:446
  64.2 0.9 copy-start.4
  81.5 0.8 copy-start.2
  82.3 9.1 %collective-permute-start.22 = (bf16[128,1152]{1,0:T(8,128)(2,1)S(1)}, bf16[128,1152]{1,0:T(8,128)(2,1)S(1)}, u32[]{:S(2)}, u32[]{:S(2)}) collective-permute-start(bf16[128,1152]{1,0:T(8,128)(2,1)S(1)} %get-tuple-element.42), channel_id=1, source_target_pairs={{0,16},{16,0},{1,17},{17,1},{2,18},{18,2},{3,19},{19,3},{4,20},{20... | collective-permute-start | bytes 884744 | tf_op jit(solution)/shard_map/ppermute | solution.py:443
  91.4 0.7 copy-start.10

commit v4 on v3

--- a/solution.py
+++ b/solution.py
@@ -254,13 +254,10 @@
 
 def other_kernel(
     step, place, other, psi_ref, weight, degree_ref, own_ends, table,
-    part_any, phi_any, ends_ref, slab_any,
+    part_any, phi_any, ends_ref,
     part_ref, phi_ref, pairs, work, sems,
 ):
     x = place[0]
-    slab = pl.ds(pl.multiple_of(place[1], slab_any.shape[0]), slab_any.shape[0])
-    copies = [pltpu.make_async_copy(table.at[slab], slab_any, sems.at[0])]
-    copies[0].start()
 
     def values_of(i, span):
         return dot_nt(other[...], table[span, :]).astype(BF16), psi_ref[:, span]
@@ -277,20 +274,22 @@
     angular_density(
         step, x, values_of, store, table, weight, degree_ref, part_ref, ends_at, pairs, work
     )
-    copies.append(pltpu.make_async_copy(part_ref, part_any, sems.at[1]))
-    copies.append(pltpu.make_async_copy(phi_ref, phi_any, sems.at[2]))
-    for copy in copies[1:]:
+    copies = [
+        pltpu.make_async_copy(part_ref, part_any, sems.at[0]),
+        pltpu.make_async_copy(phi_ref, phi_any, sems.at[1]),
+    ]
+    for copy in copies:
         copy.start()
     for copy in copies:
         copy.wait()
 
 
 def finish_kernel(
-    step, pieces, place, own, other, cont, weight, far_weight, degree_ref, earlier, later,
+    step, pieces, place, own, other, cont, weight, degree_ref, earlier, later, arrived,
     part_any, other_part_any, phi_any, other_phi_any, table_hbm, *refs
 ):
     far_hbm = refs[:pieces]
-    send_any, keep_any, send_ref, keep_ref, part, table, far_table, rows, pairs, sorted_pairs, phi_all, pot, product, work, total, sems = refs[pieces:]
+    send_any, keep_any, far_weight, send_ref, keep_ref, part, table, far_table, rows, pairs, sorted_pairs, phi_all, pot, product, work, total, sems = refs[pieces:]
     x = place[0]
     points = own.shape[0]
     half = points // 2
@@ -326,6 +325,9 @@
         copy.start()
     fetch_table.start()
     rows[span_of(1 - x, half), :] = other[span_of(x, half), :]
+    far_weight[...] = jnp.zeros_like(far_weight)
+    for row in (2 * NP + 2, 2 * NP + 1, 2 * NP):
+        far_weight[...] += arrived[row : row + 1, :quad].astype(F32)
     for copy in fetch_rows():
         copy.wait()
     for n in range(pieces):
@@ -356,8 +358,9 @@
         factor = 4.0 * step / (2.0 * degree + 1.0)
         density = dot_nn(sorted_pairs[...], far_table[:, span]) + dot_nn(by_point, part[:, span])
         work[...] = density.reshape(half, NP, TILE)
-        ahead = earlier[:, span]
-        behind = later[:, span] * shrink_behind
+        came = arrived[:, span].astype(F32)
+        ahead = earlier[:, span] + came[:NP]
+        behind = (later[:, span] + came[NP : 2 * NP]) * shrink_behind
         for j in range(half):
             ahead = ahead * shrink_ahead + work[j]
             total[j] = ahead
@@ -461,13 +464,13 @@
     hbm = pl.BlockSpec(memory_space=pltpu.HBM)
     slabs = pl.pallas_call(
         slab_kernel,
-        out_shape=tuple(jax.ShapeDtypeStruct((n * size, channels), BF16) for n in (1, 2)),
+        out_shape=tuple(jax.ShapeDtypeStruct((n * size, channels), BF16) for n in (1, 1, 2)),
         in_specs=[SMEM_SPEC, hbm],
-        out_specs=(VMEM_SPEC,) * 2,
-        scratch_shapes=[pltpu.SemaphoreType.DMA((2,))],
+        out_specs=(VMEM_SPEC,) * 3,
+        scratch_shapes=[pltpu.SemaphoreType.DMA((3,))],
         name="slabs",
     )(
-        jnp.stack([offset(corner, core, 0), offset(corner ^ 3, core, 0)]),
+        jnp.stack([offset(corner, core, 0), offset(corner, core, 1), offset(corner ^ 3, core, 0)]),
         in_hbm(harmonic_table),
     )
 
@@ -481,7 +484,8 @@
 
     other = over_x(own)
     first_a = over_x(slabs[0])
-    last = over_x(slabs[1])
+    first_b = over_x(slabs[1])
+    last = over_x(slabs[2])
     part, phi, psi, own_ends, table = pl.pallas_call(
         functools.partial(own_kernel, step),
         out_shape=(
@@ -504,16 +508,15 @@
         compiler_params=pltpu.CompilerParams(vmem_limit_bytes=16 << 20),
         name="own_orbital",
     )(place, own, cont, weight, degree, in_hbm(after(harmonic_table, slabs[0])))
-    other_part, other_phi, ends, slab = pl.pallas_call(
+    other_part, other_phi, ends = pl.pallas_call(
         functools.partial(other_kernel, step),
         out_shape=(
             part_shape,
             phi_shape,
             jax.ShapeDtypeStruct((4 * NP, channels), F32),
-            jax.ShapeDtypeStruct((size, channels), BF16),
         ),
         in_specs=[SMEM_SPEC] + [VMEM_SPEC] * 6,
-        out_specs=(ANY_SPEC, ANY_SPEC, VMEM_SPEC, ANY_SPEC),
+        out_specs=(ANY_SPEC, ANY_SPEC, VMEM_SPEC),
         scratch_shapes=[
             pltpu.VMEM((NC * half, channels), BF16),
             pltpu.VMEM((half, quad), BF16),
@@ -541,6 +544,7 @@
     both = jnp.concatenate([block_end, block_start], axis=0)
     message = both.astype(BF16)
     first_a = after(first_a, message)
+    by_y_a, by_z_a = flip(first_a, 2), flip(first_a, 4)
     earlier = jnp.zeros((NP, channels), F32)
     later = jnp.zeros((NP, channels), F32)
     row_end = ahead_by(points * (3 - u)) * block_end
@@ -554,12 +558,12 @@
         later += jnp.where(before, 0.0, behind_by(points * distance)) * came[NP:]
         row_end += ahead_by(points * (3 - v)) * came[:NP]
         row_start += behind_by(points * v) * came[NP:]
-    row_end = after(row_end.astype(BF16), first_a, last)
-    row_start = after(row_start.astype(BF16), first_a, last)
-    first_b = over_x(after(slab, row_end))
+    row_end = after(row_end.astype(BF16), first_a, first_b)
+    row_start = after(row_start.astype(BF16), first_a, first_b)
     for shift in (1, 2, 3):
         message = jnp.where(z + shift < 4, row_end, row_start)
         came = lax.ppermute(message, "grid", [(n, (n + 4 * shift) % 16) for n in everyone])
+        came = after(came, by_y_a, by_z_a, last)
         came = came.astype(F32)
         source = (z - shift) % 4
         before = source < z
@@ -578,13 +582,12 @@
     terms = jnp.pad(jnp.concatenate(terms, axis=0), ((0, NP - 3), (0, channels - quad)))
     theirs = jnp.concatenate([theirs, terms], axis=0)
     theirs = theirs.astype(BF16)
-    came = over_x(theirs).astype(F32)
-    far_weight = jnp.sum(came[2 * NP : 2 * NP + 3, :quad], axis=0, keepdims=True)
-    earlier = jnp.where(x == 0, earlier, upper_earlier) + came[:NP]
-    later = jnp.where(x == 0, lower_later, later) + came[NP : 2 * NP]
-    first_b = after(first_b, theirs)
+    arrived = over_x(theirs)
+    earlier = jnp.where(x == 0, earlier, upper_earlier)
+    later = jnp.where(x == 0, lower_later, later)
+    first_b = after(first_b, row_end)
     received = [first_a, first_b, last]
-    received += [flip(first_a, 2), flip(first_a, 4), flip(first_b, 2), flip(first_b, 4)]
+    received += [by_y_a, by_z_a, flip(first_b, 2), flip(first_b, 4)]
     which = [(corner, 0), (corner, 1), (corner ^ 3, 0)]
     which += [(corner ^ 1, 0), (corner ^ 2, 0), (corner ^ 1, 1), (corner ^ 2, 1)]
     far = received + [flip(value, 1) for value in received]
@@ -597,9 +600,10 @@
             jax.ShapeDtypeStruct((NC * half, channels // 2), BF16),
             jax.ShapeDtypeStruct((NC * half, channels // 2), F32),
         ),
-        in_specs=[SMEM_SPEC, hbm, VMEM_SPEC, hbm] + [VMEM_SPEC] * 5 + [ANY_SPEC] * 4 + [hbm] + [HBM_SPEC] * pieces,
+        in_specs=[SMEM_SPEC, hbm, VMEM_SPEC, hbm] + [VMEM_SPEC] * 5 + [hbm] * 5 + [ANY_SPEC] * pieces,
         out_specs=(ANY_SPEC,) * 2,
         scratch_shapes=[
+            pltpu.VMEM((1, quad), F32),
             pltpu.VMEM((NC * half, channels // 2), BF16),
             pltpu.VMEM((NC * half, channels // 2), F32),
             pltpu.VMEM((NP * half, channels), BF16),
@@ -618,8 +622,8 @@
         compiler_params=pltpu.CompilerParams(vmem_limit_bytes=30 << 20),
         name="finish",
     )(
-        places, in_hbm(own), other, in_hbm(cont), weight, far_weight, degree, earlier, later,
-        part, other_part, phi, other_phi, in_hbm(harmonic_table), *far,
+        places, in_hbm(own), other, in_hbm(cont), weight, degree, earlier, later, arrived,
+        in_hbm(part), in_hbm(other_part), in_hbm(phi), in_hbm(other_phi), in_hbm(harmonic_table), *far,
     )
     came = over_x(send)
     out = pl.pallas_call(

time: 95 us -> 90.6 us (0.954)
  other arithmetic: 11.9 us -> 8.6 us
  starting transfers between devices: 21.2 us -> 18 us
  local copies, waits for them, and re-layouts: 3.84 us -> 5.22 us
    ppermute x3, waiting for transfers between devices: 0.01 us -> 7.02 us  [shards_by_table(): lax.ppermute(message, 'grid', [(n, (n + 4 * shift) % 16) for n in everyone])]
    ppermute x14, waiting for transfers between devices: 9.41 us -> 5.51 us  [flip(): return lax.ppermute(value, 'grid', [(n, n ^ bits) for n in everyone])]
    ppermute x3, starting transfers between devices: 5.76 us -> 2.67 us  [shards_by_table(): lax.ppermute(message, 'grid', [(n, (n + 4 * shift) % 16) for n in everyone])]
    ppermute x6, waiting for transfers between devices: 12.7 us -> 10.4 us  [over_x(): return lax.ppermute(value, 'orb', across)]
    ppermute x6, starting transfers between devices: 8.69 us -> 6.33 us  [over_x(): return lax.ppermute(value, 'orb', across)]
    ppermute x14, starting transfers between devices: 6.7 us -> 8.97 us  [flip(): return lax.ppermute(value, 'grid', [(n, n ^ bits) for n in everyone])]
    convert_element_type x3, other arithmetic: 1.8 us -> 0.04 us  [shards_by_table(): came = flip(message, bits).astype(F32)]
    concatenate x1, other arithmetic: 0.01 us -> 1.42 us  [shards_by_table(): theirs = jnp.concatenate([theirs, terms], axis=0)]
  transfers between devices with their start and end apart: 23 -> 23, of which waited for: 10 -> 10; matrix products, arithmetic and copies ran while one was open for 12% -> 10% of each run, Pallas kernels for 17% -> 18%
where the time goes in v4:
time: 90.6 us; the launch traced here: 90 us
  Pallas kernels  35 us (39%)
  waiting for transfers between devices  22.9 us (25%)
  starting transfers between devices  18 us (20%)
  other arithmetic  8.6 us (9%)
  local copies, waits for them, and re-layouts  5.22 us (6%)
    pallas_call x1, Pallas kernels, shards_by_table(): pl.pallas_call(functools.partial(finish_kernel, step, pieces), out_shape=...  16.4 us
    ppermute x6, waiting for transfers between devices, over_x(): return lax.ppermute(value, 'orb', across)  10.4 us
    ppermute x14, starting transfers between devices, flip(): return lax.ppermute(value, 'grid', [(n, n ^ bits) for n in everyone])  8.97 us
    pallas_call x1, Pallas kernels, shards_by_table(): pl.pallas_call(functools.partial(own_kernel, step), out_shape=(part_shape...  7.37 us
    ppermute x3, waiting for transfers between devices, shards_by_table(): lax.ppermute(message, 'grid', [(n, (n + 4 * shift) % 16) for n in everyone])  7.02 us
    ppermute x6, starting transfers between devices, over_x(): return lax.ppermute(value, 'orb', across)  6.33 us
    pallas_call x1, Pallas kernels, shards_by_table(): pl.pallas_call(functools.partial(other_kernel, step), out_shape=(part_sha...  5.85 us
    ppermute x14, waiting for transfers between devices, flip(): return lax.ppermute(value, 'grid', [(n, n ^ bits) for n in everyone])  5.51 us
  transfers between devices with their start and end apart: 23, of which 10 were waited for; matrix products, arithmetic and copies ran while one was open for 10% of the time, Pallas kernels for 18%

profile of v4, /device:TPU:0, one launch (start us, length us, event | category | flops | bytes accessed | tf_op | source)
XLA Modules:
  0.0 90.0 jit_solution(4829875133961795804)
XLA Ops:
  0.0 3.0 %collective-permute-start = (bf16[64,2304]{1,0:T(8,128)(2,1)}, bf16[64,2304]{1,0:T(8,128)(2,1)S(1)}, u32[]{:S(2)}, u32[]{:S(2)}) collective-permute-start(bf16[64,2304]{1,0:T(8,128)(2,1)} %bitcast.20), channel_id=1, source_target_pairs={{0,16},{16,0},{1,17},{17,1},{2,18},{18,2},{3,19},{19,3},{4,20},{20... | collective-permute-start | bytes 884744 | tf_op jit(solution)/shard_map/ppermute | solution.py:446
  3.0 0.6 pad_add_fusion.1.place
  3.6 3.1 %slabs.1 = (bf16[80,2304]{1,0:T(8,128)(2,1)}, bf16[80,2304]{1,0:T(8,128)(2,1)}, bf16[160,2304]{1,0:T(8,128)(2,1)}) custom-call(s32[3]{0:T(128)} %pad_add_fusion.1.place, bf16[1280,2304]{1,0:T(8,128)(2,1)} %table_hbm.2), custom_call_target="tpu_custom_call" | custom-call | tf_op jit(solution)/shard_map/slabs/pallas_call | solution.py:465
  6.8 0.1 collective-permute-start.4
  6.9 1.9 %collective-permute-start.5 = (bf16[80,2304]{1,0:T(8,128)(2,1)}, bf16[80,2304]{1,0:T(8,128)(2,1)S(1)}, u32[]{:S(2)}, u32[]{:S(2)}) collective-permute-start(bf16[80,2304]{1,0:T(8,128)(2,1)} %get-tuple-element.33), channel_id=1, source_target_pairs={{0,16},{16,0},{1,17},{17,1},{2,18},{18,2},{3,19},{19,3},{4,20},{20... | collective-permute-start | bytes 1105928 | tf_op jit(solution)/shard_map/ppermute | solution.py:446
  8.9 0.1 convert_reduce_fusion
  9.1 0.1 pad_add_fusion.place
  9.2 7.4 %own_orbital.1 = (bf16[128,2304]{1,0:T(8,128)(2,1)S(1)}, bf16[32,1280]{1,0:T(8,128)(2,1)S(1)}, bf16[256,1280]{1,0:T(8,128)(2,1)S(1)}, f32[16,2304]{1,0:T(8,128)S(1)}, bf16[1280,2304]{1,0:T(8,128)(2,1)S(1)}) custom-call(s32[2]{0:T(128)S(1)} %pad_add_fusion.place, bf16[64,2304]{1,0:T(8,128)(2,1)S(1)} %bitcast.22, bf16[256,2304]{1,0:T(8,128)(2,1)S(1)} %bitcast.19, ...), custom_call_target="tpu_custom_call" | custom-call | tf_op jit(solution)/shard_map/own_orbital/pallas_call | solution.py:489
  16.6 0.9 exponential_select_fusion.5
  17.5 0.0 collective-permute-done.other
  17.5 5.8 %other_orbital.1 = (bf16[128,2304]{1,0:T(8,128)(2,1)S(1)}, bf16[32,1280]{1,0:T(8,128)(2,1)S(1)}, f32[32,2304]{1,0:T(8,128)S(1)}) custom-call(s32[2]{0:T(128)S(1)} %pad_add_fusion.place, bf16[64,2304]{1,0:T(8,128)(2,1)S(1)} %collective-permute-done.other, bf16[256,1280]{1,0:T(8,128)(2,1)S(1)} %get-tuple-element.28.psi_ref, ...), custom_call_target="tpu_custom_call" | custom-call | tf_op jit(solution)/shard_map/other_orbital/pallas_call | solution.py:511
  23.4 0.8 copy-done.3
  24.2 0.2 collective-permute-start.3
  24.4 1.5 %collective-permute-start.2 = (bf16[16,2304]{1,0:T(8,128)(2,1)S(1)}, bf16[16,2304]{1,0:T(8,128)(2,1)S(1)}, u32[]{:S(2)}, u32[]{:S(2)}) collective-permute-start(bf16[16,2304]{1,0:T(8,128)(2,1)S(1)} %pad_maximum_fusion.1), channel_id=1, source_target_pairs={{0,2},{1,3},{2,0},{3,1},{4,6},{5,7},{6,4},{7,5},{8,10},{9,11},{10,... | collective-permute-start | bytes 221192 | tf_op jit(solution)/shard_map/ppermute | solution.py:449
  25.9 0.3 collective-permute-start.1
  26.2 0.6 exponential_select_fusion.2
  26.8 0.3 collective-permute-start.9
  27.1 1.7 %collective-permute-done.3 = bf16[16,2304]{1,0:T(8,128)(2,1)S(1)} collective-permute-done((bf16[16,2304]{1,0:T(8,128)(2,1)S(1)}, bf16[16,2304]{1,0:T(8,128)(2,1)S(1)}, u32[]{:S(2)}, u32[]{:S(2)}) %collective-permute-start.3) | collective-permute-done | bytes 73760 | tf_op jit(solution)/shard_map/ppermute | solution.py:449
  28.8 1.0 %collective-permute-start.7 = (bf16[80,2304]{1,0:T(8,128)(2,1)S(1)}, bf16[80,2304]{1,0:T(8,128)(2,1)S(1)}, u32[]{:S(2)}, u32[]{:S(2)}) collective-permute-start(bf16[80,2304]{1,0:T(8,128)(2,1)S(1)} %collective-permute-done.4.refs_0_), channel_id=1, source_target_pairs={{0,2},{1,3},{2,0},{3,1},{4,6},{5,7},{6,4},{7,5},{8,10},{9,11},{10,... | collective-permute-start | bytes 1105928 | tf_op jit(solution)/shard_map/ppermute | solution.py:449
  29.8 0.6 collective-permute-done.2
  30.5 1.6 %collective-permute-start.8 = (bf16[80,2304]{1,0:T(8,128)(2,1)S(1)}, bf16[80,2304]{1,0:T(8,128)(2,1)S(1)}, u32[]{:S(2)}, u32[]{:S(2)}) collective-permute-start(bf16[80,2304]{1,0:T(8,128)(2,1)S(1)} %collective-permute-done.4.refs_0_), channel_id=1, source_target_pairs={{0,4},{1,5},{2,6},{3,7},{4,0},{5,1},{6,2},{7,3},{8,12},{9,13},{10,... | collective-permute-start | bytes 1105928 | tf_op jit(solution)/shard_map/ppermute | solution.py:449
  32.1 0.8 add_convert_fusion.1
  32.9 0.0 collective-permute-done.5.refs_1_
  32.9 0.8 add_convert_fusion
  33.7 0.6 broadcast_select_fusion.2
  34.4 2.5 %collective-permute-start.11 = (bf16[8,2304]{1,0:T(8,128)(2,1)S(1)}, bf16[8,2304]{1,0:T(8,128)(2,1)S(1)}, u32[]{:S(2)}, u32[]{:S(2)}) collective-permute-start(bf16[8,2304]{1,0:T(8,128)(2,1)S(1)} %get-tuple-element.55), channel_id=1, source_target_pairs={{0,12},{1,13},{2,14},{3,15},{4,0},{5,1},{6,2},{7,3},{8,4},{9,5},{1... | collective-permute-start | bytes 110600 | tf_op jit(solution)/shard_map/ppermute | solution.py:565
  36.9 0.2 collective-permute-start.10
  37.1 5.5 %collective-permute-done.11 = bf16[8,2304]{1,0:T(8,128)(2,1)S(1)} collective-permute-done((bf16[8,2304]{1,0:T(8,128)(2,1)S(1)}, bf16[8,2304]{1,0:T(8,128)(2,1)S(1)}, u32[]{:S(2)}, u32[]{:S(2)}) %collective-permute-start.11) | collective-permute-done | bytes 36896 | tf_op jit(solution)/shard_map/ppermute | solution.py:565
  42.6 0.6 fusion.16
  43.2 0.0 collective-permute-done.7.refs_3_
  43.2 0.6 collective-permute-start.13
  43.8 0.0 collective-permute-done.8.refs_4_
  43.9 2.7 %collective-permute-start.14 = (bf16[80,2304]{1,0:T(8,128)(2,1)S(1)}, bf16[80,2304]{1,0:T(8,128)(2,1)}, u32[]{:S(2)}, u32[]{:S(2)}) collective-permute-start(bf16[80,2304]{1,0:T(8,128)(2,1)S(1)} %collective-permute-done.5.refs_1_), channel_id=1, source_target_pairs={{0,4},{1,5},{2,6},{3,7},{4,0},{5,1},{6,2},{7,3},{8,12},{9,13},{10,... | collective-permute-start | bytes 1105928 | tf_op jit(solution)/shard_map/ppermute | solution.py:449
  46.6 0.0 collective-permute-done.10
  46.6 0.0 copy-start.14
  46.6 0.5 collective-permute-start.16
  47.1 1.5 %collective-permute-done.6 = bf16[8,2304]{1,0:T(8,128)(2,1)S(1)} collective-permute-done((bf16[8,2304]{1,0:T(8,128)(2,1)S(1)}, bf16[8,2304]{1,0:T(8,128)(2,1)S(1)}, u32[]{:S(2)}, u32[]{:S(2)}) %collective-permute-start.6) | collective-permute-done | bytes 36896 | tf_op jit(solution)/shard_map/ppermute | solution.py:565
  48.6 0.9 select_convert_fusion
  49.6 0.9 %select_convert_fusion.1 = (bf16[8,2304]{1,0:T(8,128)(2,1)S(1)}, f32[8,2304]{1,0:T(8,128)S(1)}, f32[8,2304]{1,0:T(8,128)S(1)}) fusion(f32[32,2304]{1,0:T(8,128)S(1)} %get-tuple-element.31, f32[2304]{0:T(1024)S(1)} %get-tuple-element.58, pred[]{:T(512)S(6)} %eq.14, bf16[8,2304]{1,0:T(8,128)(2,1)} %copy-done.13, f32[2304]{0:T(1024)} %get-tuple-element.67, ...), kind=kLoop, calls=%fused_computation.22 | loop fusion | flops 387072 | bytes 811009 | tf_op jit(solution)/shard_map/convert
  50.5 1.4 %pad_maximum_fusion = bf16[24,2304]{1,0:T(8,128)(2,1)} fusion(bf16[8,2304]{1,0:T(8,128)(2,1)} %fusion.16, bf16[8,2304]{1,0:T(8,128)(2,1)S(1)} %get-tuple-element.49, bf16[8,2304]{1,0:T(8,128)(2,1)S(1)} %get-tuple-element.47), kind=kLoop, calls=%fused_computation.1 | loop fusion | flops 331776 | bytes 221184 | tf_op jit(solution)/shard_map/concatenate | solution.py:583
  51.9 0.5 collective-permute-start.12
  52.4 0.1 collective-permute-done.13.refs_5_
  52.5 0.7 copy-done.7
  53.2 0.0 collective-permute-start.17
  53.2 0.1 stack.75.place
  53.3 1.2 %collective-permute-done.14.refs_6_ = bf16[80,2304]{1,0:T(8,128)(2,1)} collective-permute-done((bf16[80,2304]{1,0:T(8,128)(2,1)S(1)}, bf16[80,2304]{1,0:T(8,128)(2,1)}, u32[]{:S(2)}, u32[]{:S(2)}) %collective-permute-start.14) | collective-permute-done | bytes 368672 | tf_op jit(solution)/shard_map/ppermute | solution.py:449
  54.5 0.5 collective-permute-start.19
  55.1 0.0 collective-permute-done.16.refs_8_
  55.1 0.1 collective-permute-start.20
  55.1 1.8 %collective-permute-done.12.arrived = bf16[24,2304]{1,0:T(8,128)(2,1)S(1)} collective-permute-done((bf16[24,2304]{1,0:T(8,128)(2,1)}, bf16[24,2304]{1,0:T(8,128)(2,1)S(1)}, u32[]{:S(2)}, u32[]{:S(2)}) %collective-permute-start.12) | collective-permute-done | bytes 110624 | tf_op jit(solution)/shard_map/ppermute | solution.py:446
  56.9 0.0 collective-permute-start.21
  56.9 0.0 collective-permute-done.18.refs_10_
  56.9 0.0 collective-permute-done.19.refs_11_
  57.0 0.5 collective-permute-done.20.refs_12_
  57.5 1.3 %collective-permute-done.21.refs_13_ = bf16[80,2304]{1,0:T(8,128)(2,1)S(1)} collective-permute-done((bf16[80,2304]{1,0:T(8,128)(2,1)}, bf16[80,2304]{1,0:T(8,128)(2,1)S(1)}, u32[]{:S(2)}, u32[]{:S(2)}) %collective-permute-start.21) | collective-permute-done | bytes 368672 | tf_op jit(solution)/shard_map/ppermute | solution.py:449
  58.8 0.0 collective-permute-done.17.refs_9_
  58.8 1.0 %copy-done.6 = bf16[80,2304]{1,0:T(8,128)(2,1)S(1)} copy-done((bf16[80,2304]{1,0:T(8,128)(2,1)S(1)}, bf16[80,2304]{1,0:T(8,128)(2,1)}, u32[]{:S(2)}) %copy-start.6) | copy-done | bytes 368664
  59.8 1.0 %copy-done.8 = bf16[80,2304]{1,0:T(8,128)(2,1)S(1)} copy-done((bf16[80,2304]{1,0:T(8,128)(2,1)S(1)}, bf16[80,2304]{1,0:T(8,128)(2,1)}, u32[]{:S(2)}) %copy-start.8) | copy-done | bytes 368664
  60.8 16.4 %finish.1 = (bf16[128,1152]{1,0:T(8,128)(2,1)S(1)}, f32[128,1152]{1,0:T(8,128)S(1)}) custom-call(s32[15]{0:T(128)S(1)} %stack.75.place, bf16[64,2304]{1,0:T(8,128)(2,1)} %bitcast.21, bf16[64,2304]{1,0:T(8,128)(2,1)S(1)} %collective-permute-done.other, bf16[256,2304]{1,0:T(8,128)(2,1)} %bitcast.18, f32[1,1280]{1,0:T(1,128)S(1)} %broadcast_in_dim.24.weight, ...), custom_call_target="tpu_custom_call" | custom-call | tf_op jit(solution)/shard_map/finish/pallas_call | solution.py:597
  77.2 0.8 copy-done.4
  78.0 0.5 collective-permute-start.22
  78.4 8.6 %collective-permute-done.22.came = bf16[128,1152]{1,0:T(8,128)(2,1)S(1)} collective-permute-done((bf16[128,1152]{1,0:T(8,128)(2,1)S(1)}, bf16[128,1152]{1,0:T(8,128)(2,1)S(1)}, u32[]{:S(2)}, u32[]{:S(2)}) %collective-permute-start.22) | collective-permute-done | bytes 294944 | tf_op jit(solution)/shard_map/ppermute | solution.py:446
  87.0 0.7 copy-done.12
  87.8 2.2 %place.1 = f32[4,64,1152]{2,1,0:T(8,128)} custom-call(s32[2]{0:T(128)} %copy-done.11, f32[128,1152]{1,0:T(8,128)} %copy-done.4, bf16[128,1152]{1,0:T(8,128)(2,1)} %copy-done.12), custom_call_target="tpu_custom_call" | custom-call | tf_op jit(solution)/shard_map/place/pallas_call | solution.py:629
  (49 shorter events, 0.2 us)
Async XLA Ops:
  0.0 9.2 %copy-start.1 = (bf16[1,64,2304]{2,1,0:T(8,128)(2,1)S(1)}, bf16[1,64,2304]{2,1,0:T(8,128)(2,1)}, u32[]{:S(2)}) copy-start(bf16[1,64,2304]{2,1,0:T(8,128)(2,1)} %param.5) | copy-start | bytes 884740
  0.0 8.9 %copy-start.16 = (f32[1280]{0:T(1024)S(1)}, f32[1280]{0:T(1024)}, u32[]{:S(2)}) copy-start(f32[1280]{0:T(1024)} %param.8) | copy-start | bytes 15364
  0.0 8.9 %copy-start.17 = (s32[2304]{0:T(1024)S(1)}, s32[2304]{0:T(1024)}, u32[]{:S(2)}) copy-start(s32[2304]{0:T(1024)} %param.9) | copy-start | bytes 27652
  0.0 9.2 %copy-start = (bf16[4,64,2304]{2,1,0:T(8,128)(2,1)S(1)}, bf16[4,64,2304]{2,1,0:T(8,128)(2,1)}, u32[]{:S(2)}) copy-start(bf16[4,64,2304]{2,1,0:T(8,128)(2,1)} %param.6) | copy-start | bytes 3538948
  0.0 17.5 %collective-permute-start = (bf16[64,2304]{1,0:T(8,128)(2,1)}, bf16[64,2304]{1,0:T(8,128)(2,1)S(1)}, u32[]{:S(2)}, u32[]{:S(2)}) collective-permute-start(bf16[64,2304]{1,0:T(8,128)(2,1)} %bitcast.20), channel_id=1, source_target_pairs={{0,16},{16,0},{1,17},{17,1},{2,18},{18,2},{3,19},{19,3},{4,20},{20... | collective-permute-start | bytes 884744 | tf_op jit(solution)/shard_map/ppermute | solution.py:446
  6.8 20.0 %collective-permute-start.4 = (bf16[80,2304]{1,0:T(8,128)(2,1)}, bf16[80,2304]{1,0:T(8,128)(2,1)S(1)}, u32[]{:S(2)}, u32[]{:S(2)}) collective-permute-start(bf16[80,2304]{1,0:T(8,128)(2,1)} %get-tuple-element.26), channel_id=1, source_target_pairs={{0,16},{16,0},{1,17},{17,1},{2,18},{18,2},{3,19},{19,3},{4,20},{20... | collective-permute-start | bytes 1105928 | tf_op jit(solution)/shard_map/ppermute | solution.py:446
  6.9 26.0 %collective-permute-start.5 = (bf16[80,2304]{1,0:T(8,128)(2,1)}, bf16[80,2304]{1,0:T(8,128)(2,1)S(1)}, u32[]{:S(2)}, u32[]{:S(2)}) collective-permute-start(bf16[80,2304]{1,0:T(8,128)(2,1)} %get-tuple-element.33), channel_id=1, source_target_pairs={{0,16},{16,0},{1,17},{17,1},{2,18},{18,2},{3,19},{19,3},{4,20},{20... | collective-permute-start | bytes 1105928 | tf_op jit(solution)/shard_map/ppermute | solution.py:446
  9.2 14.1 %copy-start.11 = (s32[2]{0:T(128)}, s32[2]{0:T(128)S(1)}, u32[]{:S(2)}) copy-start(s32[2]{0:T(128)S(1)} %pad_add_fusion.place) | copy-start | bytes 28
  16.6 6.8 %copy-start.2 = (bf16[128,2304]{1,0:T(8,128)(2,1)}, bf16[128,2304]{1,0:T(8,128)(2,1)S(1)}, u32[]{:S(2)}) copy-start(bf16[128,2304]{1,0:T(8,128)(2,1)S(1)} %get-tuple-element.40.part_any) | copy-start | bytes 1769476
  16.6 7.6 %copy-start.9 = (bf16[32,1280]{1,0:T(8,128)(2,1)}, bf16[32,1280]{1,0:T(8,128)(2,1)S(1)}, u32[]{:S(2)}) copy-start(bf16[32,1280]{1,0:T(8,128)(2,1)S(1)} %get-tuple-element.42.phi_any) | copy-start | bytes 245764
  23.4 0.8 copy-start.3
  24.2 26.3 %copy-start.10 = (bf16[32,1280]{1,0:T(8,128)(2,1)}, bf16[32,1280]{1,0:T(8,128)(2,1)S(1)}, u32[]{:S(2)}) copy-start(bf16[32,1280]{1,0:T(8,128)(2,1)S(1)} %get-tuple-element.43.other_phi_any) | copy-start | bytes 245764
  24.2 4.6 %collective-permute-start.3 = (bf16[16,2304]{1,0:T(8,128)(2,1)S(1)}, bf16[16,2304]{1,0:T(8,128)(2,1)S(1)}, u32[]{:S(2)}, u32[]{:S(2)}) collective-permute-start(bf16[16,2304]{1,0:T(8,128)(2,1)S(1)} %pad_maximum_fusion.1), channel_id=1, source_target_pairs={{0,3},{1,2},{2,1},{3,0},{4,7},{5,6},{6,5},{7,4},{8,11},{9,10},{10,... | collective-permute-start | bytes 221192 | tf_op jit(solution)/shard_map/ppermute | solution.py:449
  24.4 6.0 %collective-permute-start.2 = (bf16[16,2304]{1,0:T(8,128)(2,1)S(1)}, bf16[16,2304]{1,0:T(8,128)(2,1)S(1)}, u32[]{:S(2)}, u32[]{:S(2)}) collective-permute-start(bf16[16,2304]{1,0:T(8,128)(2,1)S(1)} %pad_maximum_fusion.1), channel_id=1, source_target_pairs={{0,2},{1,3},{2,0},{3,1},{4,6},{5,7},{6,4},{7,5},{8,10},{9,11},{10,... | collective-permute-start | bytes 221192 | tf_op jit(solution)/shard_map/ppermute | solution.py:449
  25.9 6.1 %collective-permute-start.1 = (bf16[16,2304]{1,0:T(8,128)(2,1)S(1)}, bf16[16,2304]{1,0:T(8,128)(2,1)S(1)}, u32[]{:S(2)}, u32[]{:S(2)}) collective-permute-start(bf16[16,2304]{1,0:T(8,128)(2,1)S(1)} %pad_maximum_fusion.1), channel_id=1, source_target_pairs={{0,1},{1,0},{2,3},{3,2},{4,5},{5,4},{6,7},{7,6},{8,9},{9,8},{10,11... | collective-permute-start | bytes 221192 | tf_op jit(solution)/shard_map/ppermute | solution.py:449
  26.8 19.8 %collective-permute-start.9 = (bf16[160,2304]{1,0:T(8,128)(2,1)}, bf16[160,2304]{1,0:T(8,128)(2,1)S(1)}, u32[]{:S(2)}, u32[]{:S(2)}) collective-permute-start(bf16[160,2304]{1,0:T(8,128)(2,1)} %get-tuple-element.36), channel_id=1, source_target_pairs={{0,16},{16,0},{1,17},{17,1},{2,18},{18,2},{3,19},{19,3},{4,20},{20... | collective-permute-start | bytes 2211848 | tf_op jit(solution)/shard_map/ppermute | solution.py:446
  28.8 14.4 %collective-permute-start.7 = (bf16[80,2304]{1,0:T(8,128)(2,1)S(1)}, bf16[80,2304]{1,0:T(8,128)(2,1)S(1)}, u32[]{:S(2)}, u32[]{:S(2)}) collective-permute-start(bf16[80,2304]{1,0:T(8,128)(2,1)S(1)} %collective-permute-done.4.refs_0_), channel_id=1, source_target_pairs={{0,2},{1,3},{2,0},{3,1},{4,6},{5,7},{6,4},{7,5},{8,10},{9,11},{10,... | collective-permute-start | bytes 1105928 | tf_op jit(solution)/shard_map/ppermute | solution.py:449
  30.5 13.4 %collective-permute-start.8 = (bf16[80,2304]{1,0:T(8,128)(2,1)S(1)}, bf16[80,2304]{1,0:T(8,128)(2,1)S(1)}, u32[]{:S(2)}, u32[]{:S(2)}) collective-permute-start(bf16[80,2304]{1,0:T(8,128)(2,1)S(1)} %collective-permute-done.4.refs_0_), channel_id=1, source_target_pairs={{0,4},{1,5},{2,6},{3,7},{4,0},{5,1},{6,2},{7,3},{8,12},{9,13},{10,... | collective-permute-start | bytes 1105928 | tf_op jit(solution)/shard_map/ppermute | solution.py:449
  34.4 8.2 %collective-permute-start.11 = (bf16[8,2304]{1,0:T(8,128)(2,1)S(1)}, bf16[8,2304]{1,0:T(8,128)(2,1)S(1)}, u32[]{:S(2)}, u32[]{:S(2)}) collective-permute-start(bf16[8,2304]{1,0:T(8,128)(2,1)S(1)} %get-tuple-element.55), channel_id=1, source_target_pairs={{0,12},{1,13},{2,14},{3,15},{4,0},{5,1},{6,2},{7,3},{8,4},{9,5},{1... | collective-permute-start | bytes 110600 | tf_op jit(solution)/shard_map/ppermute | solution.py:565
  36.9 9.7 %collective-permute-start.10 = (bf16[8,2304]{1,0:T(8,128)(2,1)}, bf16[8,2304]{1,0:T(8,128)(2,1)S(1)}, u32[]{:S(2)}, u32[]{:S(2)}) collective-permute-start(bf16[8,2304]{1,0:T(8,128)(2,1)} %get-tuple-element.56), channel_id=1, source_target_pairs={{0,8},{1,9},{2,10},{3,11},{4,12},{5,13},{6,14},{7,15},{8,0},{9,1},... | collective-permute-start | bytes 110600 | tf_op jit(solution)/shard_map/ppermute | solution.py:565
  42.6 7.0 %copy-start.13 = (bf16[8,2304]{1,0:T(8,128)(2,1)}, bf16[8,2304]{1,0:T(8,128)(2,1)S(1)}, u32[]{:S(2)}) copy-start(bf16[8,2304]{1,0:T(8,128)(2,1)S(1)} %collective-permute-done.11) | copy-start | bytes 110596
  42.6 6.1 %collective-permute-start.6 = (bf16[8,2304]{1,0:T(8,128)(2,1)S(1)}, bf16[8,2304]{1,0:T(8,128)(2,1)S(1)}, u32[]{:S(2)}, u32[]{:S(2)}) collective-permute-start(bf16[8,2304]{1,0:T(8,128)(2,1)S(1)} %get-tuple-element.54), channel_id=1, source_target_pairs={{0,4},{1,5},{2,6},{3,7},{4,8},{5,9},{6,10},{7,11},{8,12},{9,13},{1... | collective-permute-start | bytes 110600 | tf_op jit(solution)/shard_map/ppermute | solution.py:565
  43.2 9.3 %collective-permute-start.13 = (bf16[80,2304]{1,0:T(8,128)(2,1)S(1)}, bf16[80,2304]{1,0:T(8,128)(2,1)S(1)}, u32[]{:S(2)}, u32[]{:S(2)}) collective-permute-start(bf16[80,2304]{1,0:T(8,128)(2,1)S(1)} %collective-permute-done.5.refs_1_), channel_id=1, source_target_pairs={{0,2},{1,3},{2,0},{3,1},{4,6},{5,7},{6,4},{7,5},{8,10},{9,11},{10,... | collective-permute-start | bytes 1105928 | tf_op jit(solution)/shard_map/ppermute | solution.py:449
  43.9 8.5 %copy-start.5 = (bf16[80,2304]{1,0:T(8,128)(2,1)}, bf16[80,2304]{1,0:T(8,128)(2,1)S(1)}, u32[]{:S(2)}) copy-start(bf16[80,2304]{1,0:T(8,128)(2,1)S(1)} %collective-permute-done.8.refs_4_) | copy-start | bytes 1105924
  43.9 10.7 %collective-permute-start.14 = (bf16[80,2304]{1,0:T(8,128)(2,1)S(1)}, bf16[80,2304]{1,0:T(8,128)(2,1)}, u32[]{:S(2)}, u32[]{:S(2)}) collective-permute-start(bf16[80,2304]{1,0:T(8,128)(2,1)S(1)} %collective-permute-done.5.refs_1_), channel_id=1, source_target_pairs={{0,4},{1,5},{2,6},{3,7},{4,0},{5,1},{6,2},{7,3},{8,12},{9,13},{10,... | collective-permute-start | bytes 1105928 | tf_op jit(solution)/shard_map/ppermute | solution.py:449
  46.6 7.9 %collective-permute-start.15 = (bf16[80,2304]{1,0:T(8,128)(2,1)S(1)}, bf16[80,2304]{1,0:T(8,128)(2,1)}, u32[]{:S(2)}, u32[]{:S(2)}) collective-permute-start(bf16[80,2304]{1,0:T(8,128)(2,1)S(1)} %collective-permute-done.4.refs_0_), channel_id=1, source_target_pairs={{0,1},{1,0},{2,3},{3,2},{4,5},{5,4},{6,7},{7,6},{8,9},{9,8},{10,11... | collective-permute-start | bytes 1105928 | tf_op jit(solution)/shard_map/ppermute | solution.py:449
  46.6 2.9 %copy-start.14 = (bf16[8,2304]{1,0:T(8,128)(2,1)}, bf16[8,2304]{1,0:T(8,128)(2,1)S(1)}, u32[]{:S(2)}) copy-start(bf16[8,2304]{1,0:T(8,128)(2,1)S(1)} %collective-permute-done.10) | copy-start | bytes 110596
  46.6 8.4 %collective-permute-start.16 = (bf16[80,2304]{1,0:T(8,128)(2,1)S(1)}, bf16[80,2304]{1,0:T(8,128)(2,1)}, u32[]{:S(2)}, u32[]{:S(2)}) collective-permute-start(bf16[80,2304]{1,0:T(8,128)(2,1)S(1)} %collective-permute-done.5.refs_1_), channel_id=1, source_target_pairs={{0,1},{1,0},{2,3},{3,2},{4,5},{5,4},{6,7},{7,6},{8,9},{9,8},{10,11... | collective-permute-start | bytes 1105928 | tf_op jit(solution)/shard_map/ppermute | solution.py:449
  48.6 0.9 %copy-start.15 = (bf16[8,2304]{1,0:T(8,128)(2,1)}, bf16[8,2304]{1,0:T(8,128)(2,1)S(1)}, u32[]{:S(2)}) copy-start(bf16[8,2304]{1,0:T(8,128)(2,1)S(1)} %collective-permute-done.6) | copy-start | bytes 110596
  51.9 5.0 %collective-permute-start.12 = (bf16[24,2304]{1,0:T(8,128)(2,1)}, bf16[24,2304]{1,0:T(8,128)(2,1)S(1)}, u32[]{:S(2)}, u32[]{:S(2)}) collective-permute-start(bf16[24,2304]{1,0:T(8,128)(2,1)} %pad_maximum_fusion), channel_id=1, source_target_pairs={{0,16},{16,0},{1,17},{17,1},{2,18},{18,2},{3,19},{19,3},{4,20},{20... | collective-permute-start | bytes 331784 | tf_op jit(solution)/shard_map/ppermute | solution.py:446
  52.5 0.7 copy-start.7
  53.2 5.6 %collective-permute-start.17 = (bf16[160,2304]{1,0:T(8,128)(2,1)S(1)}, bf16[160,2304]{1,0:T(8,128)(2,1)S(1)}, u32[]{:S(2)}, u32[]{:S(2)}) collective-permute-start(bf16[160,2304]{1,0:T(8,128)(2,1)S(1)} %collective-permute-done.9.refs_2_), channel_id=1, source_target_pairs={{0,1},{1,0},{2,3},{3,2},{4,5},{5,4},{6,7},{7,6},{8,9},{9,8},{10,11... | collective-permute-start | bytes 2211848 | tf_op jit(solution)/shard_map/ppermute | solution.py:449
  54.5 2.4 %collective-permute-start.18 = (bf16[80,2304]{1,0:T(8,128)(2,1)S(1)}, bf16[80,2304]{1,0:T(8,128)(2,1)S(1)}, u32[]{:S(2)}, u32[]{:S(2)}) collective-permute-start(bf16[80,2304]{1,0:T(8,128)(2,1)S(1)} %collective-permute-done.7.refs_3_), channel_id=1, source_target_pairs={{0,1},{1,0},{2,3},{3,2},{4,5},{5,4},{6,7},{7,6},{8,9},{9,8},{10,11... | collective-permute-start | bytes 1105928 | tf_op jit(solution)/shard_map/ppermute | solution.py:449
  54.5 2.4 %collective-permute-start.19 = (bf16[80,2304]{1,0:T(8,128)(2,1)}, bf16[80,2304]{1,0:T(8,128)(2,1)S(1)}, u32[]{:S(2)}, u32[]{:S(2)}) collective-permute-start(bf16[80,2304]{1,0:T(8,128)(2,1)} %copy-done.5), channel_id=1, source_target_pairs={{0,1},{1,0},{2,3},{3,2},{4,5},{5,4},{6,7},{7,6},{8,9},{9,8},{10,11... | collective-permute-start | bytes 1105928 | tf_op jit(solution)/shard_map/ppermute | solution.py:449
  55.1 2.4 %collective-permute-start.20 = (bf16[80,2304]{1,0:T(8,128)(2,1)}, bf16[80,2304]{1,0:T(8,128)(2,1)S(1)}, u32[]{:S(2)}, u32[]{:S(2)}) collective-permute-start(bf16[80,2304]{1,0:T(8,128)(2,1)} %copy-done.7), channel_id=1, source_target_pairs={{0,1},{1,0},{2,3},{3,2},{4,5},{5,4},{6,7},{7,6},{8,9},{9,8},{10,11... | collective-permute-start | bytes 1105928 | tf_op jit(solution)/shard_map/ppermute | solution.py:449
  56.9 1.9 %collective-permute-start.21 = (bf16[80,2304]{1,0:T(8,128)(2,1)}, bf16[80,2304]{1,0:T(8,128)(2,1)S(1)}, u32[]{:S(2)}, u32[]{:S(2)}) collective-permute-start(bf16[80,2304]{1,0:T(8,128)(2,1)} %collective-permute-done.14.refs_6_), channel_id=1, source_target_pairs={{0,1},{1,0},{2,3},{3,2},{4,5},{5,4},{6,7},{7,6},{8,9},{9,8},{10,11... | collective-permute-start | bytes 1105928 | tf_op jit(solution)/shard_map/ppermute | solution.py:449
  58.8 1.0 %copy-start.6 = (bf16[80,2304]{1,0:T(8,128)(2,1)S(1)}, bf16[80,2304]{1,0:T(8,128)(2,1)}, u32[]{:S(2)}) copy-start(bf16[80,2304]{1,0:T(8,128)(2,1)} %copy-done.5) | copy-start | bytes 1105924
  59.8 1.0 %copy-start.8 = (bf16[80,2304]{1,0:T(8,128)(2,1)S(1)}, bf16[80,2304]{1,0:T(8,128)(2,1)}, u32[]{:S(2)}) copy-start(bf16[80,2304]{1,0:T(8,128)(2,1)} %copy-done.7) | copy-start | bytes 1105924
  77.2 0.8 copy-start.4
  78.0 9.1 %collective-permute-start.22 = (bf16[128,1152]{1,0:T(8,128)(2,1)S(1)}, bf16[128,1152]{1,0:T(8,128)(2,1)S(1)}, u32[]{:S(2)}, u32[]{:S(2)}) collective-permute-start(bf16[128,1152]{1,0:T(8,128)(2,1)S(1)} %get-tuple-element.46), channel_id=1, source_target_pairs={{0,16},{16,0},{1,17},{17,1},{2,18},{18,2},{3,19},{19,3},{4,20},{20... | collective-permute-start | bytes 884744 | tf_op jit(solution)/shard_map/ppermute | solution.py:446
  87.0 0.7 copy-start.12

commit v5 on v4

--- a/solution.py
+++ b/solution.py
@@ -591,6 +591,7 @@
     which = [(corner, 0), (corner, 1), (corner ^ 3, 0)]
     which += [(corner ^ 1, 0), (corner ^ 2, 0), (corner ^ 1, 1), (corner ^ 2, 1)]
     far = received + [flip(value, 1) for value in received]
+    far[4:6] = [in_hbm(value) for value in far[4:6]]
     offsets = [offset(w, core, n) for w, n in which] + [offset(w, 1 - core, n) for w, n in which]
     places = jnp.stack([x] + offsets).astype(jnp.int32)
 

time: 90.6 us -> 86.4 us (0.954)
  other arithmetic: 8.6 us -> 1.96 us
  waiting for transfers between devices: 22.9 us -> 27 us
  local copies, waits for them, and re-layouts: 5.22 us -> 3.26 us
    ppermute x14, waiting for transfers between devices: 5.51 us -> 8.87 us  [flip(): return lax.ppermute(value, 'grid', [(n, n ^ bits) for n in everyone])]
    ppermute x3, waiting for transfers between devices: 7.02 us -> 9.7 us  [shards_by_table(): lax.ppermute(message, 'grid', [(n, (n + 4 * shift) % 16) for n in everyone])]
    unnamed x36 -> x24, local copies, waits for them, and re-layouts: 5.1 us -> 3.14 us
    ppermute x6, waiting for transfers between devices: 10.4 us -> 8.42 us  [over_x(): return lax.ppermute(value, 'orb', across)]
    another operation x4, other arithmetic: 1.86 us -> 0.18 us
  transfers between devices with their start and end apart: 23 -> 23, of which waited for: 10 -> 11; matrix products, arithmetic and copies ran while one was open for 10% -> 2% of each run, Pallas kernels for 18% -> 19%
where the time goes in v5:
time: 86.4 us; the launch traced here: 86.2 us
  Pallas kernels  35 us (41%)
  waiting for transfers between devices  27 us (31%)
  starting transfers between devices  18.7 us (22%)
  local copies, waits for them, and re-layouts  3.26 us (4%)
  other arithmetic  1.96 us (2%)
    pallas_call x1, Pallas kernels, shards_by_table(): pl.pallas_call(functools.partial(finish_kernel, step, pieces), out_shape=...  16.4 us
    ppermute x3, waiting for transfers between devices, shards_by_table(): lax.ppermute(message, 'grid', [(n, (n + 4 * shift) % 16) for n in everyone])  9.7 us
    ppermute x14, starting transfers between devices, flip(): return lax.ppermute(value, 'grid', [(n, n ^ bits) for n in everyone])  9.46 us
    ppermute x14, waiting for transfers between devices, flip(): return lax.ppermute(value, 'grid', [(n, n ^ bits) for n in everyone])  8.87 us
    ppermute x6, waiting for transfers between devices, over_x(): return lax.ppermute(value, 'orb', across)  8.42 us
    pallas_call x1, Pallas kernels, shards_by_table(): pl.pallas_call(functools.partial(own_kernel, step), out_shape=(part_shape...  7.37 us
    ppermute x6, starting transfers between devices, over_x(): return lax.ppermute(value, 'orb', across)  6.45 us
    pallas_call x1, Pallas kernels, shards_by_table(): pl.pallas_call(functools.partial(other_kernel, step), out_shape=(part_sha...  5.85 us
  transfers between devices with their start and end apart: 23, of which 11 were waited for; matrix products, arithmetic and copies ran while one was open for 2% of the time, Pallas kernels for 19%

profile of v5, /device:TPU:0, one launch (start us, length us, event | category | flops | bytes accessed | tf_op | source)
XLA Modules:
  0.0 86.2 jit_solution(4160096914414591331)
XLA Ops:
  0.0 3.0 %collective-permute-start = (bf16[64,2304]{1,0:T(8,128)(2,1)}, bf16[64,2304]{1,0:T(8,128)(2,1)S(1)}, u32[]{:S(2)}, u32[]{:S(2)}) collective-permute-start(bf16[64,2304]{1,0:T(8,128)(2,1)} %bitcast.20), channel_id=1, source_target_pairs={{0,16},{16,0},{1,17},{17,1},{2,18},{18,2},{3,19},{19,3},{4,20},{20... | collective-permute-start | bytes 884744 | tf_op jit(solution)/shard_map/ppermute | solution.py:446
  3.0 0.6 pad_add_fusion.1.place
  3.6 3.1 %slabs.1 = (bf16[80,2304]{1,0:T(8,128)(2,1)}, bf16[80,2304]{1,0:T(8,128)(2,1)}, bf16[160,2304]{1,0:T(8,128)(2,1)}) custom-call(s32[3]{0:T(128)} %pad_add_fusion.1.place, bf16[1280,2304]{1,0:T(8,128)(2,1)} %table_hbm.2), custom_call_target="tpu_custom_call" | custom-call | tf_op jit(solution)/shard_map/slabs/pallas_call | solution.py:465
  6.8 0.1 collective-permute-start.4
  6.9 1.9 %collective-permute-start.5 = (bf16[80,2304]{1,0:T(8,128)(2,1)}, bf16[80,2304]{1,0:T(8,128)(2,1)S(1)}, u32[]{:S(2)}, u32[]{:S(2)}) collective-permute-start(bf16[80,2304]{1,0:T(8,128)(2,1)} %get-tuple-element.33), channel_id=1, source_target_pairs={{0,16},{16,0},{1,17},{17,1},{2,18},{18,2},{3,19},{19,3},{4,20},{20... | collective-permute-start | bytes 1105928 | tf_op jit(solution)/shard_map/ppermute | solution.py:446
  8.9 0.1 convert_reduce_fusion
  9.1 0.1 pad_add_fusion.place
  9.2 7.4 %own_orbital.1 = (bf16[128,2304]{1,0:T(8,128)(2,1)S(1)}, bf16[32,1280]{1,0:T(8,128)(2,1)S(1)}, bf16[256,1280]{1,0:T(8,128)(2,1)S(1)}, f32[16,2304]{1,0:T(8,128)S(1)}, bf16[1280,2304]{1,0:T(8,128)(2,1)S(1)}) custom-call(s32[2]{0:T(128)S(1)} %pad_add_fusion.place, bf16[64,2304]{1,0:T(8,128)(2,1)S(1)} %bitcast.22, bf16[256,2304]{1,0:T(8,128)(2,1)S(1)} %bitcast.19, ...), custom_call_target="tpu_custom_call" | custom-call | tf_op jit(solution)/shard_map/own_orbital/pallas_call | solution.py:489
  16.6 0.1 exponential_select_fusion.5
  16.6 0.0 collective-permute-done.other
  16.7 5.9 %other_orbital.1 = (bf16[128,2304]{1,0:T(8,128)(2,1)S(1)}, bf16[32,1280]{1,0:T(8,128)(2,1)S(1)}, f32[32,2304]{1,0:T(8,128)S(1)}) custom-call(s32[2]{0:T(128)S(1)} %pad_add_fusion.place, bf16[64,2304]{1,0:T(8,128)(2,1)S(1)} %collective-permute-done.other, bf16[256,1280]{1,0:T(8,128)(2,1)S(1)} %get-tuple-element.28.psi_ref, ...), custom_call_target="tpu_custom_call" | custom-call | tf_op jit(solution)/shard_map/other_orbital/pallas_call | solution.py:511
  22.5 0.8 copy-done.3
  23.4 0.2 collective-permute-start.3
  23.6 1.5 %collective-permute-start.2 = (bf16[16,2304]{1,0:T(8,128)(2,1)S(1)}, bf16[16,2304]{1,0:T(8,128)(2,1)S(1)}, u32[]{:S(2)}, u32[]{:S(2)}) collective-permute-start(bf16[16,2304]{1,0:T(8,128)(2,1)S(1)} %pad_maximum_fusion.1), channel_id=1, source_target_pairs={{0,2},{1,3},{2,0},{3,1},{4,6},{5,7},{6,4},{7,5},{8,10},{9,11},{10,... | collective-permute-start | bytes 221192 | tf_op jit(solution)/shard_map/ppermute | solution.py:449
  25.1 0.3 collective-permute-start.1
  25.4 0.0 collective-permute-done.4.refs_0_
  25.4 0.4 collective-permute-start.9
  25.8 2.2 %collective-permute-done.3 = bf16[16,2304]{1,0:T(8,128)(2,1)S(1)} collective-permute-done((bf16[16,2304]{1,0:T(8,128)(2,1)S(1)}, bf16[16,2304]{1,0:T(8,128)(2,1)S(1)}, u32[]{:S(2)}, u32[]{:S(2)}) %collective-permute-start.3) | collective-permute-done | bytes 73760 | tf_op jit(solution)/shard_map/ppermute | solution.py:449
  28.0 1.0 %collective-permute-start.7 = (bf16[80,2304]{1,0:T(8,128)(2,1)S(1)}, bf16[80,2304]{1,0:T(8,128)(2,1)S(1)}, u32[]{:S(2)}, u32[]{:S(2)}) collective-permute-start(bf16[80,2304]{1,0:T(8,128)(2,1)S(1)} %collective-permute-done.4.refs_0_), channel_id=1, source_target_pairs={{0,2},{1,3},{2,0},{3,1},{4,6},{5,7},{6,4},{7,5},{8,10},{9,11},{10,... | collective-permute-start | bytes 1105928 | tf_op jit(solution)/shard_map/ppermute | solution.py:449
  29.0 0.7 collective-permute-done.2
  29.6 1.6 %collective-permute-start.8 = (bf16[80,2304]{1,0:T(8,128)(2,1)S(1)}, bf16[80,2304]{1,0:T(8,128)(2,1)}, u32[]{:S(2)}, u32[]{:S(2)}) collective-permute-start(bf16[80,2304]{1,0:T(8,128)(2,1)S(1)} %collective-permute-done.4.refs_0_), channel_id=1, source_target_pairs={{0,4},{1,5},{2,6},{3,7},{4,0},{5,1},{6,2},{7,3},{8,12},{9,13},{10,... | collective-permute-start | bytes 1105928 | tf_op jit(solution)/shard_map/ppermute | solution.py:449
  31.2 0.0 collective-permute-done.1
  31.3 0.1 add_convert_fusion.1
  31.3 0.0 collective-permute-done.5.refs_1_
  31.3 0.1 add_convert_fusion
  31.4 2.5 %collective-permute-start.11 = (bf16[8,2304]{1,0:T(8,128)(2,1)S(1)}, bf16[8,2304]{1,0:T(8,128)(2,1)S(1)}, u32[]{:S(2)}, u32[]{:S(2)}) collective-permute-start(bf16[8,2304]{1,0:T(8,128)(2,1)S(1)} %get-tuple-element.55), channel_id=1, source_target_pairs={{0,12},{1,13},{2,14},{3,15},{4,0},{5,1},{6,2},{7,3},{8,4},{9,5},{1... | collective-permute-start | bytes 110600 | tf_op jit(solution)/shard_map/ppermute | solution.py:565
  34.0 0.2 collective-permute-start.10
  34.2 7.6 %collective-permute-done.11 = bf16[8,2304]{1,0:T(8,128)(2,1)S(1)} collective-permute-done((bf16[8,2304]{1,0:T(8,128)(2,1)S(1)}, bf16[8,2304]{1,0:T(8,128)(2,1)S(1)}, u32[]{:S(2)}, u32[]{:S(2)}) %collective-permute-start.11) | collective-permute-done | bytes 36896 | tf_op jit(solution)/shard_map/ppermute | solution.py:565
  41.8 0.0 collective-permute-start.6
  41.8 0.0 collective-permute-done.7.refs_3_
  41.8 0.7 collective-permute-start.13
  42.5 0.0 collective-permute-done.8.refs_4_
  42.5 2.8 %collective-permute-start.14 = (bf16[80,2304]{1,0:T(8,128)(2,1)S(1)}, bf16[80,2304]{1,0:T(8,128)(2,1)}, u32[]{:S(2)}, u32[]{:S(2)}) collective-permute-start(bf16[80,2304]{1,0:T(8,128)(2,1)S(1)} %collective-permute-done.5.refs_1_), channel_id=1, source_target_pairs={{0,4},{1,5},{2,6},{3,7},{4,0},{5,1},{6,2},{7,3},{8,12},{9,13},{10,... | collective-permute-start | bytes 1105928 | tf_op jit(solution)/shard_map/ppermute | solution.py:449
  45.3 0.0 collective-permute-done.9.refs_2_
  45.3 0.0 collective-permute-start.15
  45.3 0.0 collective-permute-done.10
  45.3 0.5 collective-permute-start.16
  45.8 2.1 %collective-permute-done.6 = bf16[8,2304]{1,0:T(8,128)(2,1)S(1)} collective-permute-done((bf16[8,2304]{1,0:T(8,128)(2,1)S(1)}, bf16[8,2304]{1,0:T(8,128)(2,1)S(1)}, u32[]{:S(2)}, u32[]{:S(2)}) %collective-permute-start.6) | collective-permute-done | bytes 36896 | tf_op jit(solution)/shard_map/ppermute | solution.py:565
  47.9 0.1 select_convert_fusion
  48.0 0.1 select_convert_fusion.1
  48.1 0.7 pad_maximum_fusion
  48.7 0.3 collective-permute-start.12
  49.1 2.6 %collective-permute-done.13.refs_5_ = bf16[80,2304]{1,0:T(8,128)(2,1)S(1)} collective-permute-done((bf16[80,2304]{1,0:T(8,128)(2,1)S(1)}, bf16[80,2304]{1,0:T(8,128)(2,1)S(1)}, u32[]{:S(2)}, u32[]{:S(2)}) %collective-permute-start.13) | collective-permute-done | bytes 368672 | tf_op jit(solution)/shard_map/ppermute | solution.py:449
  51.7 0.7 copy-done.8
  52.4 0.0 collective-permute-start.17
  52.4 0.1 stack.75.place
  52.5 0.8 collective-permute-done.14.refs_6_
  53.3 0.0 collective-permute-start.18
  53.3 0.0 collective-permute-done.15.refs_7_
  53.3 0.5 collective-permute-start.19
  53.8 0.0 collective-permute-done.16.refs_8_
  53.9 0.1 collective-permute-start.20
  53.9 0.0 collective-permute-done.12.arrived
  53.9 0.4 collective-permute-start.21
  54.4 1.3 %collective-permute-done.18.refs_10_ = bf16[80,2304]{1,0:T(8,128)(2,1)S(1)} collective-permute-done((bf16[80,2304]{1,0:T(8,128)(2,1)S(1)}, bf16[80,2304]{1,0:T(8,128)(2,1)S(1)}, u32[]{:S(2)}, u32[]{:S(2)}) %collective-permute-start.18) | collective-permute-done | bytes 368672 | tf_op jit(solution)/shard_map/ppermute | solution.py:449
  55.7 0.2 collective-permute-done.19.refs_11_
  55.9 0.5 collective-permute-done.20.refs_12_
  56.4 0.5 collective-permute-done.21.refs_13_
  56.9 16.4 %finish.1 = (bf16[128,1152]{1,0:T(8,128)(2,1)S(1)}, f32[128,1152]{1,0:T(8,128)S(1)}) custom-call(s32[15]{0:T(128)S(1)} %stack.75.place, bf16[64,2304]{1,0:T(8,128)(2,1)} %bitcast.21, bf16[64,2304]{1,0:T(8,128)(2,1)S(1)} %collective-permute-done.other, bf16[256,2304]{1,0:T(8,128)(2,1)} %bitcast.18, f32[1,1280]{1,0:T(1,128)S(1)} %broadcast_in_dim.24.weight, ...), custom_call_target="tpu_custom_call" | custom-call | tf_op jit(solution)/shard_map/finish/pallas_call | solution.py:598
  73.4 0.8 copy-done.4
  74.2 0.6 collective-permute-start.22
  74.8 8.4 %collective-permute-done.22.came = bf16[128,1152]{1,0:T(8,128)(2,1)S(1)} collective-permute-done((bf16[128,1152]{1,0:T(8,128)(2,1)S(1)}, bf16[128,1152]{1,0:T(8,128)(2,1)S(1)}, u32[]{:S(2)}, u32[]{:S(2)}) %collective-permute-start.22) | collective-permute-done | bytes 294944 | tf_op jit(solution)/shard_map/ppermute | solution.py:446
  83.2 0.7 copy-done.9
  84.0 2.2 %place.1 = f32[4,64,1152]{2,1,0:T(8,128)} custom-call(s32[2]{0:T(128)} %copy-done.7, f32[128,1152]{1,0:T(8,128)} %copy-done.4, bf16[128,1152]{1,0:T(8,128)(2,1)} %copy-done.9), custom_call_target="tpu_custom_call" | custom-call | tf_op jit(solution)/shard_map/place/pallas_call | solution.py:630
  (37 shorter events, 0.2 us)
Async XLA Ops:
  0.0 9.2 %copy-start.1 = (bf16[1,64,2304]{2,1,0:T(8,128)(2,1)S(1)}, bf16[1,64,2304]{2,1,0:T(8,128)(2,1)}, u32[]{:S(2)}) copy-start(bf16[1,64,2304]{2,1,0:T(8,128)(2,1)} %param.5) | copy-start | bytes 884740
  0.0 8.9 %copy-start.10 = (f32[1280]{0:T(1024)S(1)}, f32[1280]{0:T(1024)}, u32[]{:S(2)}) copy-start(f32[1280]{0:T(1024)} %param.8) | copy-start | bytes 15364
  0.0 8.9 %copy-start.11 = (s32[2304]{0:T(1024)S(1)}, s32[2304]{0:T(1024)}, u32[]{:S(2)}) copy-start(s32[2304]{0:T(1024)} %param.9) | copy-start | bytes 27652
  0.0 9.2 %copy-start = (bf16[4,64,2304]{2,1,0:T(8,128)(2,1)S(1)}, bf16[4,64,2304]{2,1,0:T(8,128)(2,1)}, u32[]{:S(2)}) copy-start(bf16[4,64,2304]{2,1,0:T(8,128)(2,1)} %param.6) | copy-start | bytes 3538948
  0.0 16.6 %collective-permute-start = (bf16[64,2304]{1,0:T(8,128)(2,1)}, bf16[64,2304]{1,0:T(8,128)(2,1)S(1)}, u32[]{:S(2)}, u32[]{:S(2)}) collective-permute-start(bf16[64,2304]{1,0:T(8,128)(2,1)} %bitcast.20), channel_id=1, source_target_pairs={{0,16},{16,0},{1,17},{17,1},{2,18},{18,2},{3,19},{19,3},{4,20},{20... | collective-permute-start | bytes 884744 | tf_op jit(solution)/shard_map/ppermute | solution.py:446
  6.8 18.6 %collective-permute-start.4 = (bf16[80,2304]{1,0:T(8,128)(2,1)}, bf16[80,2304]{1,0:T(8,128)(2,1)S(1)}, u32[]{:S(2)}, u32[]{:S(2)}) collective-permute-start(bf16[80,2304]{1,0:T(8,128)(2,1)} %get-tuple-element.26), channel_id=1, source_target_pairs={{0,16},{16,0},{1,17},{17,1},{2,18},{18,2},{3,19},{19,3},{4,20},{20... | collective-permute-start | bytes 1105928 | tf_op jit(solution)/shard_map/ppermute | solution.py:446
  6.9 24.4 %collective-permute-start.5 = (bf16[80,2304]{1,0:T(8,128)(2,1)}, bf16[80,2304]{1,0:T(8,128)(2,1)S(1)}, u32[]{:S(2)}, u32[]{:S(2)}) collective-permute-start(bf16[80,2304]{1,0:T(8,128)(2,1)} %get-tuple-element.33), channel_id=1, source_target_pairs={{0,16},{16,0},{1,17},{17,1},{2,18},{18,2},{3,19},{19,3},{4,20},{20... | collective-permute-start | bytes 1105928 | tf_op jit(solution)/shard_map/ppermute | solution.py:446
  9.2 13.4 %copy-start.7 = (s32[2]{0:T(128)}, s32[2]{0:T(128)S(1)}, u32[]{:S(2)}) copy-start(s32[2]{0:T(128)S(1)} %pad_add_fusion.place) | copy-start | bytes 28
  16.6 6.0 %copy-start.2 = (bf16[128,2304]{1,0:T(8,128)(2,1)}, bf16[128,2304]{1,0:T(8,128)(2,1)S(1)}, u32[]{:S(2)}) copy-start(bf16[128,2304]{1,0:T(8,128)(2,1)S(1)} %get-tuple-element.40.part_any) | copy-start | bytes 1769476
  16.6 6.8 %copy-start.5 = (bf16[32,1280]{1,0:T(8,128)(2,1)}, bf16[32,1280]{1,0:T(8,128)(2,1)S(1)}, u32[]{:S(2)}) copy-start(bf16[32,1280]{1,0:T(8,128)(2,1)S(1)} %get-tuple-element.42.phi_any) | copy-start | bytes 245764
  22.5 0.8 copy-start.3
  23.4 24.7 %copy-start.6 = (bf16[32,1280]{1,0:T(8,128)(2,1)}, bf16[32,1280]{1,0:T(8,128)(2,1)S(1)}, u32[]{:S(2)}) copy-start(bf16[32,1280]{1,0:T(8,128)(2,1)S(1)} %get-tuple-element.43.other_phi_any) | copy-start | bytes 245764
  23.4 4.6 %collective-permute-start.3 = (bf16[16,2304]{1,0:T(8,128)(2,1)S(1)}, bf16[16,2304]{1,0:T(8,128)(2,1)S(1)}, u32[]{:S(2)}, u32[]{:S(2)}) collective-permute-start(bf16[16,2304]{1,0:T(8,128)(2,1)S(1)} %pad_maximum_fusion.1), channel_id=1, source_target_pairs={{0,3},{1,2},{2,1},{3,0},{4,7},{5,6},{6,5},{7,4},{8,11},{9,10},{10,... | collective-permute-start | bytes 221192 | tf_op jit(solution)/shard_map/ppermute | solution.py:449
  23.6 6.0 %collective-permute-start.2 = (bf16[16,2304]{1,0:T(8,128)(2,1)S(1)}, bf16[16,2304]{1,0:T(8,128)(2,1)S(1)}, u32[]{:S(2)}, u32[]{:S(2)}) collective-permute-start(bf16[16,2304]{1,0:T(8,128)(2,1)S(1)} %pad_maximum_fusion.1), channel_id=1, source_target_pairs={{0,2},{1,3},{2,0},{3,1},{4,6},{5,7},{6,4},{7,5},{8,10},{9,11},{10,... | collective-permute-start | bytes 221192 | tf_op jit(solution)/shard_map/ppermute | solution.py:449
  25.1 6.1 %collective-permute-start.1 = (bf16[16,2304]{1,0:T(8,128)(2,1)S(1)}, bf16[16,2304]{1,0:T(8,128)(2,1)S(1)}, u32[]{:S(2)}, u32[]{:S(2)}) collective-permute-start(bf16[16,2304]{1,0:T(8,128)(2,1)S(1)} %pad_maximum_fusion.1), channel_id=1, source_target_pairs={{0,1},{1,0},{2,3},{3,2},{4,5},{5,4},{6,7},{7,6},{8,9},{9,8},{10,11... | collective-permute-start | bytes 221192 | tf_op jit(solution)/shard_map/ppermute | solution.py:449
  25.4 19.9 %collective-permute-start.9 = (bf16[160,2304]{1,0:T(8,128)(2,1)}, bf16[160,2304]{1,0:T(8,128)(2,1)S(1)}, u32[]{:S(2)}, u32[]{:S(2)}) collective-permute-start(bf16[160,2304]{1,0:T(8,128)(2,1)} %get-tuple-element.36), channel_id=1, source_target_pairs={{0,16},{16,0},{1,17},{17,1},{2,18},{18,2},{3,19},{19,3},{4,20},{20... | collective-permute-start | bytes 2211848 | tf_op jit(solution)/shard_map/ppermute | solution.py:446
  28.0 13.8 %collective-permute-start.7 = (bf16[80,2304]{1,0:T(8,128)(2,1)S(1)}, bf16[80,2304]{1,0:T(8,128)(2,1)S(1)}, u32[]{:S(2)}, u32[]{:S(2)}) collective-permute-start(bf16[80,2304]{1,0:T(8,128)(2,1)S(1)} %collective-permute-done.4.refs_0_), channel_id=1, source_target_pairs={{0,2},{1,3},{2,0},{3,1},{4,6},{5,7},{6,4},{7,5},{8,10},{9,11},{10,... | collective-permute-start | bytes 1105928 | tf_op jit(solution)/shard_map/ppermute | solution.py:449
  29.6 12.9 %collective-permute-start.8 = (bf16[80,2304]{1,0:T(8,128)(2,1)S(1)}, bf16[80,2304]{1,0:T(8,128)(2,1)}, u32[]{:S(2)}, u32[]{:S(2)}) collective-permute-start(bf16[80,2304]{1,0:T(8,128)(2,1)S(1)} %collective-permute-done.4.refs_0_), channel_id=1, source_target_pairs={{0,4},{1,5},{2,6},{3,7},{4,0},{5,1},{6,2},{7,3},{8,12},{9,13},{10,... | collective-permute-start | bytes 1105928 | tf_op jit(solution)/shard_map/ppermute | solution.py:449
  31.4 10.3 %collective-permute-start.11 = (bf16[8,2304]{1,0:T(8,128)(2,1)S(1)}, bf16[8,2304]{1,0:T(8,128)(2,1)S(1)}, u32[]{:S(2)}, u32[]{:S(2)}) collective-permute-start(bf16[8,2304]{1,0:T(8,128)(2,1)S(1)} %get-tuple-element.55), channel_id=1, source_target_pairs={{0,12},{1,13},{2,14},{3,15},{4,0},{5,1},{6,2},{7,3},{8,4},{9,5},{1... | collective-permute-start | bytes 110600 | tf_op jit(solution)/shard_map/ppermute | solution.py:565
  34.0 11.3 %collective-permute-start.10 = (bf16[8,2304]{1,0:T(8,128)(2,1)S(1)}, bf16[8,2304]{1,0:T(8,128)(2,1)S(1)}, u32[]{:S(2)}, u32[]{:S(2)}) collective-permute-start(bf16[8,2304]{1,0:T(8,128)(2,1)S(1)} %get-tuple-element.56), channel_id=1, source_target_pairs={{0,8},{1,9},{2,10},{3,11},{4,12},{5,13},{6,14},{7,15},{8,0},{9,1},... | collective-permute-start | bytes 110600 | tf_op jit(solution)/shard_map/ppermute | solution.py:565
  41.8 6.1 %collective-permute-start.6 = (bf16[8,2304]{1,0:T(8,128)(2,1)S(1)}, bf16[8,2304]{1,0:T(8,128)(2,1)S(1)}, u32[]{:S(2)}, u32[]{:S(2)}) collective-permute-start(bf16[8,2304]{1,0:T(8,128)(2,1)S(1)} %get-tuple-element.54), channel_id=1, source_target_pairs={{0,4},{1,5},{2,6},{3,7},{4,8},{5,9},{6,10},{7,11},{8,12},{9,13},{1... | collective-permute-start | bytes 110600 | tf_op jit(solution)/shard_map/ppermute | solution.py:565
  41.8 9.9 %collective-permute-start.13 = (bf16[80,2304]{1,0:T(8,128)(2,1)S(1)}, bf16[80,2304]{1,0:T(8,128)(2,1)S(1)}, u32[]{:S(2)}, u32[]{:S(2)}) collective-permute-start(bf16[80,2304]{1,0:T(8,128)(2,1)S(1)} %collective-permute-done.5.refs_1_), channel_id=1, source_target_pairs={{0,2},{1,3},{2,0},{3,1},{4,6},{5,7},{6,4},{7,5},{8,10},{9,11},{10,... | collective-permute-start | bytes 1105928 | tf_op jit(solution)/shard_map/ppermute | solution.py:449
  42.5 10.8 %collective-permute-start.14 = (bf16[80,2304]{1,0:T(8,128)(2,1)S(1)}, bf16[80,2304]{1,0:T(8,128)(2,1)}, u32[]{:S(2)}, u32[]{:S(2)}) collective-permute-start(bf16[80,2304]{1,0:T(8,128)(2,1)S(1)} %collective-permute-done.5.refs_1_), channel_id=1, source_target_pairs={{0,4},{1,5},{2,6},{3,7},{4,0},{5,1},{6,2},{7,3},{8,12},{9,13},{10,... | collective-permute-start | bytes 1105928 | tf_op jit(solution)/shard_map/ppermute | solution.py:449
  45.3 8.1 %collective-permute-start.15 = (bf16[80,2304]{1,0:T(8,128)(2,1)S(1)}, bf16[80,2304]{1,0:T(8,128)(2,1)}, u32[]{:S(2)}, u32[]{:S(2)}) collective-permute-start(bf16[80,2304]{1,0:T(8,128)(2,1)S(1)} %collective-permute-done.4.refs_0_), channel_id=1, source_target_pairs={{0,1},{1,0},{2,3},{3,2},{4,5},{5,4},{6,7},{7,6},{8,9},{9,8},{10,11... | collective-permute-start | bytes 1105928 | tf_op jit(solution)/shard_map/ppermute | solution.py:449
  45.3 8.6 %collective-permute-start.16 = (bf16[80,2304]{1,0:T(8,128)(2,1)S(1)}, bf16[80,2304]{1,0:T(8,128)(2,1)}, u32[]{:S(2)}, u32[]{:S(2)}) collective-permute-start(bf16[80,2304]{1,0:T(8,128)(2,1)S(1)} %collective-permute-done.5.refs_1_), channel_id=1, source_target_pairs={{0,1},{1,0},{2,3},{3,2},{4,5},{5,4},{6,7},{7,6},{8,9},{9,8},{10,11... | collective-permute-start | bytes 1105928 | tf_op jit(solution)/shard_map/ppermute | solution.py:449
  48.7 5.2 %collective-permute-start.12 = (bf16[24,2304]{1,0:T(8,128)(2,1)}, bf16[24,2304]{1,0:T(8,128)(2,1)S(1)}, u32[]{:S(2)}, u32[]{:S(2)}) collective-permute-start(bf16[24,2304]{1,0:T(8,128)(2,1)} %pad_maximum_fusion), channel_id=1, source_target_pairs={{0,16},{16,0},{1,17},{17,1},{2,18},{18,2},{3,19},{19,3},{4,20},{20... | collective-permute-start | bytes 331784 | tf_op jit(solution)/shard_map/ppermute | solution.py:446
  51.7 0.7 copy-start.8
  52.4 4.5 %collective-permute-start.17 = (bf16[160,2304]{1,0:T(8,128)(2,1)S(1)}, bf16[160,2304]{1,0:T(8,128)(2,1)S(1)}, u32[]{:S(2)}, u32[]{:S(2)}) collective-permute-start(bf16[160,2304]{1,0:T(8,128)(2,1)S(1)} %collective-permute-done.9.refs_2_), channel_id=1, source_target_pairs={{0,1},{1,0},{2,3},{3,2},{4,5},{5,4},{6,7},{7,6},{8,9},{9,8},{10,11... | collective-permute-start | bytes 2211848 | tf_op jit(solution)/shard_map/ppermute | solution.py:449
  53.3 2.3 %collective-permute-start.18 = (bf16[80,2304]{1,0:T(8,128)(2,1)S(1)}, bf16[80,2304]{1,0:T(8,128)(2,1)S(1)}, u32[]{:S(2)}, u32[]{:S(2)}) collective-permute-start(bf16[80,2304]{1,0:T(8,128)(2,1)S(1)} %collective-permute-done.7.refs_3_), channel_id=1, source_target_pairs={{0,1},{1,0},{2,3},{3,2},{4,5},{5,4},{6,7},{7,6},{8,9},{9,8},{10,11... | collective-permute-start | bytes 1105928 | tf_op jit(solution)/shard_map/ppermute | solution.py:449
  53.3 2.5 %collective-permute-start.19 = (bf16[80,2304]{1,0:T(8,128)(2,1)}, bf16[80,2304]{1,0:T(8,128)(2,1)S(1)}, u32[]{:S(2)}, u32[]{:S(2)}) collective-permute-start(bf16[80,2304]{1,0:T(8,128)(2,1)} %collective-permute-done.8.refs_4_), channel_id=1, source_target_pairs={{0,1},{1,0},{2,3},{3,2},{4,5},{5,4},{6,7},{7,6},{8,9},{9,8},{10,11... | collective-permute-start | bytes 1105928 | tf_op jit(solution)/shard_map/ppermute | solution.py:449
  53.9 2.6 %collective-permute-start.20 = (bf16[80,2304]{1,0:T(8,128)(2,1)}, bf16[80,2304]{1,0:T(8,128)(2,1)S(1)}, u32[]{:S(2)}, u32[]{:S(2)}) collective-permute-start(bf16[80,2304]{1,0:T(8,128)(2,1)} %copy-done.8), channel_id=1, source_target_pairs={{0,1},{1,0},{2,3},{3,2},{4,5},{5,4},{6,7},{7,6},{8,9},{9,8},{10,11... | collective-permute-start | bytes 1105928 | tf_op jit(solution)/shard_map/ppermute | solution.py:449
  53.9 3.0 %collective-permute-start.21 = (bf16[80,2304]{1,0:T(8,128)(2,1)}, bf16[80,2304]{1,0:T(8,128)(2,1)S(1)}, u32[]{:S(2)}, u32[]{:S(2)}) collective-permute-start(bf16[80,2304]{1,0:T(8,128)(2,1)} %collective-permute-done.14.refs_6_), channel_id=1, source_target_pairs={{0,1},{1,0},{2,3},{3,2},{4,5},{5,4},{6,7},{7,6},{8,9},{9,8},{10,11... | collective-permute-start | bytes 1105928 | tf_op jit(solution)/shard_map/ppermute | solution.py:449
  73.4 0.8 copy-start.4
  74.2 9.1 %collective-permute-start.22 = (bf16[128,1152]{1,0:T(8,128)(2,1)S(1)}, bf16[128,1152]{1,0:T(8,128)(2,1)S(1)}, u32[]{:S(2)}, u32[]{:S(2)}) collective-permute-start(bf16[128,1152]{1,0:T(8,128)(2,1)S(1)} %get-tuple-element.46), channel_id=1, source_target_pairs={{0,16},{16,0},{1,17},{17,1},{2,18},{18,2},{3,19},{19,3},{4,20},{20... | collective-permute-start | bytes 884744 | tf_op jit(solution)/shard_map/ppermute | solution.py:446
  83.2 0.7 copy-start.9

commit v6 on v5

--- a/solution.py
+++ b/solution.py
@@ -143,7 +143,7 @@
 NI = 2
 NP = NI * NC
 CHUNK = 256
-WIDE = 640
+WIDE = 1280
 TILE = 768
 F32 = jnp.float32
 BF16 = jnp.bfloat16

time: 86.4 us -> 85.1 us (0.985)
  Pallas kernels: 35 us -> 33.8 us
    pallas_call x1, Pallas kernels: 16.4 us -> 15.2 us  [shards_by_table(): pl.pallas_call(functools.partial(finish_kernel, step, pieces), out_shape=...]
where the time goes in v6:
time: 85.1 us; the launch traced here: 85 us
  Pallas kernels  33.8 us (40%)
  waiting for transfers between devices  26.9 us (32%)
  starting transfers between devices  18.8 us (22%)
  local copies, waits for them, and re-layouts  3.26 us (4%)
  other arithmetic  1.96 us (2%)
    pallas_call x1, Pallas kernels, shards_by_table(): pl.pallas_call(functools.partial(finish_kernel, step, pieces), out_shape=...  15.2 us
    ppermute x3, waiting for transfers between devices, shards_by_table(): lax.ppermute(message, 'grid', [(n, (n + 4 * shift) % 16) for n in everyone])  9.69 us
    ppermute x14, starting transfers between devices, flip(): return lax.ppermute(value, 'grid', [(n, n ^ bits) for n in everyone])  9.48 us
    ppermute x14, waiting for transfers between devices, flip(): return lax.ppermute(value, 'grid', [(n, n ^ bits) for n in everyone])  8.82 us
    ppermute x6, waiting for transfers between devices, over_x(): return lax.ppermute(value, 'orb', across)  8.36 us
    pallas_call x1, Pallas kernels, shards_by_table(): pl.pallas_call(functools.partial(own_kernel, step), out_shape=(part_shape...  7.37 us
    ppermute x6, starting transfers between devices, over_x(): return lax.ppermute(value, 'orb', across)  6.55 us
    pallas_call x1, Pallas kernels, shards_by_table(): pl.pallas_call(functools.partial(other_kernel, step), out_shape=(part_sha...  5.85 us
  transfers between devices with their start and end apart: 23, of which 11 were waited for; matrix products, arithmetic and copies ran while one was open for 2% of the time, Pallas kernels for 19%

profile of v6, /device:TPU:0, one launch (start us, length us, event | category | flops | bytes accessed | tf_op | source)
XLA Modules:
  0.0 85.0 jit_solution(15847319545864535338)
XLA Ops:
  0.0 3.0 %collective-permute-start = (bf16[64,2304]{1,0:T(8,128)(2,1)}, bf16[64,2304]{1,0:T(8,128)(2,1)S(1)}, u32[]{:S(2)}, u32[]{:S(2)}) collective-permute-start(bf16[64,2304]{1,0:T(8,128)(2,1)} %bitcast.20), channel_id=1, source_target_pairs={{0,16},{16,0},{1,17},{17,1},{2,18},{18,2},{3,19},{19,3},{4,20},{20... | collective-permute-start | bytes 884744 | tf_op jit(solution)/shard_map/ppermute | solution.py:446
  3.0 0.6 pad_add_fusion.1.place
  3.6 3.1 %slabs.1 = (bf16[80,2304]{1,0:T(8,128)(2,1)}, bf16[80,2304]{1,0:T(8,128)(2,1)}, bf16[160,2304]{1,0:T(8,128)(2,1)}) custom-call(s32[3]{0:T(128)} %pad_add_fusion.1.place, bf16[1280,2304]{1,0:T(8,128)(2,1)} %table_hbm.2), custom_call_target="tpu_custom_call" | custom-call | tf_op jit(solution)/shard_map/slabs/pallas_call | solution.py:465
  6.8 0.1 collective-permute-start.4
  6.9 1.9 %collective-permute-start.5 = (bf16[80,2304]{1,0:T(8,128)(2,1)}, bf16[80,2304]{1,0:T(8,128)(2,1)S(1)}, u32[]{:S(2)}, u32[]{:S(2)}) collective-permute-start(bf16[80,2304]{1,0:T(8,128)(2,1)} %get-tuple-element.33), channel_id=1, source_target_pairs={{0,16},{16,0},{1,17},{17,1},{2,18},{18,2},{3,19},{19,3},{4,20},{20... | collective-permute-start | bytes 1105928 | tf_op jit(solution)/shard_map/ppermute | solution.py:446
  8.9 0.1 convert_reduce_fusion
  9.1 0.1 pad_add_fusion.place
  9.2 7.4 %own_orbital.1 = (bf16[128,2304]{1,0:T(8,128)(2,1)S(1)}, bf16[32,1280]{1,0:T(8,128)(2,1)S(1)}, bf16[256,1280]{1,0:T(8,128)(2,1)S(1)}, f32[16,2304]{1,0:T(8,128)S(1)}, bf16[1280,2304]{1,0:T(8,128)(2,1)S(1)}) custom-call(s32[2]{0:T(128)S(1)} %pad_add_fusion.place, bf16[64,2304]{1,0:T(8,128)(2,1)S(1)} %bitcast.22, bf16[256,2304]{1,0:T(8,128)(2,1)S(1)} %bitcast.19, ...), custom_call_target="tpu_custom_call" | custom-call | tf_op jit(solution)/shard_map/own_orbital/pallas_call | solution.py:489
  16.6 0.1 exponential_select_fusion.5
  16.6 0.0 collective-permute-done.other
  16.7 5.9 %other_orbital.1 = (bf16[128,2304]{1,0:T(8,128)(2,1)S(1)}, bf16[32,1280]{1,0:T(8,128)(2,1)S(1)}, f32[32,2304]{1,0:T(8,128)S(1)}) custom-call(s32[2]{0:T(128)S(1)} %pad_add_fusion.place, bf16[64,2304]{1,0:T(8,128)(2,1)S(1)} %collective-permute-done.other, bf16[256,1280]{1,0:T(8,128)(2,1)S(1)} %get-tuple-element.28.psi_ref, ...), custom_call_target="tpu_custom_call" | custom-call | tf_op jit(solution)/shard_map/other_orbital/pallas_call | solution.py:511
  22.5 0.8 copy-done.3
  23.4 0.2 collective-permute-start.3
  23.6 1.5 %collective-permute-start.2 = (bf16[16,2304]{1,0:T(8,128)(2,1)S(1)}, bf16[16,2304]{1,0:T(8,128)(2,1)S(1)}, u32[]{:S(2)}, u32[]{:S(2)}) collective-permute-start(bf16[16,2304]{1,0:T(8,128)(2,1)S(1)} %pad_maximum_fusion.1), channel_id=1, source_target_pairs={{0,2},{1,3},{2,0},{3,1},{4,6},{5,7},{6,4},{7,5},{8,10},{9,11},{10,... | collective-permute-start | bytes 221192 | tf_op jit(solution)/shard_map/ppermute | solution.py:449
  25.1 0.3 collective-permute-start.1
  25.4 0.0 collective-permute-done.4.refs_0_
  25.4 0.4 collective-permute-start.9
  25.8 2.2 %collective-permute-done.3 = bf16[16,2304]{1,0:T(8,128)(2,1)S(1)} collective-permute-done((bf16[16,2304]{1,0:T(8,128)(2,1)S(1)}, bf16[16,2304]{1,0:T(8,128)(2,1)S(1)}, u32[]{:S(2)}, u32[]{:S(2)}) %collective-permute-start.3) | collective-permute-done | bytes 73760 | tf_op jit(solution)/shard_map/ppermute | solution.py:449
  28.0 1.0 %collective-permute-start.7 = (bf16[80,2304]{1,0:T(8,128)(2,1)S(1)}, bf16[80,2304]{1,0:T(8,128)(2,1)S(1)}, u32[]{:S(2)}, u32[]{:S(2)}) collective-permute-start(bf16[80,2304]{1,0:T(8,128)(2,1)S(1)} %collective-permute-done.4.refs_0_), channel_id=1, source_target_pairs={{0,2},{1,3},{2,0},{3,1},{4,6},{5,7},{6,4},{7,5},{8,10},{9,11},{10,... | collective-permute-start | bytes 1105928 | tf_op jit(solution)/shard_map/ppermute | solution.py:449
  29.0 0.6 collective-permute-done.2
  29.6 1.6 %collective-permute-start.8 = (bf16[80,2304]{1,0:T(8,128)(2,1)S(1)}, bf16[80,2304]{1,0:T(8,128)(2,1)}, u32[]{:S(2)}, u32[]{:S(2)}) collective-permute-start(bf16[80,2304]{1,0:T(8,128)(2,1)S(1)} %collective-permute-done.4.refs_0_), channel_id=1, source_target_pairs={{0,4},{1,5},{2,6},{3,7},{4,0},{5,1},{6,2},{7,3},{8,12},{9,13},{10,... | collective-permute-start | bytes 1105928 | tf_op jit(solution)/shard_map/ppermute | solution.py:449
  31.2 0.0 collective-permute-done.1
  31.3 0.1 add_convert_fusion.1
  31.3 0.0 collective-permute-done.5.refs_1_
  31.3 0.1 add_convert_fusion
  31.4 2.5 %collective-permute-start.11 = (bf16[8,2304]{1,0:T(8,128)(2,1)S(1)}, bf16[8,2304]{1,0:T(8,128)(2,1)S(1)}, u32[]{:S(2)}, u32[]{:S(2)}) collective-permute-start(bf16[8,2304]{1,0:T(8,128)(2,1)S(1)} %get-tuple-element.55), channel_id=1, source_target_pairs={{0,12},{1,13},{2,14},{3,15},{4,0},{5,1},{6,2},{7,3},{8,4},{9,5},{1... | collective-permute-start | bytes 110600 | tf_op jit(solution)/shard_map/ppermute | solution.py:565
  34.0 0.2 collective-permute-start.10
  34.2 7.6 %collective-permute-done.11 = bf16[8,2304]{1,0:T(8,128)(2,1)S(1)} collective-permute-done((bf16[8,2304]{1,0:T(8,128)(2,1)S(1)}, bf16[8,2304]{1,0:T(8,128)(2,1)S(1)}, u32[]{:S(2)}, u32[]{:S(2)}) %collective-permute-start.11) | collective-permute-done | bytes 36896 | tf_op jit(solution)/shard_map/ppermute | solution.py:565
  41.7 0.0 collective-permute-start.6
  41.8 0.0 collective-permute-done.7.refs_3_
  41.8 0.7 collective-permute-start.13
  42.5 0.0 collective-permute-done.8.refs_4_
  42.5 2.7 %collective-permute-start.14 = (bf16[80,2304]{1,0:T(8,128)(2,1)S(1)}, bf16[80,2304]{1,0:T(8,128)(2,1)}, u32[]{:S(2)}, u32[]{:S(2)}) collective-permute-start(bf16[80,2304]{1,0:T(8,128)(2,1)S(1)} %collective-permute-done.5.refs_1_), channel_id=1, source_target_pairs={{0,4},{1,5},{2,6},{3,7},{4,0},{5,1},{6,2},{7,3},{8,12},{9,13},{10,... | collective-permute-start | bytes 1105928 | tf_op jit(solution)/shard_map/ppermute | solution.py:449
  45.3 0.0 collective-permute-done.9.refs_2_
  45.3 0.0 collective-permute-start.15
  45.3 0.0 collective-permute-done.10
  45.3 0.5 collective-permute-start.16
  45.8 2.1 %collective-permute-done.6 = bf16[8,2304]{1,0:T(8,128)(2,1)S(1)} collective-permute-done((bf16[8,2304]{1,0:T(8,128)(2,1)S(1)}, bf16[8,2304]{1,0:T(8,128)(2,1)S(1)}, u32[]{:S(2)}, u32[]{:S(2)}) %collective-permute-start.6) | collective-permute-done | bytes 36896 | tf_op jit(solution)/shard_map/ppermute | solution.py:565
  47.9 0.1 select_convert_fusion
  48.0 0.1 select_convert_fusion.1
  48.1 0.7 pad_maximum_fusion
  48.7 0.4 collective-permute-start.12
  49.1 2.6 %collective-permute-done.13.refs_5_ = bf16[80,2304]{1,0:T(8,128)(2,1)S(1)} collective-permute-done((bf16[80,2304]{1,0:T(8,128)(2,1)S(1)}, bf16[80,2304]{1,0:T(8,128)(2,1)S(1)}, u32[]{:S(2)}, u32[]{:S(2)}) %collective-permute-start.13) | collective-permute-done | bytes 368672 | tf_op jit(solution)/shard_map/ppermute | solution.py:449
  51.7 0.7 copy-done.8
  52.4 0.0 collective-permute-start.17
  52.4 0.1 stack.75.place
  52.5 0.8 collective-permute-done.14.refs_6_
  53.3 0.0 collective-permute-start.18
  53.3 0.0 collective-permute-done.15.refs_7_
  53.3 0.5 collective-permute-start.19
  53.8 0.1 collective-permute-start.20
  53.9 0.0 collective-permute-done.12.arrived
  53.9 0.4 collective-permute-start.21
  54.4 1.3 %collective-permute-done.18.refs_10_ = bf16[80,2304]{1,0:T(8,128)(2,1)S(1)} collective-permute-done((bf16[80,2304]{1,0:T(8,128)(2,1)S(1)}, bf16[80,2304]{1,0:T(8,128)(2,1)S(1)}, u32[]{:S(2)}, u32[]{:S(2)}) %collective-permute-start.18) | collective-permute-done | bytes 368672 | tf_op jit(solution)/shard_map/ppermute | solution.py:449
  55.7 0.2 collective-permute-done.19.refs_11_
  55.9 0.5 collective-permute-done.20.refs_12_
  56.4 0.5 collective-permute-done.21.refs_13_
  56.9 0.0 collective-permute-done.17.refs_9_
  56.9 15.2 %finish.1 = (bf16[128,1152]{1,0:T(8,128)(2,1)S(1)}, f32[128,1152]{1,0:T(8,128)S(1)}) custom-call(s32[15]{0:T(128)S(1)} %stack.75.place, bf16[64,2304]{1,0:T(8,128)(2,1)} %bitcast.21, bf16[64,2304]{1,0:T(8,128)(2,1)S(1)} %collective-permute-done.other, bf16[256,2304]{1,0:T(8,128)(2,1)} %bitcast.18, f32[1,1280]{1,0:T(1,128)S(1)} %broadcast_in_dim.24.weight, ...), custom_call_target="tpu_custom_call" | custom-call | tf_op jit(solution)/shard_map/finish/pallas_call | solution.py:598
  72.1 0.8 copy-done.4
  72.9 0.7 collective-permute-start.22
  73.6 8.3 %collective-permute-done.22.came = bf16[128,1152]{1,0:T(8,128)(2,1)S(1)} collective-permute-done((bf16[128,1152]{1,0:T(8,128)(2,1)S(1)}, bf16[128,1152]{1,0:T(8,128)(2,1)S(1)}, u32[]{:S(2)}, u32[]{:S(2)}) %collective-permute-start.22) | collective-permute-done | bytes 294944 | tf_op jit(solution)/shard_map/ppermute | solution.py:446
  82.0 0.7 copy-done.9
  82.7 2.2 %place.1 = f32[4,64,1152]{2,1,0:T(8,128)} custom-call(s32[2]{0:T(128)} %copy-done.7, f32[128,1152]{1,0:T(8,128)} %copy-done.4, bf16[128,1152]{1,0:T(8,128)(2,1)} %copy-done.9), custom_call_target="tpu_custom_call" | custom-call | tf_op jit(solution)/shard_map/place/pallas_call | solution.py:630
  (37 shorter events, 0.2 us)
Async XLA Ops:
  0.0 9.2 %copy-start.1 = (bf16[1,64,2304]{2,1,0:T(8,128)(2,1)S(1)}, bf16[1,64,2304]{2,1,0:T(8,128)(2,1)}, u32[]{:S(2)}) copy-start(bf16[1,64,2304]{2,1,0:T(8,128)(2,1)} %param.5) | copy-start | bytes 884740
  0.0 8.9 %copy-start.10 = (f32[1280]{0:T(1024)S(1)}, f32[1280]{0:T(1024)}, u32[]{:S(2)}) copy-start(f32[1280]{0:T(1024)} %param.8) | copy-start | bytes 15364
  0.0 8.9 %copy-start.11 = (s32[2304]{0:T(1024)S(1)}, s32[2304]{0:T(1024)}, u32[]{:S(2)}) copy-start(s32[2304]{0:T(1024)} %param.9) | copy-start | bytes 27652
  0.0 9.2 %copy-start = (bf16[4,64,2304]{2,1,0:T(8,128)(2,1)S(1)}, bf16[4,64,2304]{2,1,0:T(8,128)(2,1)}, u32[]{:S(2)}) copy-start(bf16[4,64,2304]{2,1,0:T(8,128)(2,1)} %param.6) | copy-start | bytes 3538948
  0.0 16.6 %collective-permute-start = (bf16[64,2304]{1,0:T(8,128)(2,1)}, bf16[64,2304]{1,0:T(8,128)(2,1)S(1)}, u32[]{:S(2)}, u32[]{:S(2)}) collective-permute-start(bf16[64,2304]{1,0:T(8,128)(2,1)} %bitcast.20), channel_id=1, source_target_pairs={{0,16},{16,0},{1,17},{17,1},{2,18},{18,2},{3,19},{19,3},{4,20},{20... | collective-permute-start | bytes 884744 | tf_op jit(solution)/shard_map/ppermute | solution.py:446
  6.8 18.6 %collective-permute-start.4 = (bf16[80,2304]{1,0:T(8,128)(2,1)}, bf16[80,2304]{1,0:T(8,128)(2,1)S(1)}, u32[]{:S(2)}, u32[]{:S(2)}) collective-permute-start(bf16[80,2304]{1,0:T(8,128)(2,1)} %get-tuple-element.26), channel_id=1, source_target_pairs={{0,16},{16,0},{1,17},{17,1},{2,18},{18,2},{3,19},{19,3},{4,20},{20... | collective-permute-start | bytes 1105928 | tf_op jit(solution)/shard_map/ppermute | solution.py:446
  6.9 24.4 %collective-permute-start.5 = (bf16[80,2304]{1,0:T(8,128)(2,1)}, bf16[80,2304]{1,0:T(8,128)(2,1)S(1)}, u32[]{:S(2)}, u32[]{:S(2)}) collective-permute-start(bf16[80,2304]{1,0:T(8,128)(2,1)} %get-tuple-element.33), channel_id=1, source_target_pairs={{0,16},{16,0},{1,17},{17,1},{2,18},{18,2},{3,19},{19,3},{4,20},{20... | collective-permute-start | bytes 1105928 | tf_op jit(solution)/shard_map/ppermute | solution.py:446
  9.2 13.3 %copy-start.7 = (s32[2]{0:T(128)}, s32[2]{0:T(128)S(1)}, u32[]{:S(2)}) copy-start(s32[2]{0:T(128)S(1)} %pad_add_fusion.place) | copy-start | bytes 28
  16.6 6.0 %copy-start.2 = (bf16[128,2304]{1,0:T(8,128)(2,1)}, bf16[128,2304]{1,0:T(8,128)(2,1)S(1)}, u32[]{:S(2)}) copy-start(bf16[128,2304]{1,0:T(8,128)(2,1)S(1)} %get-tuple-element.40.part_any) | copy-start | bytes 1769476
  16.6 6.8 %copy-start.5 = (bf16[32,1280]{1,0:T(8,128)(2,1)}, bf16[32,1280]{1,0:T(8,128)(2,1)S(1)}, u32[]{:S(2)}) copy-start(bf16[32,1280]{1,0:T(8,128)(2,1)S(1)} %get-tuple-element.42.phi_any) | copy-start | bytes 245764
  22.5 0.8 copy-start.3
  23.4 24.7 %copy-start.6 = (bf16[32,1280]{1,0:T(8,128)(2,1)}, bf16[32,1280]{1,0:T(8,128)(2,1)S(1)}, u32[]{:S(2)}) copy-start(bf16[32,1280]{1,0:T(8,128)(2,1)S(1)} %get-tuple-element.43.other_phi_any) | copy-start | bytes 245764
  23.4 4.6 %collective-permute-start.3 = (bf16[16,2304]{1,0:T(8,128)(2,1)S(1)}, bf16[16,2304]{1,0:T(8,128)(2,1)S(1)}, u32[]{:S(2)}, u32[]{:S(2)}) collective-permute-start(bf16[16,2304]{1,0:T(8,128)(2,1)S(1)} %pad_maximum_fusion.1), channel_id=1, source_target_pairs={{0,3},{1,2},{2,1},{3,0},{4,7},{5,6},{6,5},{7,4},{8,11},{9,10},{10,... | collective-permute-start | bytes 221192 | tf_op jit(solution)/shard_map/ppermute | solution.py:449
  23.6 6.0 %collective-permute-start.2 = (bf16[16,2304]{1,0:T(8,128)(2,1)S(1)}, bf16[16,2304]{1,0:T(8,128)(2,1)S(1)}, u32[]{:S(2)}, u32[]{:S(2)}) collective-permute-start(bf16[16,2304]{1,0:T(8,128)(2,1)S(1)} %pad_maximum_fusion.1), channel_id=1, source_target_pairs={{0,2},{1,3},{2,0},{3,1},{4,6},{5,7},{6,4},{7,5},{8,10},{9,11},{10,... | collective-permute-start | bytes 221192 | tf_op jit(solution)/shard_map/ppermute | solution.py:449
  25.1 6.1 %collective-permute-start.1 = (bf16[16,2304]{1,0:T(8,128)(2,1)S(1)}, bf16[16,2304]{1,0:T(8,128)(2,1)S(1)}, u32[]{:S(2)}, u32[]{:S(2)}) collective-permute-start(bf16[16,2304]{1,0:T(8,128)(2,1)S(1)} %pad_maximum_fusion.1), channel_id=1, source_target_pairs={{0,1},{1,0},{2,3},{3,2},{4,5},{5,4},{6,7},{7,6},{8,9},{9,8},{10,11... | collective-permute-start | bytes 221192 | tf_op jit(solution)/shard_map/ppermute | solution.py:449
  25.4 19.9 %collective-permute-start.9 = (bf16[160,2304]{1,0:T(8,128)(2,1)}, bf16[160,2304]{1,0:T(8,128)(2,1)S(1)}, u32[]{:S(2)}, u32[]{:S(2)}) collective-permute-start(bf16[160,2304]{1,0:T(8,128)(2,1)} %get-tuple-element.36), channel_id=1, source_target_pairs={{0,16},{16,0},{1,17},{17,1},{2,18},{18,2},{3,19},{19,3},{4,20},{20... | collective-permute-start | bytes 2211848 | tf_op jit(solution)/shard_map/ppermute | solution.py:446
  28.0 13.8 %collective-permute-start.7 = (bf16[80,2304]{1,0:T(8,128)(2,1)S(1)}, bf16[80,2304]{1,0:T(8,128)(2,1)S(1)}, u32[]{:S(2)}, u32[]{:S(2)}) collective-permute-start(bf16[80,2304]{1,0:T(8,128)(2,1)S(1)} %collective-permute-done.4.refs_0_), channel_id=1, source_target_pairs={{0,2},{1,3},{2,0},{3,1},{4,6},{5,7},{6,4},{7,5},{8,10},{9,11},{10,... | collective-permute-start | bytes 1105928 | tf_op jit(solution)/shard_map/ppermute | solution.py:449
  29.6 12.9 %collective-permute-start.8 = (bf16[80,2304]{1,0:T(8,128)(2,1)S(1)}, bf16[80,2304]{1,0:T(8,128)(2,1)}, u32[]{:S(2)}, u32[]{:S(2)}) collective-permute-start(bf16[80,2304]{1,0:T(8,128)(2,1)S(1)} %collective-permute-done.4.refs_0_), channel_id=1, source_target_pairs={{0,4},{1,5},{2,6},{3,7},{4,0},{5,1},{6,2},{7,3},{8,12},{9,13},{10,... | collective-permute-start | bytes 1105928 | tf_op jit(solution)/shard_map/ppermute | solution.py:449
  31.4 10.3 %collective-permute-start.11 = (bf16[8,2304]{1,0:T(8,128)(2,1)S(1)}, bf16[8,2304]{1,0:T(8,128)(2,1)S(1)}, u32[]{:S(2)}, u32[]{:S(2)}) collective-permute-start(bf16[8,2304]{1,0:T(8,128)(2,1)S(1)} %get-tuple-element.55), channel_id=1, source_target_pairs={{0,12},{1,13},{2,14},{3,15},{4,0},{5,1},{6,2},{7,3},{8,4},{9,5},{1... | collective-permute-start | bytes 110600 | tf_op jit(solution)/shard_map/ppermute | solution.py:565
  34.0 11.3 %collective-permute-start.10 = (bf16[8,2304]{1,0:T(8,128)(2,1)S(1)}, bf16[8,2304]{1,0:T(8,128)(2,1)S(1)}, u32[]{:S(2)}, u32[]{:S(2)}) collective-permute-start(bf16[8,2304]{1,0:T(8,128)(2,1)S(1)} %get-tuple-element.56), channel_id=1, source_target_pairs={{0,8},{1,9},{2,10},{3,11},{4,12},{5,13},{6,14},{7,15},{8,0},{9,1},... | collective-permute-start | bytes 110600 | tf_op jit(solution)/shard_map/ppermute | solution.py:565
  41.7 6.1 %collective-permute-start.6 = (bf16[8,2304]{1,0:T(8,128)(2,1)S(1)}, bf16[8,2304]{1,0:T(8,128)(2,1)S(1)}, u32[]{:S(2)}, u32[]{:S(2)}) collective-permute-start(bf16[8,2304]{1,0:T(8,128)(2,1)S(1)} %get-tuple-element.54), channel_id=1, source_target_pairs={{0,4},{1,5},{2,6},{3,7},{4,8},{5,9},{6,10},{7,11},{8,12},{9,13},{1... | collective-permute-start | bytes 110600 | tf_op jit(solution)/shard_map/ppermute | solution.py:565
  41.8 9.9 %collective-permute-start.13 = (bf16[80,2304]{1,0:T(8,128)(2,1)S(1)}, bf16[80,2304]{1,0:T(8,128)(2,1)S(1)}, u32[]{:S(2)}, u32[]{:S(2)}) collective-permute-start(bf16[80,2304]{1,0:T(8,128)(2,1)S(1)} %collective-permute-done.5.refs_1_), channel_id=1, source_target_pairs={{0,2},{1,3},{2,0},{3,1},{4,6},{5,7},{6,4},{7,5},{8,10},{9,11},{10,... | collective-permute-start | bytes 1105928 | tf_op jit(solution)/shard_map/ppermute | solution.py:449
  42.5 10.8 %collective-permute-start.14 = (bf16[80,2304]{1,0:T(8,128)(2,1)S(1)}, bf16[80,2304]{1,0:T(8,128)(2,1)}, u32[]{:S(2)}, u32[]{:S(2)}) collective-permute-start(bf16[80,2304]{1,0:T(8,128)(2,1)S(1)} %collective-permute-done.5.refs_1_), channel_id=1, source_target_pairs={{0,4},{1,5},{2,6},{3,7},{4,0},{5,1},{6,2},{7,3},{8,12},{9,13},{10,... | collective-permute-start | bytes 1105928 | tf_op jit(solution)/shard_map/ppermute | solution.py:449
  45.3 8.1 %collective-permute-start.15 = (bf16[80,2304]{1,0:T(8,128)(2,1)S(1)}, bf16[80,2304]{1,0:T(8,128)(2,1)}, u32[]{:S(2)}, u32[]{:S(2)}) collective-permute-start(bf16[80,2304]{1,0:T(8,128)(2,1)S(1)} %collective-permute-done.4.refs_0_), channel_id=1, source_target_pairs={{0,1},{1,0},{2,3},{3,2},{4,5},{5,4},{6,7},{7,6},{8,9},{9,8},{10,11... | collective-permute-start | bytes 1105928 | tf_op jit(solution)/shard_map/ppermute | solution.py:449
  45.3 8.6 %collective-permute-start.16 = (bf16[80,2304]{1,0:T(8,128)(2,1)S(1)}, bf16[80,2304]{1,0:T(8,128)(2,1)}, u32[]{:S(2)}, u32[]{:S(2)}) collective-permute-start(bf16[80,2304]{1,0:T(8,128)(2,1)S(1)} %collective-permute-done.5.refs_1_), channel_id=1, source_target_pairs={{0,1},{1,0},{2,3},{3,2},{4,5},{5,4},{6,7},{7,6},{8,9},{9,8},{10,11... | collective-permute-start | bytes 1105928 | tf_op jit(solution)/shard_map/ppermute | solution.py:449
  48.7 5.2 %collective-permute-start.12 = (bf16[24,2304]{1,0:T(8,128)(2,1)}, bf16[24,2304]{1,0:T(8,128)(2,1)S(1)}, u32[]{:S(2)}, u32[]{:S(2)}) collective-permute-start(bf16[24,2304]{1,0:T(8,128)(2,1)} %pad_maximum_fusion), channel_id=1, source_target_pairs={{0,16},{16,0},{1,17},{17,1},{2,18},{18,2},{3,19},{19,3},{4,20},{20... | collective-permute-start | bytes 331784 | tf_op jit(solution)/shard_map/ppermute | solution.py:446
  51.7 0.7 copy-start.8
  52.4 4.5 %collective-permute-start.17 = (bf16[160,2304]{1,0:T(8,128)(2,1)S(1)}, bf16[160,2304]{1,0:T(8,128)(2,1)S(1)}, u32[]{:S(2)}, u32[]{:S(2)}) collective-permute-start(bf16[160,2304]{1,0:T(8,128)(2,1)S(1)} %collective-permute-done.9.refs_2_), channel_id=1, source_target_pairs={{0,1},{1,0},{2,3},{3,2},{4,5},{5,4},{6,7},{7,6},{8,9},{9,8},{10,11... | collective-permute-start | bytes 2211848 | tf_op jit(solution)/shard_map/ppermute | solution.py:449
  53.3 2.3 %collective-permute-start.18 = (bf16[80,2304]{1,0:T(8,128)(2,1)S(1)}, bf16[80,2304]{1,0:T(8,128)(2,1)S(1)}, u32[]{:S(2)}, u32[]{:S(2)}) collective-permute-start(bf16[80,2304]{1,0:T(8,128)(2,1)S(1)} %collective-permute-done.7.refs_3_), channel_id=1, source_target_pairs={{0,1},{1,0},{2,3},{3,2},{4,5},{5,4},{6,7},{7,6},{8,9},{9,8},{10,11... | collective-permute-start | bytes 1105928 | tf_op jit(solution)/shard_map/ppermute | solution.py:449
  53.3 2.5 %collective-permute-start.19 = (bf16[80,2304]{1,0:T(8,128)(2,1)}, bf16[80,2304]{1,0:T(8,128)(2,1)S(1)}, u32[]{:S(2)}, u32[]{:S(2)}) collective-permute-start(bf16[80,2304]{1,0:T(8,128)(2,1)} %collective-permute-done.8.refs_4_), channel_id=1, source_target_pairs={{0,1},{1,0},{2,3},{3,2},{4,5},{5,4},{6,7},{7,6},{8,9},{9,8},{10,11... | collective-permute-start | bytes 1105928 | tf_op jit(solution)/shard_map/ppermute | solution.py:449
  53.8 2.6 %collective-permute-start.20 = (bf16[80,2304]{1,0:T(8,128)(2,1)}, bf16[80,2304]{1,0:T(8,128)(2,1)S(1)}, u32[]{:S(2)}, u32[]{:S(2)}) collective-permute-start(bf16[80,2304]{1,0:T(8,128)(2,1)} %copy-done.8), channel_id=1, source_target_pairs={{0,1},{1,0},{2,3},{3,2},{4,5},{5,4},{6,7},{7,6},{8,9},{9,8},{10,11... | collective-permute-start | bytes 1105928 | tf_op jit(solution)/shard_map/ppermute | solution.py:449
  53.9 3.0 %collective-permute-start.21 = (bf16[80,2304]{1,0:T(8,128)(2,1)}, bf16[80,2304]{1,0:T(8,128)(2,1)S(1)}, u32[]{:S(2)}, u32[]{:S(2)}) collective-permute-start(bf16[80,2304]{1,0:T(8,128)(2,1)} %collective-permute-done.14.refs_6_), channel_id=1, source_target_pairs={{0,1},{1,0},{2,3},{3,2},{4,5},{5,4},{6,7},{7,6},{8,9},{9,8},{10,11... | collective-permute-start | bytes 1105928 | tf_op jit(solution)/shard_map/ppermute | solution.py:449
  72.1 0.8 copy-start.4
  72.9 9.1 %collective-permute-start.22 = (bf16[128,1152]{1,0:T(8,128)(2,1)S(1)}, bf16[128,1152]{1,0:T(8,128)(2,1)S(1)}, u32[]{:S(2)}, u32[]{:S(2)}) collective-permute-start(bf16[128,1152]{1,0:T(8,128)(2,1)S(1)} %get-tuple-element.46), channel_id=1, source_target_pairs={{0,16},{16,0},{1,17},{17,1},{2,18},{18,2},{3,19},{19,3},{4,20},{20... | collective-permute-start | bytes 884744 | tf_op jit(solution)/shard_map/ppermute | solution.py:446
  82.0 0.7 copy-start.9
